TPU v7x, 32 devices: a whole 2x2x4 slice. The times are simulated.
32 devices in a mesh: dp: 16 (over z, y, x), tensor: 2 (over core).
Axes of the slice: x: 2, y: 2, z: 4, core: 2. Of those that a mesh axis runs over, the one named last changes fastest.
Arguments:
- obs: bfloat16 [65536, 376], P('dp'), may hold values from -6 to 6
- action: bfloat16 [65536, 17], P('dp'), may hold values from -0.94921875 to 0.94921875
- next_obs: bfloat16 [65536, 376], P('dp'), may hold values from -6 to 6
- reward: float32 [65536], P('dp'), may hold values from -6 to 6
- terminal: int32 [65536], P('dp'), may hold values 0 or 1
- noise: float32 [65536, 17], P('dp'), may hold values from -4 to 4
- next_noise: float32 [65536, 17], P('dp'), may hold values from -4 to 4
- counts: int32 [16], P('dp'), may hold values from 2048 to 4096, as said below
- step_count: int32 [1], replicated, may hold values from 2 to 21
- a_w1: float32 [377, 256], P(None, 'tensor'), may hold values from -0.3125 to 0.3125
- a_w2: float32 [256, 256], P('tensor'), may hold values from -0.375 to 0.375
- a_head: float32 [257, 34], replicated, may hold values from -0.375 to 0.375
- c_w1: float32 [2, 394, 256], P(None, None, 'tensor'), may hold values from -0.3125 to 0.3125
- c_w2: float32 [2, 256, 256], P(None, 'tensor'), may hold values from -0.375 to 0.375
- c_head: float32 [2, 257, 2], replicated, may hold values from -0.375 to 0.375
- bias2: float32 [3, 256], replicated, may hold values from -1.5 to 1.5
- tc_w1: float32 [2, 394, 256], P(None, None, 'tensor'), may hold values from -0.3125 to 0.3125
- tc_w2: float32 [2, 256, 256], P(None, 'tensor'), may hold values from -0.375 to 0.375
- tc_head: float32 [2, 257, 2], replicated, may hold values from -0.375 to 0.375
- tc_bias2: float32 [2, 256], replicated, may hold values from -1.5 to 1.5
- a_w1_mom: float32 [2, 377, 256], P(None, None, 'tensor'), as said below
- a_w2_mom: float32 [2, 256, 256], P(None, 'tensor'), as said below
- a_head_mom: float32 [2, 257, 34], replicated, as said below
- c_w1_mom: float32 [2, 2, 394, 256], P(None, None, None, 'tensor'), as said below
- c_w2_mom: float32 [2, 2, 256, 256], P(None, None, 'tensor'), as said below
- c_head_mom: float32 [2, 2, 257, 2], replicated, as said below
- bias2_mom: float32 [2, 3, 256], replicated, as said below
- state: float32 [4], replicated, as said below
Outputs:
- a_w1_new: float32 [377, 256], P(None, 'tensor')
- a_w1_first: float32 [377, 256], P(None, 'tensor')
- a_w1_second: float32 [377, 256], P(None, 'tensor')
- a_w2_new: float32 [256, 256], P('tensor')
- a_w2_first: float32 [256, 256], P('tensor')
- a_w2_second: float32 [256, 256], P('tensor')
- a_head_new: float32 [257, 34], replicated
- a_head_first: float32 [257, 34], replicated
- a_head_second: float32 [257, 34], replicated
- c_w1_new: float32 [4, 394, 256], P(None, None, 'tensor')
- c_w1_first: float32 [2, 394, 256], P(None, None, 'tensor')
- c_w1_second: float32 [2, 394, 256], P(None, None, 'tensor')
- c_w2_new: float32 [4, 256, 256], P(None, 'tensor')
- c_w2_first: float32 [2, 256, 256], P(None, 'tensor')
- c_w2_second: float32 [2, 256, 256], P(None, 'tensor')
- c_head_new: float32 [4, 257, 2], replicated
- c_head_first: float32 [2, 257, 2], replicated
- c_head_second: float32 [2, 257, 2], replicated
- bias2_new: float32 [5, 256], replicated
- bias2_first: float32 [3, 256], replicated
- bias2_second: float32 [3, 256], replicated
- scalars: float32 [5], replicated
- grad_norm: float32 [1], replicated
Inputs may be any that keep to these rules, and one draw needn't show every extreme that they name: Each index of dp holds its valid transitions in its first counts rows; some index is full. `a_w1_mom`: index 0 along the first dimension holds first moments, index 1 positive second moments. `a_w2_mom`: as for a_w1_mom. `a_head_mom`: as for a_w1_mom. `c_w1_mom`: as for a_w1_mom. `c_w2_mom`: as for a_w1_mom. `c_head_mom`: as for a_w1_mom. `bias2_mom`: as for a_w1_mom. `state`: the temperature's second moment and the std statistic are positive.
All inputs are finite; a program needn't handle non-finite values. No bound on the sum of `terminal` on one device may be relied on, other than what follows from the above.
Results may differ from a plain program's by a relative error of at most 0.0003.
The roundings to bfloat16 on the way count: a program that leaves them out, or rounds other values in their place, can miss the bound.
Values may be sent and summed in bfloat16 or wider, within the bound.
No kernel may reach another device: no remote copies, remote signals or barrier semaphores. Data moves between devices by JAX's collectives and lax.ppermute only.
A program may use at most 192 MiB of HBM per device.

v0:
```python
import math

import jax
import jax.numpy as jnp
from jax import lax
from jax.sharding import PartitionSpec as P

OBS = 376
ACT = 17
MB = 2
B_MB = 2048


GAMMA = 0.99
RHO = 0.005
TAU_STAT = 0.1
CLIP = 0.005
RATE = 0.05
BETA_ONE = 0.9
BETA_TWO = 0.999
ADAM_EPS = 1e-08
DECAY = 0.01
HALF_LOG_TAU = 0.5 * math.log(2.0 * math.pi)
LOG_TWO = math.log(2.0)
F32 = jnp.float32
B16 = jnp.bfloat16


def gelu_grad(values, upstream):
    return jax.vjp(jax.nn.gelu, values)[1](upstream)[0]


def with_ones(values):
    ones = jnp.ones(values.shape[:-1] + (1,), values.dtype)
    return jnp.concatenate([values, ones], axis=-1)


def net_forward(inputs, w_first, w_second, b_second, w_head, reduce_layer):
    z_first = jnp.einsum("crk,ckh->crh", inputs, w_first, preferred_element_type=F32)
    h_first = jax.nn.gelu(z_first).astype(B16)
    partial_value = jnp.einsum("crh,chg->crg", h_first, w_second, preferred_element_type=F32)
    z_second = reduce_layer(partial_value)
    pre_second = z_second + b_second[:, None, :]
    h_second = with_ones(jax.nn.gelu(pre_second).astype(B16))
    out = jnp.einsum("crg,cgo->cro", h_second, w_head, preferred_element_type=F32)
    return (out, (z_first, h_first, pre_second, h_second))


def net_backward(d_out, kept, w_second, w_head, spread_grad):
    z_first, h_first, pre_second, h_second = kept
    d_low = d_out.astype(B16)
    d_head = jnp.einsum("crg,cro->cgo", h_second, d_low, preferred_element_type=F32)
    d_hidden = jnp.einsum("cro,cgo->crg", d_low, w_head[:, :-1, :], preferred_element_type=F32)
    d_pre = gelu_grad(pre_second, d_hidden)
    d_bias = jnp.sum(d_pre, axis=1)
    d_second = spread_grad(d_pre.astype(B16))
    d_first_h = jnp.einsum("crg,chg->crh", d_second, w_second, preferred_element_type=F32)
    d_first = gelu_grad(z_first, d_first_h).astype(B16)
    return (d_head, d_bias, d_first, d_second)


def weight_grads(inputs, h_first, d_first, d_second):
    grad_first = jnp.einsum("crk,crh->ckh", inputs, d_first, preferred_element_type=F32)
    grad_second = jnp.einsum("crh,crg->chg", h_first, d_second, preferred_element_type=F32)
    return (grad_first, grad_second)


def policy_post(out, noise):
    mean = out[:, :ACT]
    log_std = jnp.tanh(out[:, ACT:]) - 1.0
    u_pre = mean + jnp.exp(log_std) * noise
    act = jnp.tanh(u_pre)
    terms = (
        -0.5 * noise * noise
        - log_std
        - HALF_LOG_TAU
        - 2.0 * (LOG_TWO - u_pre - jax.nn.softplus(-2.0 * u_pre))
    )
    return (act, jnp.sum(terms, axis=1))


def critic_terms(out, target, weight, valid):
    q_mean = out[..., 0]
    log_sigma = jnp.tanh(out[..., 1])
    sigma = jnp.exp(log_sigma)
    error = target[None] - q_mean
    terms = weight * (error * error / (2.0 * sigma * sigma) + log_sigma)
    return (jnp.sum(valid[None] * terms), jnp.sum(valid[None] * sigma))


def adam_step(weight, moments, grad, first_fix, second_fix, decay):
    first = BETA_ONE * moments[0] + (1.0 - BETA_ONE) * grad
    second = BETA_TWO * moments[1] + (1.0 - BETA_TWO) * grad * grad
    step = first / first_fix / (jnp.sqrt(second / second_fix) + ADAM_EPS)
    return (weight - RATE * (step + decay * weight), first, second)


def repeat_two(values):
    return jnp.broadcast_to(values[None], (2,) + values.shape)


def square_sum(arrays):
    total = jnp.float32(0.0)
    for item in arrays:
        total = total + jnp.sum(item * item)
    return total


def shards(
    obs,
    action,
    next_obs,
    reward,
    terminal,
    noise,
    next_noise,
    counts,
    step_count,
    a_w1,
    a_w2,
    a_head,
    c_w1,
    c_w2,
    c_head,
    bias2,
    tc_w1,
    tc_w2,
    tc_head,
    tc_bias2,
    a_w1_mom,
    a_w2_mom,
    a_head_mom,
    c_w1_mom,
    c_w2_mom,
    c_head_mom,
    bias2_mom,
    state,
):
    tensor_index = lax.axis_index("tensor")
    groups = lax.axis_size("tensor")
    half = B_MB // groups
    count_local = counts[0]
    alpha = jnp.exp(state[0])
    omega = state[3] * state[3]
    count = lax.psum(count_local.astype(F32), "dp")
    split_masters = (
        a_w1.astype(B16),
        a_w2.astype(B16),
        c_w1.astype(B16),
        c_w2.astype(B16),
        tc_w1.astype(B16),
        tc_w2.astype(B16),
    )

    def reduce_layer(partial_value):
        return lax.psum_scatter(partial_value, "tensor", scatter_dimension=1, tiled=True)

    def spread_grad(d_pre):
        return lax.all_gather(d_pre, "tensor", axis=1, tiled=True)

    first_a, second_a, first_c, second_c, first_t, second_t = split_masters
    data_rows = B_MB
    actor_first = repeat_two(first_a)
    actor_second = repeat_two(second_a)
    actor_head = repeat_two(a_head.astype(B16))
    actor_bias = jnp.concatenate([bias2[0:1], bias2[0:1]])
    critic_first = jnp.concatenate([first_c, first_c, first_t])
    critic_second = jnp.concatenate([second_c, second_c, second_t])
    critic_head = jnp.concatenate([c_head, c_head, tc_head]).astype(B16)
    critic_bias = jnp.concatenate([bias2[1:3], bias2[1:3], tc_bias2])
    total_grads = None
    loss_part = jnp.float32(0.0)
    sigma_part = jnp.float32(0.0)
    for micro in range(MB):
        row_start = micro * B_MB
        obs_mb = lax.dynamic_slice_in_dim(obs, row_start, data_rows)
        next_mb = lax.dynamic_slice_in_dim(next_obs, row_start, data_rows)
        action_mb = lax.dynamic_slice_in_dim(action, row_start, data_rows)
        start = micro * B_MB + tensor_index * half
        reward_half = lax.dynamic_slice_in_dim(reward, start, half)
        alive = 1.0 - lax.dynamic_slice_in_dim(terminal, start, half).astype(F32)
        noise_half = lax.dynamic_slice_in_dim(noise, start, half)
        next_noise_half = lax.dynamic_slice_in_dim(next_noise, start, half)
        valid = (start + jnp.arange(half, dtype=jnp.int32) < count_local).astype(F32)
        actor_in = jnp.stack([with_ones(obs_mb), with_ones(next_mb)])
        out_actor, kept_actor = net_forward(
            actor_in, actor_first, actor_second, actor_bias, actor_head, reduce_layer
        )
        (act_new, logp_new), policy_pull = jax.vjp(
            lambda o: policy_post(o, noise_half), out_actor[0]
        )
        act_next, logp_next = policy_post(out_actor[1], next_noise_half)
        actions = lax.all_gather(
            jnp.stack([act_new, act_next]).astype(B16), "tensor", axis=1, tiled=True
        )
        data_in = with_ones(jnp.concatenate([obs_mb, action_mb], axis=1))
        new_in = with_ones(jnp.concatenate([obs_mb, actions[0]], axis=1))
        next_in = with_ones(jnp.concatenate([next_mb, actions[1]], axis=1))
        critic_in = jnp.stack([data_in, data_in, new_in, new_in, next_in, next_in])
        out_critic, kept_critic = net_forward(
            critic_in, critic_first, critic_second, critic_bias, critic_head, reduce_layer
        )
        target = reward_half + GAMMA * alive * (
            jnp.minimum(out_critic[4, :, 0], out_critic[5, :, 0]) - alpha * logp_next
        )
        critic_sum, critic_pull, sigma_sum = jax.vjp(
            lambda o: critic_terms(o, target, omega, valid), out_critic[:2], has_aux=True
        )
        d_data = critic_pull(jnp.float32(1.0))[0]
        d_new = repeat_two(jnp.stack([-0.5 * valid, jnp.zeros_like(valid)], axis=1))
        kept_four = tuple((k[:4] for k in kept_critic))
        d_head_c, d_bias_c, d_first_c, d_second_c = net_backward(
            jnp.concatenate([d_data, d_new]),
            kept_four,
            critic_second[:4],
            critic_head[:4],
            spread_grad,
        )
        grad_c1, grad_c2 = weight_grads(
            critic_in[:2], kept_four[1][:2], d_first_c[:2], d_second_c[:2]
        )
        d_act_part = jnp.einsum(
            "crh,ckh->rk",
            d_first_c[2:4],
            critic_first[2:4, OBS : OBS + ACT, :],
            preferred_element_type=F32,
        )
        d_act = lax.psum_scatter(
            d_act_part.astype(jnp.bfloat16), "tensor", scatter_dimension=0, tiled=True
        ).astype(jnp.float32)
        d_out_actor = policy_pull((d_act, alpha * valid))[0]
        kept_one = tuple((k[:1] for k in kept_actor))
        d_head_a, d_bias_a, d_first_a, d_second_a = net_backward(
            d_out_actor[None], kept_one, actor_second[:1], actor_head[:1], spread_grad
        )
        grad_a1, grad_a2 = weight_grads(actor_in[:1], kept_one[1], d_first_a, d_second_a)
        actor_sum = jnp.sum(
            valid * (alpha * logp_new - 0.5 * (out_critic[2, :, 0] + out_critic[3, :, 0]))
        )
        alpha_grad = -jnp.sum(valid * (logp_next - ACT))
        micro_grads = (
            grad_a1[0],
            grad_a2[0],
            d_head_a[0],
            grad_c1,
            grad_c2,
            d_head_c[:2],
            jnp.concatenate([d_bias_a, d_bias_c[:2]]),
            alpha_grad,
        )
        if total_grads is None:
            total_grads = micro_grads
        else:
            total_grads = jax.tree.map(jnp.add, total_grads, micro_grads)
        loss_part = loss_part + critic_sum + actor_sum
        sigma_part = sigma_part + sigma_sum
    grads = total_grads
    grads = lax.psum(grads, "dp")
    g_a1, g_a2, g_ahead, g_c1, g_c2, g_chead, g_bias, g_alpha = grads
    split_squares = square_sum([g_a1, g_a2, g_c1, g_c2])
    g_ahead, g_chead, g_bias, g_alpha, split_squares = lax.psum(
        (g_ahead, g_chead, g_bias, g_alpha, split_squares), "tensor"
    )
    squares = split_squares + square_sum([g_ahead, g_chead, g_bias])
    grads, g_alpha, squares = ([g_a1, g_a2, g_ahead, g_c1, g_c2, g_chead, g_bias], g_alpha, squares)
    loss_total, sigma_total = lax.psum((loss_part, sigma_part), ("dp", "tensor"))
    inverse = 1.0 / count
    grad_norm = jnp.sqrt(squares) * inverse
    clip = jnp.minimum(1.0, CLIP / (grad_norm + 1e-06))
    t_step = step_count[0].astype(F32)
    first_fix = 1.0 - jnp.power(BETA_ONE, t_step)
    second_fix = 1.0 - jnp.power(BETA_TWO, t_step)
    weights = [a_w1, a_w2, a_head, c_w1, c_w2, c_head, bias2]
    moments = [a_w1_mom, a_w2_mom, a_head_mom, c_w1_mom, c_w2_mom, c_head_mom, bias2_mom]
    results = []
    for weight, mom, grad in zip(weights, moments, grads):
        results.append(
            adam_step(weight, mom, clip * (grad * inverse), first_fix, second_fix, DECAY)
        )
    tc_w1_new = (1.0 - RHO) * tc_w1 + RHO * results[3][0]
    tc_w2_new = (1.0 - RHO) * tc_w2 + RHO * results[4][0]
    tc_head_new = (1.0 - RHO) * tc_head + RHO * results[5][0]
    tc_bias2_new = (1.0 - RHO) * tc_bias2 + RHO * results[6][0][1:3]
    alpha_grad_total = g_alpha * inverse
    alpha_new, alpha_first, alpha_second = adam_step(
        state[0], state[1:3], alpha_grad_total, first_fix, second_fix, 0.0
    )
    stat_new = (1.0 - TAU_STAT) * state[3] + TAU_STAT * sigma_total / (2.0 * count)
    loss = (loss_total + state[0] * g_alpha) * inverse
    scalars = jnp.stack([alpha_new, alpha_first, alpha_second, stat_new, loss])
    return (
        results[0][0],
        results[0][1],
        results[0][2],
        results[1][0],
        results[1][1],
        results[1][2],
        results[2][0],
        results[2][1],
        results[2][2],
        jnp.concatenate([results[3][0], tc_w1_new]),
        results[3][1],
        results[3][2],
        jnp.concatenate([results[4][0], tc_w2_new]),
        results[4][1],
        results[4][2],
        jnp.concatenate([results[5][0], tc_head_new]),
        results[5][1],
        results[5][2],
        jnp.concatenate([results[6][0], tc_bias2_new]),
        results[6][1],
        results[6][2],
        scalars,
        grad_norm[None],
    )


def solution(mesh):
    in_specs = (
        P("dp", None),
        P("dp", None),
        P("dp", None),
        P("dp"),
        P("dp"),
        P("dp", None),
        P("dp", None),
        P("dp"),
        P(),
        P(None, "tensor"),
        P("tensor", None),
        P(),
        P(None, None, "tensor"),
        P(None, "tensor", None),
        P(),
        P(),
        P(None, None, "tensor"),
        P(None, "tensor", None),
        P(),
        P(),
        P(None, None, "tensor"),
        P(None, "tensor", None),
        P(),
        P(None, None, None, "tensor"),
        P(None, None, "tensor", None),
        P(),
        P(),
        P(),
    )
    out_specs = (
        P(None, "tensor"),
        P(None, "tensor"),
        P(None, "tensor"),
        P("tensor", None),
        P("tensor", None),
        P("tensor", None),
        P(),
        P(),
        P(),
        P(None, None, "tensor"),
        P(None, None, "tensor"),
        P(None, None, "tensor"),
        P(None, "tensor", None),
        P(None, "tensor", None),
        P(None, "tensor", None),
        P(),
        P(),
        P(),
        P(),
        P(),
        P(),
        P(),
        P(),
    )
    return jax.shard_map(shards, mesh=mesh, in_specs=in_specs, out_specs=out_specs, check_vma=False)
```

profile of v0, /device:TPU:0, one launch (start us, length us, event | category | flops | bytes accessed | tf_op | source)
XLA Modules:
  0.0 467.1 jit_solution(287767680569412260)
XLA Ops:
  7.2 3.4 fusion.390
  18.2 4.5 fusion.115
  23.6 2.7 fusion.287
  28.3 2.6 copy.266
  32.5 2.8 fusion.99
  36.2 3.1 fusion.289
  55.2 2.7 pad_maximum_fusion.5
  57.9 3.0 constant_dynamic-update-slice_fusion.1
  63.7 5.7 %fusion.107 = (bf16[2,1024,256]{2,1,0:T(8,128)(2,1)S(1)}, f32[2,1024,256]{2,1,0:T(8,128)}, bf16[2,1024,256]{2,1,0:T(8,128)(2,1)S(1)}, f32[2,1024,256]{2,1,0:T(8,128)}) fusion(f32[2,1024,256]{2,1,0:T(8,128)} %reduce-scatter.7.cloned.1.call-done, f32[2,256]{1,0:T(2,128)} %pad_maximum_fusion.26, f32[2,1024,256]{2,1,0:T(8,128)} %reduce-scatter.13.cloned.1.call-done), kind=kLoop, calls=%fused_computation.133 | loop fusion | flops 10485760 | bytes 10487808 | tf_op jit(solution)/shard_map/convert_element_type | solution.py:44
  78.3 3.2 fusion.152
  81.5 2.1 fusion.153
  87.3 2.4 all_gather.21
  92.3 3.8 fusion.150
  96.1 3.2 constant_dynamic-update-slice_fusion.3
  100.8 2.1 fusion.154
  102.9 2.2 fusion.155
  107.0 3.8 fusion.148
  110.8 2.2 fusion.149
  113.1 6.8 %fusion.228 = f32[6,2048,128]{2,1,0:T(8,128)S(1)} fusion(bf16[6,2048,394]{2,1,0:T(8,128)(2,1)} %fusion.149, bf16[6,394,128]{2,0,1:T(8,128)(2,1)S(1)} %copy-done.15), kind=kOutput, calls=%fused_computation.258 | convolution fusion | flops 1239416832 | bytes 16579584 | tf_op jit(solution)/shard_map/crk,ckh->crh/dot_general | solution.py:39
  119.9 2.7 copy-done.1
  122.6 5.9 %fusion.240 = f32[6,2048,256]{2,1,0:T(8,128)} fusion(bf16[2,128,256]{2,1,0:T(8,128)(2,1)S(1)} %copy-done.35, bf16[2,128,256]{2,1,0:T(8,128)(2,1)S(1)} %copy-done.33, f32[6,2048,128]{2,1,0:T(8,128)S(1)} %fusion.228), kind=kOutput, calls=%fused_computation.293 | convolution fusion | flops 819855360 | bytes 19136512 | tf_op jit(solution)/shard_map/crh,chg->crg/dot_general | solution.py:41
  128.6 6.7 %fusion.230 = f32[6,2048,128]{2,1,0:T(8,128)S(1)} fusion(bf16[6,2048,394]{2,1,0:T(8,128)(2,1)} %get-tuple-element.243, bf16[6,394,128]{2,0,1:T(8,128)(2,1)} %pad_maximum_fusion.5), kind=kOutput, calls=%fused_computation.260 | convolution fusion | flops 1239416832 | bytes 16579584 | tf_op jit(solution)/shard_map/crk,ckh->crh/dot_general | solution.py:39
  135.3 3.1 copy-done
  138.5 9.8 %fusion.241 = f32[6,2048,256]{2,1,0:T(8,128)} fusion(bf16[2,128,256]{2,1,0:T(8,128)(2,1)S(1)} %copy-done.36, bf16[2,128,256]{2,1,0:T(8,128)(2,1)S(1)} %copy-done.34, f32[6,2048,128]{2,1,0:T(8,128)S(1)} %fusion.230), kind=kOutput, calls=%fused_computation.294 | convolution fusion | flops 819855360 | bytes 19136512 | tf_op jit(solution)/shard_map/crh,chg->crg/dot_general | solution.py:41
  158.7 14.7 %reduce-scatter.9.cloned.1.call-done = f32[6,1024,256]{2,1,0:T(8,128)} async-done(((f32[6,2048,256]{2,1,0:T(8,128)}), f32[6,1024,256]{2,1,0:T(8,128)}) %reduce-scatter.9.cloned.1.call-update) | async-done | bytes 6291472 | tf_op jit(solution)/shard_map/reduce_scatter | solution.py:156
  173.3 9.0 %fusion.15 = (bf16[6,1024,256]{2,1,0:T(8,128)(2,1)S(1)}, f32[6,1024,256]{2,1,0:T(8,128)}, bf16[6,1024,256]{2,1,0:T(8,128)(2,1)S(1)}, f32[6,1024,256]{2,1,0:T(8,128)S(1)}) fusion(f32[6,1024,256]{2,1,0:T(8,128)} %reduce-scatter.9.cloned.1.call-done, f32[6,256]{1,0:T(8,128)} %pad_maximum_fusion.23, f32[6,1024,256]{2,1,0:T(8,128)} %reduce-scatter.15.cloned.1.call-done), kind=kLoop, calls=%fused_computation.19 | loop fusion | flops 31457280 | bytes 31463424 | tf_op jit(solution)/shard_map/convert_element_type | solution.py:44
  182.5 2.3 fusion.34
  188.8 5.8 %fusion.388 = (f32[4,256]{1,0:T(4,128)}, bf16[4,1024,256]{2,1,0:T(8,128)(2,1)}) fusion(f32[6,1024,256]{2,1,0:T(8,128)S(1)} %get-tuple-element.236, bf16[2,257,2]{1,2,0:T(2,128)(2,1)} %copy-done.90, bf16[4,1024,2]{1,0,2:T(4,128)(2,1)S(1)} %pad_maximum_fusion.20), kind=kOutput, calls=%fused_computation.535 | convolution fusion | flops 26221568 | bytes 6313992 | tf_op jit(solution)/shard_map/cro,cgo->crg/dot_general | solution.py:53
  197.6 6.7 %fusion.389 = (f32[4,256]{1,0:T(4,128)}, bf16[4,1024,256]{2,1,0:T(8,128)(2,1)}) fusion(f32[6,1024,256]{2,1,0:T(8,128)} %get-tuple-element.176, bf16[2,257,2]{1,2,0:T(2,128)(2,1)} %copy-done.90, bf16[4,1024,2]{1,0,2:T(4,128)(2,1)S(1)} %pad_maximum_fusion.19), kind=kOutput, calls=%fused_computation.536 | convolution fusion | flops 26221568 | bytes 6313992 | tf_op jit(solution)/shard_map/cro,cgo->crg/dot_general | solution.py:53
  214.7 2.2 fusion.395
  216.9 2.1 fusion.394
  220.3 7.8 %fusion.65 = bf16[4,2048,128]{2,1,0:T(8,128)(2,1)S(1)} fusion(f32[6,2048,128]{2,1,0:T(8,128)} %copy-done.1, bf16[4,2048,256]{2,1,0:T(8,128)(2,1)} %all-gather.9.cloned.1.call-done, bf16[2,128,256]{2,1,0:T(8,128)(2,1)} %convert_element_type.129), kind=kOutput, calls=%fused_computation.77 | convolution fusion | flops 557973504 | bytes 10616832 | tf_op jit(solution)/shard_map/crg,chg->crh/dot_general | solution.py:57
  230.8 6.6 %fusion.52 = bf16[4,2048,128]{2,1,0:T(8,128)(2,1)S(1)} fusion(f32[6,2048,128]{2,1,0:T(8,128)} %copy-done, bf16[4,2048,256]{2,1,0:T(8,128)(2,1)} %all-gather.5.cloned.1.call-done, bf16[2,128,256]{2,1,0:T(8,128)(2,1)} %convert_element_type.129), kind=kOutput, calls=%fused_computation.64 | convolution fusion | flops 557973504 | bytes 10616832 | tf_op jit(solution)/shard_map/crg,chg->crh/dot_general | solution.py:57
  244.5 6.5 %reduce-scatter.11.cloned.1.call-done = bf16[1024,17]{0,1:T(8,128)(2,1)} async-done(((bf16[2048,17]{0,1:T(8,128)(2,1)}), bf16[1024,17]{0,1:T(8,128)(2,1)}) %reduce-scatter.11.cloned.1.call-update) | async-done | bytes 34832 | tf_op jit(solution)/shard_map/reduce_scatter | solution.py:228
  251.0 2.2 multiply_multiply_fusion.37
  253.8 3.5 fusion.393
  257.4 5.0 %fusion.66 = f32[2,394,128]{2,1,0:T(8,128)} fusion(bf16[1,2048,394]{2,1,0:T(8,128)(2,1)} %copy-done.13, bf16[4,2048,128]{2,1,0:T(8,128)(2,1)} %copy-done.24), kind=kOutput, calls=%fused_computation.78 | convolution fusion | flops 414752768 | bytes 3549184 | tf_op jit(solution)/shard_map/crk,crh->ckh/dot_general | solution.py:63
  262.4 3.4 fusion.124
  265.8 2.3 fusion.392
  268.5 5.0 %fusion.136 = f32[2,394,128]{2,1,0:T(8,128)} fusion(f32[2,394,128]{2,1,0:T(8,128)} %fusion.66, bf16[1,2048,394]{2,1,0:T(8,128)(2,1)} %copy-done.14, bf16[4,2048,128]{2,1,0:T(8,128)(2,1)} %copy-done.23), kind=kOutput, calls=%fused_computation.180 | convolution fusion | flops 414853632 | bytes 3958784 | tf_op jit(solution)/shard_map/crk,crh->ckh/dot_general | solution.py:63
  273.4 3.2 fusion.139
  276.7 2.5 fusion.186
  279.9 2.4 convolution_add_fusion
  282.2 3.4 fusion.132
  285.6 3.4 fusion.142
  293.1 40.6 %all-reduce.18 = (f32[]{:T(128)}, f32[]{:T(128)}) all-reduce(f32[]{:T(128)S(6)} %add.656, f32[]{:T(128)S(6)} %add.664), channel_id=1, replica_groups=mesh['dp'=16,'tensor'=2] {'dp','tensor'}, use_global_device_ids=true, to_apply=%region_37.39 | all-reduce | flops 2 | bytes 16 | tf_op jit(solution)/shard_map/psum | solution.py:266
  342.9 78.0 %all-reduce.19 = (f32[]{:T(128)}, f32[257,34]{0,1:T(8,128)S(1)}, f32[2,257,2]{1,2,0:T(2,128)S(1)}, f32[3,256]{1,0:T(4,128)S(1)}, f32[]{:T(128)}) all-reduce(f32[]{:T(128)S(6)} %convert_element_type.152, f32[257,34]{0,1:T(8,128)S(1)} %convolution_add_fusion.1, f32[2,257,2]{1,2,0:T(2,128)} %fusion.145, ...), channel_id=1, replica_groups=mesh['dp'=16,'tensor'=2] {'dp'}, use_global_device_ids=true, to_apply=%region_30.32 | all-reduce | flops 10536 | bytes 84288 | tf_op jit(solution)/shard_map/psum | solution.py:145
  431.3 4.7 all-reduce.21
  (324 shorter events, 115.5 us)
Async XLA Ops:
  7.2 56.5 %reduce-scatter.13.cloned.1.call-start = ((), (), s32[]{:S(2)}) async-start(), calls=%async_computation.11 | async-start | bytes 6291456 | tf_op jit(solution)/shard_map/reduce_scatter | solution.py:156
  18.2 17.1 %copy-start.45 = (bf16[128,256]{1,0:T(8,128)(2,1)}, bf16[128,256]{1,0:T(8,128)(2,1)S(1)}, u32[]{:S(2)}) copy-start(bf16[128,256]{1,0:T(8,128)(2,1)S(1)} %convert_element_type.123) | copy-start | bytes 196612
  26.3 37.4 %reduce-scatter.7.cloned.1.call-start = ((), (), s32[]{:S(2)}) async-start(), calls=%async_computation.6 | async-start | bytes 6291456 | tf_op jit(solution)/shard_map/reduce_scatter | solution.py:156
  39.3 10.4 %copy-start.27 = (f32[2,394,128]{2,0,1:T(2,128)S(1)}, f32[2,394,128]{2,0,1:T(2,128)}, u32[]{:S(2)}) copy-start(f32[2,394,128]{2,0,1:T(2,128)} %param.45) | copy-start | bytes 1210372
  39.3 119.3 %reduce-scatter.15.cloned.1.call-start = ((), (), s32[]{:S(2)}) async-start(), calls=%async_computation.12 | async-start | bytes 18874368 | tf_op jit(solution)/shard_map/reduce_scatter | solution.py:156
  63.7 5.7 %copy-start.60 = (bf16[257,34]{0,1:T(8,128)(2,1)S(1)}, bf16[257,34]{0,1:T(8,128)(2,1)}, u32[]{:S(2)}) copy-start(bf16[257,34]{0,1:T(8,128)(2,1)} %convert_element_type.125) | copy-start | bytes 52432
  107.0 6.0 %copy-start.15 = (bf16[6,394,128]{2,0,1:T(8,128)(2,1)S(1)}, bf16[6,394,128]{2,0,1:T(8,128)(2,1)}, u32[]{:S(2)}) copy-start(bf16[6,394,128]{2,0,1:T(8,128)(2,1)} %pad_maximum_fusion.5) | copy-start | bytes 1815556
  113.0 9.6 %copy-start.33 = (bf16[2,128,256]{2,1,0:T(8,128)(2,1)S(1)}, bf16[2,128,256]{2,1,0:T(8,128)(2,1)}, u32[]{:S(2)}) copy-start(bf16[2,128,256]{2,1,0:T(8,128)(2,1)} %convert_element_type.129) | copy-start | bytes 393220
  113.0 9.6 %copy-start.35 = (bf16[2,128,256]{2,1,0:T(8,128)(2,1)S(1)}, bf16[2,128,256]{2,1,0:T(8,128)(2,1)}, u32[]{:S(2)}) copy-start(bf16[2,128,256]{2,1,0:T(8,128)(2,1)} %convert_element_type.130) | copy-start | bytes 393220
  128.6 44.8 %reduce-scatter.9.cloned.1.call-start = ((), (), s32[]{:S(2)}) async-start(), calls=%async_computation.7 | async-start | bytes 18874368 | tf_op jit(solution)/shard_map/reduce_scatter | solution.py:156
  128.6 9.9 %copy-start.34 = (bf16[2,128,256]{2,1,0:T(8,128)(2,1)S(1)}, bf16[2,128,256]{2,1,0:T(8,128)(2,1)}, u32[]{:S(2)}) copy-start(bf16[2,128,256]{2,1,0:T(8,128)(2,1)} %convert_element_type.129) | copy-start | bytes 393220
  128.6 9.9 %copy-start.36 = (bf16[2,128,256]{2,1,0:T(8,128)(2,1)S(1)}, bf16[2,128,256]{2,1,0:T(8,128)(2,1)}, u32[]{:S(2)}) copy-start(bf16[2,128,256]{2,1,0:T(8,128)(2,1)} %convert_element_type.130) | copy-start | bytes 393220
  148.3 72.1 %all-gather.9.cloned.1.call-start = ((), (), s32[]{:S(2)}) async-start(), calls=%async_computation.13 | async-start | bytes 6291456 | tf_op jit(solution)/shard_map/all_gather | solution.py:159
  150.2 35.2 %copy-start.90 = (bf16[2,257,2]{1,2,0:T(2,128)(2,1)}, bf16[2,257,2]{1,2,0:T(2,128)(2,1)S(1)}, u32[]{:S(2)}) copy-start(bf16[2,257,2]{1,2,0:T(2,128)(2,1)S(1)} %convert.39) | copy-start | bytes 6172
  182.5 6.2 %copy-start.83 = (f32[1024]{0:T(1024)S(1)}, f32[1024]{0:T(1024)}, u32[]{:S(2)}) copy-start(f32[1024]{0:T(1024)} %get-tuple-element.268) | copy-start | bytes 12292
  182.5 6.3 %copy-start.82 = (bf16[1024,2]{0,1:T(2,128)(2,1)S(1)}, bf16[1024,2]{0,1:T(2,128)(2,1)}, u32[]{:S(2)}) copy-start(bf16[1024,2]{0,1:T(2,128)(2,1)} %pad_convert_fusion) | copy-start | bytes 12292
  185.4 9.2 %copy-start.71 = (f32[2,1024,1]{1,2,0:T(1,128)}, f32[2,1024,1]{1,2,0:T(1,128)S(1)}, u32[]{:S(2)}) copy-start(f32[2,1024,1]{1,2,0:T(1,128)S(1)} %get-tuple-element.227) | copy-start | bytes 24580
  185.4 9.2 %copy-start.72 = (f32[2,1024,1]{1,2,0:T(1,128)}, f32[2,1024,1]{1,2,0:T(1,128)S(1)}, u32[]{:S(2)}) copy-start(f32[2,1024,1]{1,2,0:T(1,128)S(1)} %get-tuple-element.228) | copy-start | bytes 24580
  188.8 5.8 %copy-start.75 = (bf16[4,1024,2]{1,0,2:T(4,128)(2,1)}, bf16[4,1024,2]{1,0,2:T(4,128)(2,1)S(1)}, u32[]{:S(2)}) copy-start(bf16[4,1024,2]{1,0,2:T(4,128)(2,1)S(1)} %pad_maximum_fusion.20) | copy-start | bytes 49156
  194.6 36.1 %all-gather.5.cloned.1.call-start = ((), (), s32[]{:S(2)}) async-start(), calls=%async_computation.8 | async-start | bytes 6291456 | tf_op jit(solution)/shard_map/all_gather | solution.py:159
  197.6 6.7 %copy-start.76 = (bf16[4,1024,2]{1,0,2:T(4,128)(2,1)}, bf16[4,1024,2]{1,0,2:T(4,128)(2,1)S(1)}, u32[]{:S(2)}) copy-start(bf16[4,1024,2]{1,0,2:T(4,128)(2,1)S(1)} %pad_maximum_fusion.19) | copy-start | bytes 49156
  204.3 40.2 %reduce-scatter.17.cloned.1.call-start = ((), (), s32[]{:S(2)}) async-start(), calls=%async_computation.14 | async-start | bytes 147456 | tf_op jit(solution)/shard_map/reduce_scatter | solution.py:228
  220.3 9.1 %copy-start.66 = (bf16[2,17,128]{2,0,1:T(2,128)(2,1)S(1)}, bf16[2,17,128]{2,0,1:T(2,128)(2,1)}, u32[]{:S(2)}) copy-start(bf16[2,17,128]{2,0,1:T(2,128)(2,1)} %slice.368) | copy-start | bytes 26116
  230.5 20.5 %reduce-scatter.11.cloned.1.call-start = ((), (), s32[]{:S(2)}) async-start(), calls=%async_computation.9 | async-start | bytes 147456 | tf_op jit(solution)/shard_map/reduce_scatter | solution.py:228
  230.8 8.0 %copy-start.67 = (bf16[2,17,128]{2,0,1:T(2,128)(2,1)S(1)}, bf16[2,17,128]{2,0,1:T(2,128)(2,1)}, u32[]{:S(2)}) copy-start(bf16[2,17,128]{2,0,1:T(2,128)(2,1)} %slice.368) | copy-start | bytes 26116
  239.8 36.9 %all-gather.7.cloned.1.call-start = ((), (), s32[]{:S(2)}) async-start(), calls=%async_computation.10 | async-start | bytes 1572864 | tf_op jit(solution)/shard_map/all_gather | solution.py:159
  257.4 22.5 %all-gather.11.cloned.1.call-start = ((), (), s32[]{:S(2)}) async-start(), calls=%async_computation.15 | async-start | bytes 1572864 | tf_op jit(solution)/shard_map/all_gather | solution.py:159
  257.4 5.0 %copy-start.92 = (bf16[4,2048,256]{2,1,0:T(8,128)(2,1)S(1)}, bf16[4,2048,256]{2,1,0:T(8,128)(2,1)}, u32[]{:S(2)}) copy-start(bf16[4,2048,256]{2,1,0:T(8,128)(2,1)} %all-gather.9.cloned.1.call-done) | copy-start | bytes 12582916
  268.1 154.1 %all-reduce.24.cloned.1.call-start = ((), (), s32[]{:S(2)}) async-start(), calls=%async_computation.16 | async-start | bytes 1998848 | tf_op jit(solution)/shard_map/psum | solution.py:258
  268.4 5.0 %copy-start.93 = (bf16[4,2048,256]{2,1,0:T(8,128)(2,1)S(1)}, bf16[4,2048,256]{2,1,0:T(8,128)(2,1)}, u32[]{:S(2)}) copy-start(bf16[4,2048,256]{2,1,0:T(8,128)(2,1)} %all-gather.5.cloned.1.call-done) | copy-start | bytes 12582916
  268.4 5.0 %copy-start.94 = (f32[2,128,256]{2,1,0:T(8,128)S(1)}, f32[2,128,256]{2,1,0:T(8,128)}, u32[]{:S(2)}) copy-start(f32[2,128,256]{2,1,0:T(8,128)} %fusion.124) | copy-start | bytes 786436
  289.1 50.0 %copy-start.7 = (bf16[6,1024,256]{2,1,0:T(8,128)(2,1)S(1)}, bf16[6,1024,256]{2,1,0:T(8,128)(2,1)}, u32[]{:S(2)}) copy-start(bf16[6,1024,256]{2,1,0:T(8,128)(2,1)} %copy-done.6) | copy-start | bytes 9437188
  339.1 104.7 %copy-start.85 = (f32[3,256]{1,0:T(4,128)S(1)}, f32[3,256]{1,0:T(4,128)}, u32[]{:S(2)}) copy-start(f32[3,256]{1,0:T(4,128)} %param.44) | copy-start | bytes 9220
  340.8 107.0 %copy-start.37 = (f32[2,128,256]{2,1,0:T(8,128)S(1)}, f32[2,128,256]{2,1,0:T(8,128)}, u32[]{:S(2)}) copy-start(f32[2,128,256]{2,1,0:T(8,128)} %param.46) | copy-start | bytes 786436
  340.8 107.0 %copy-start.38 = (f32[2,128,256]{2,1,0:T(8,128)S(1)}, f32[2,128,256]{2,1,0:T(8,128)}, u32[]{:S(2)}) copy-start(f32[2,128,256]{2,1,0:T(8,128)} %param.42) | copy-start | bytes 786436
  340.8 107.0 %copy-start.50 = (f32[2,2,128,256]{3,2,1,0:T(8,128)S(1)}, f32[2,2,128,256]{3,2,1,0:T(8,128)}, u32[]{:S(2)}) copy-start(f32[2,2,128,256]{3,2,1,0:T(8,128)} %param.53) | copy-start | bytes 1572868
  340.8 109.0 %copy-start.28 = (f32[2,394,128]{2,0,1:T(2,128)S(1)}, f32[2,394,128]{2,0,1:T(2,128)}, u32[]{:S(2)}) copy-start(f32[2,394,128]{2,0,1:T(2,128)} %param.41) | copy-start | bytes 1210372
  340.8 109.0 %copy-start.29 = (f32[1,2,394,128]{3,1,2,0:T(2,128)S(1)}, f32[1,2,394,128]{3,1,2,0:T(2,128)}, u32[]{:S(2)}) copy-start(f32[1,2,394,128]{3,1,2,0:T(2,128)} %get-tuple-element.201) | copy-start | bytes 1210372
  340.8 108.9 %copy-start.30 = (f32[1,2,394,128]{3,1,2,0:T(2,128)S(1)}, f32[1,2,394,128]{3,1,2,0:T(2,128)}, u32[]{:S(2)}) copy-start(f32[1,2,394,128]{3,1,2,0:T(2,128)} %get-tuple-element.202) | copy-start | bytes 1210372
  436.0 13.8 %copy-start.62 = (f32[257,34]{0,1:T(8,128)}, f32[257,34]{0,1:T(8,128)S(1)}, u32[]{:S(2)}) copy-start(f32[257,34]{0,1:T(8,128)S(1)} %get-tuple-element.143) | copy-start | bytes 104860
  451.3 5.5 %copy-start.46 = (f32[257,34]{0,1:T(8,128)S(1)}, f32[257,34]{0,1:T(8,128)}, u32[]{:S(2)}) copy-start(f32[257,34]{0,1:T(8,128)} %param.40) | copy-start | bytes 104860
  451.3 5.5 %copy-start.63 = (f32[257,34]{0,1:T(8,128)S(1)}, f32[257,34]{0,1:T(8,128)}, u32[]{:S(2)}) copy-start(f32[257,34]{0,1:T(8,128)} %copy-done.62) | copy-start | bytes 104860
  451.3 5.5 %copy-start.64 = (f32[1,257,34]{1,0,2:T(1,128)S(1)}, f32[1,257,34]{1,0,2:T(1,128)}, u32[]{:S(2)}) copy-start(f32[1,257,34]{1,0,2:T(1,128)} %get-tuple-element.219) | copy-start | bytes 104860
  451.3 5.5 %copy-start.65 = (f32[1,257,34]{1,0,2:T(1,128)S(1)}, f32[1,257,34]{1,0,2:T(1,128)}, u32[]{:S(2)}) copy-start(f32[1,257,34]{1,0,2:T(1,128)} %get-tuple-element.220) | copy-start | bytes 104860
  451.3 6.2 %copy-start.41 = (f32[377,128]{1,0:T(8,128)S(1)}, f32[377,128]{1,0:T(8,128)}, u32[]{:S(2)}) copy-start(f32[377,128]{1,0:T(8,128)} %param.38) | copy-start | bytes 579076
  451.3 6.2 %copy-start.42 = (f32[377,128]{1,0:T(8,128)S(1)}, f32[377,128]{1,0:T(8,128)}, u32[]{:S(2)}) copy-start(f32[377,128]{1,0:T(8,128)} %get-tuple-element.138) | copy-start | bytes 579076
  451.3 6.2 %copy-start.43 = (f32[1,377,128]{2,0,1:T(1,128)S(1)}, f32[1,377,128]{2,0,1:T(1,128)}, u32[]{:S(2)}) copy-start(f32[1,377,128]{2,0,1:T(1,128)} %get-tuple-element.207) | copy-start | bytes 579076
  451.3 6.2 %copy-start.44 = (f32[1,377,128]{2,0,1:T(1,128)S(1)}, f32[1,377,128]{2,0,1:T(1,128)}, u32[]{:S(2)}) copy-start(f32[1,377,128]{2,0,1:T(1,128)} %get-tuple-element.208) | copy-start | bytes 579076
  (58 other events, 176.4 us)
Sparse Core Ops, SparseCore 0:
  26.5 14.7 reduce-scatter.12
  43.5 13.3 reduce-scatter.6
  128.7 21.6 reduce-scatter.14
  152.5 20.7 reduce-scatter.8
  194.8 14.9 all-gather.8
  211.1 14.8 all-gather.4
  230.6 8.8 reduce-scatter.16
  242.3 8.6 reduce-scatter.10
  257.5 10.1 all-gather.6
  269.6 10.1 all-gather.10
  289.2 114.3 all-reduce.23
where the time goes:
time: 475 us; the launch traced here: 467 us
  blocking collectives  128 us (27%)
  matrix products  114 us (24%)
  other arithmetic  94.4 us (20%)
  local copies, waits for them, and re-layouts  69.6 us (15%)
  between operations  38 us (8%)
  waiting for transfers between devices  22.1 us (5%)
    psum x1, blocking collectives, shards(): count = lax.psum(count_local.astype(F32), 'dp')  78 us
    psum x1, blocking collectives, shards(): lax.psum((loss_part, sigma_part), ('dp', 'tensor'))  40.6 us
    unnamed x201, local copies, waits for them, and re-layouts  34.2 us
    unnamed x8, other arithmetic  23.4 us
    dot_general x4, matrix products, net_forward(): jnp.einsum('crh,chg->crg', h_first, w_second, preferred_element_type=F32)  21.5 us
    dot_general x4, matrix products, net_forward(): jnp.einsum('crk,ckh->crh', inputs, w_first, preferred_element_type=F32)  20.7 us
    dot_general x4, matrix products, net_backward(): jnp.einsum('cro,cgo->crg', d_low, w_head[:, :-1, :], preferred_element_ty...  18.2 us
    dot_general x4, matrix products, weight_grads(): jnp.einsum('crk,crh->ckh', inputs, d_first, preferred_element_type=F32)  16.8 us
  transfers between devices with their start and end apart: 11, of which 3 were waited for; matrix products, arithmetic and copies ran while one was open for 27% of the time, Pallas kernels for 0%

commit v1 on v0

v1 whole, which is shorter than its diff:
```python
import functools
import math

import jax
import jax.numpy as jnp
from jax import lax
from jax.experimental import pallas as pl
from jax.experimental.pallas import tpu as pltpu
from jax.sharding import PartitionSpec as P

OBS = 376
ACT = 17
H = 256
GAMMA = 0.99
RHO = 0.005
TAU_STAT = 0.1
CLIP = 0.005
RATE = 0.05
BETA_ONE = 0.9
BETA_TWO = 0.999
ADAM_EPS = 1e-08
DECAY = 0.01
HALF_LOG_TAU = 0.5 * math.log(2.0 * math.pi)
LOG_TWO = math.log(2.0)
GELU_A = math.sqrt(2.0 / math.pi)
GELU_B = GELU_A * 0.044715
F32 = jnp.float32
B16 = jnp.bfloat16

A_IN = OBS + 1
C_IN = OBS + ACT + 1
BIAS_ROW = OBS + ACT
K_PAD = 512
K_USE = 400
HALF = H // 2
VMEM = pltpu.VMEM
VMEM_LIMIT = 62 * 1024 * 1024

PACK_W2 = 5 * 4 * HALF
PACK_ACT = PACK_W2 + 5 * 2 * HALF
PACK_ROWS = PACK_ACT + 2 * 32

FLAT_CW1 = 0
FLAT_AW1 = 792
FLAT_AW2 = FLAT_AW1 + 384
FLAT_CW2 = FLAT_AW2 + H
FLAT_SMALL = FLAT_CW2 + 2 * H
FLAT_AHEAD = FLAT_SMALL
FLAT_CHEAD = FLAT_AHEAD + 80
FLAT_B2 = FLAT_CHEAD + 8
FLAT_SUMS = FLAT_B2 + 8
FLAT_ROWS = FLAT_SUMS + 8
LANE_C = 48
LANE_LOSS = 64
LANE_SIGMA = 72
LANE_NEXT = 80
LANE_COUNT = 88


def dot_nn(a, b):
    return lax.dot_general(a, b, (((1,), (0,)), ((), ())), preferred_element_type=F32)


def dot_nt(a, b):
    return lax.dot_general(a, b, (((1,), (1,)), ((), ())), preferred_element_type=F32)


def gelu_only(z):
    zz = z * z
    t = jnp.tanh(z * (GELU_A + GELU_B * zz))
    return z * (0.5 + 0.5 * t)


def gelu_both(z):
    zz = z * z
    s = 0.5 + 0.5 * jnp.tanh(z * (GELU_A + GELU_B * zz))
    value = z * s
    slope = s + value * (1.0 - s) * (2.0 * GELU_A + 6.0 * GELU_B * zz)
    return value, slope


def pack_kernel(a_w1, c_w1, t_w1, a_w2, c_w2, t_w2, out, wide):
    for net in range(5):
        wide[...] = jnp.zeros_like(wide)
        if net == 0:
            wide[0:OBS, :] = a_w1[0:OBS, :]
            wide[BIAS_ROW : BIAS_ROW + 1, :] = a_w1[OBS:A_IN, :]
        else:
            source = c_w1 if net < 3 else t_w1
            wide[0:C_IN, :] = source[:, (net - 1) % 2, :]
        for tile in range(4):
            base = (net * 4 + tile) * HALF
            out[base : base + HALF, :] = jnp.transpose(wide[tile * 128 : tile * 128 + 128, :]).astype(B16)
        if net in (1, 2):
            base = PACK_ACT + (net - 1) * 32
            rows = lax.broadcasted_iota(jnp.int32, (32, 128), 0)
            out[base : base + 32, :] = jnp.where(rows < ACT, wide[OBS : OBS + 32, :], 0.0).astype(B16)
        for part in range(2):
            base = PACK_W2 + (net * 2 + part) * HALF
            lanes = slice(part * 128, part * 128 + 128)
            if net == 0:
                block = a_w2[:, lanes]
            else:
                block = (c_w2 if net < 3 else t_w2)[(net - 1) % 2, :, lanes]
            out[base : base + HALF, :] = block.astype(B16)


def pack_weights(a_w1, c_w1, t_w1, a_w2, c_w2, t_w2):
    return pl.pallas_call(
        pack_kernel,
        out_shape=jax.ShapeDtypeStruct((PACK_ROWS, 128), B16),
        scratch_shapes=[VMEM((K_PAD, 128), F32)],
        name="pack",
    )(a_w1, c_w1, t_w1, a_w2, c_w2, t_w2)


def step_kernel(
    rows_tile,
    chunk_ids,
    n_own,
    count_ref,
    state_ref,
    obs_ref,
    next_ref,
    action_ref,
    noise_ref,
    next_noise_ref,
    reward_ref,
    terminal_ref,
    pack_own,
    pack_par,
    a_head_ref,
    c_head_ref,
    t_head_ref,
    bias2_ref,
    t_bias2_ref,
    *rest,
):
    own_outs = rest[:n_own]
    par_out = rest[n_own]
    (
        w1t, w2, w2t, w1a, wht_a, wh_a, wht_c, wh_c, hb, b2b,
        xn, xd, xq,
        z1, z1q, z2, z2q, zn, zt, h1n, h2n, h1, h2, h1q, h2q, h1t, h2t,
        g1, g1q, g2, g2q,
        dz1, dz2, dzq1, dzq2,
        acc1, acc2, acc_ha, acc_hc, acc_b, acc_s, flat,
    ) = rest[n_own + 1 :]
    step = pl.program_id(0)
    n_steps = pl.num_programs(0)
    t_index = lax.axis_index("tensor")
    rt = rows_tile
    lane_tiles = rt // 128

    @pl.when(step == 0)
    def _():
        for net in range(5):
            for side, pack in enumerate((pack_own, pack_par)):
                rows = slice(net * H + side * HALF, net * H + side * HALF + HALF)
                for tile in range(4):
                    base = (net * 4 + tile) * HALF
                    w1t[rows, tile * 128 : tile * 128 + 128] = pack[base : base + HALF, :]
                for part in range(2):
                    base = PACK_W2 + (net * 2 + part) * HALF
                    w2[rows, part * 128 : part * 128 + 128] = pack[base : base + HALF, :]
        for side, pack in enumerate((pack_own, pack_par)):
            w1a[:, side * HALF : side * HALF + HALF] = pack[PACK_ACT:PACK_ROWS, :]
        for net in range(5):
            w2t[net * H : net * H + H, :] = jnp.transpose(w2[net * H : net * H + H, :])
        wht_a[...] = jnp.zeros_like(wht_a)
        hb[...] = jnp.zeros_like(hb)
        for part in range(2):
            rows = a_head_ref[part * ACT : part * ACT + ACT, :].astype(B16)
            wht_a[part * 24 : part * 24 + ACT, :] = rows[:, 0:H].astype(F32)
            hb[part * 24 : part * 24 + ACT, :] = jnp.broadcast_to(rows[:, H : H + 1].astype(F32), (ACT, 128))
        wh_a[...] = jnp.transpose(wht_a[...]).astype(B16)
        wht_c[...] = jnp.zeros_like(wht_c)
        for net in range(4):
            head = (c_head_ref if net < 2 else t_head_ref)[net % 2].astype(B16).astype(F32)
            wht_c[net * 8 : net * 8 + 2, :] = head[:, 0:H]
            hb[48 + net * 8 : 48 + net * 8 + 2, :] = jnp.broadcast_to(head[:, H : H + 1], (2, 128))
        wh_c[...] = jnp.transpose(wht_c[...]).astype(B16)
        for net in range(5):
            bias = bias2_ref[net : net + 1, :] if net < 3 else t_bias2_ref[net - 3 : net - 2, :]
            b2b[net * H : net * H + H, :] = jnp.transpose(jnp.broadcast_to(bias, (128, H)))
        tail = lax.broadcasted_iota(jnp.int32, (K_PAD - OBS, rt), 0)
        ones = jnp.where(tail == ACT, 1.0, 0.0).astype(B16)
        xn[OBS:K_PAD, :] = ones
        xd[OBS:K_PAD, :] = ones
        xq[OBS:K_PAD, :] = ones
        acc1[...] = jnp.zeros_like(acc1)
        acc2[...] = jnp.zeros_like(acc2)
        acc_ha[...] = jnp.zeros_like(acc_ha)
        acc_hc[...] = jnp.zeros_like(acc_hc)
        acc_b[...] = jnp.zeros_like(acc_b)
        acc_s[...] = jnp.zeros_like(acc_s)

    def lanes_of(column, rows):
        return jnp.concatenate([column] * lane_tiles, axis=1)

    def lane_sum(value):
        total = value[:, 0:128]
        for tile in range(1, lane_tiles):
            total = total + value[:, tile * 128 : tile * 128 + 128]
        return total

    def act_rows(source, target, slope, rows, bias_base=None):
        for r in range(0, rows, 16):
            z = source[r : r + 16, :]
            if bias_base is not None:
                z = z + lanes_of(b2b[bias_base + r : bias_base + r + 16, :], 16)
            if slope is None:
                target[r : r + 16, :] = gelu_only(z).astype(B16)
            else:
                value, grad = gelu_both(z)
                target[r : r + 16, :] = value.astype(B16)
                slope[r : r + 16, :] = grad

    xn[0:OBS, :] = next_ref[...]
    xd[0:OBS, :] = obs_ref[...]
    xq[0:OBS, :] = obs_ref[...]
    xd[OBS : OBS + ACT, :] = action_ref[...]

    index = t_index * (n_steps * rt) + step * rt + lax.broadcasted_iota(jnp.int32, (1, rt), 1)
    valid = (index < count_ref[0]).astype(F32)
    alpha = jnp.exp(jnp.full((1, rt), state_ref[0], F32))
    omega = state_ref[3] * state_ref[3]

    zn[...] = dot_nn(w1t[0:H, :], xn[...])
    z1[...] = dot_nn(w1t[0 : 3 * H, :], xd[...])
    act_rows(zn, h1n, None, H)
    act_rows(z1, h1, g1, 3 * H)
    zn[...] = dot_nn(w2t[0:H, :], h1n[...])
    for net in range(3):
        rows = slice(net * H, net * H + H)
        z2[rows, :] = dot_nn(w2t[rows, :], h1[rows, :])
    act_rows(zn, h2n, None, H, 0)
    act_rows(z2, h2, g2, 3 * H, 0)

    wht_a16 = wht_a[...].astype(B16)
    hb_a = lanes_of(hb[0:48, :], 48)

    def policy(hidden, noise):
        out = dot_nn(wht_a16, hidden) + hb_a
        pad = jnp.zeros((24 - ACT, rt), F32)
        eps = jnp.concatenate([noise, pad], axis=0)
        tl = jnp.tanh(out[24:48])
        ls = tl - 1.0
        spread = jnp.exp(ls) * eps
        u = out[0:24] + spread
        act = jnp.tanh(u)
        soft = jnp.maximum(-2.0 * u, 0.0) + jnp.log(1.0 + jnp.exp(-jnp.abs(2.0 * u)))
        terms = -0.5 * eps * eps - ls - HALF_LOG_TAU - 2.0 * (LOG_TWO - u - soft)
        keep = lax.broadcasted_iota(jnp.int32, (24, rt), 0) < ACT
        logp = jnp.sum(jnp.where(keep, terms, 0.0), axis=0, keepdims=True)
        return act, logp, tl, spread

    act_next, logp_next, _, _ = policy(h2n[...], next_noise_ref[...])
    act_new, logp_new, tl_new, spread_new = policy(h2[0:H, :], noise_ref[...])
    xn[OBS : OBS + ACT, :] = act_next[0:ACT].astype(B16)
    xq[OBS : OBS + ACT, :] = act_new[0:ACT].astype(B16)

    zt[...] = dot_nn(w1t[3 * H : 5 * H, :], xn[...])
    z1q[...] = dot_nn(w1t[H : 3 * H, :], xq[...])
    act_rows(zt, h1t, None, 2 * H)
    act_rows(z1q, h1q, g1q, 2 * H)
    for net in range(2):
        rows = slice(net * H, net * H + H)
        zt[rows, :] = dot_nn(w2t[(3 + net) * H : (4 + net) * H, :], h1t[rows, :])
        z2q[rows, :] = dot_nn(w2t[(1 + net) * H : (2 + net) * H, :], h1q[rows, :])
    act_rows(zt, h2t, None, 2 * H, 3 * H)
    act_rows(z2q, h2q, g2q, 2 * H, H)

    wht_c16 = wht_c[...].astype(B16)

    def head(net, hidden):
        rows = slice(net * 8, net * 8 + 8)
        return dot_nn(wht_c16[rows], hidden) + lanes_of(hb[48 + net * 8 : 56 + net * 8, :], 8)

    out_t = [head(2 + net, h2t[net * H : net * H + H, :])[0:1] for net in range(2)]
    out_d = [head(net, h2[(1 + net) * H : (2 + net) * H, :]) for net in range(2)]
    out_q = [head(net, h2q[net * H : net * H + H, :])[0:1] for net in range(2)]
    alive = 1.0 - terminal_ref[...].astype(F32)
    target = reward_ref[...] + GAMMA * alive * (jnp.minimum(out_t[0], out_t[1]) - alpha * logp_next)

    loss_row = valid * (alpha * logp_new - 0.5 * (out_q[0] + out_q[1]))
    sigma_row = jnp.zeros((1, rt), F32)
    next_row = valid * (logp_next - ACT)
    d_heads = []
    for net in range(2):
        log_sigma = jnp.tanh(out_d[net][1:2])
        sigma = jnp.exp(log_sigma)
        error = target - out_d[net][0:1]
        inverse = 1.0 / (sigma * sigma)
        scaled = error * inverse
        square = error * scaled
        loss_row = loss_row + valid * (omega * (0.5 * square + log_sigma))
        sigma_row = sigma_row + valid * sigma
        d_q = -(omega * valid) * scaled
        d_s = (omega * valid) * (1.0 - square) * (1.0 - log_sigma * log_sigma)
        d_heads.append(jnp.concatenate([d_q, d_s, jnp.zeros((6, rt), F32)], axis=0).astype(B16))
    acc_s[64:65, :] += lane_sum(loss_row)
    acc_s[72:73, :] += lane_sum(sigma_row)
    acc_s[80:81, :] += lane_sum(next_row)

    for net in range(2):
        rows = slice((1 + net) * H, (2 + net) * H)
        acc_s[48 + net * 8 : 56 + net * 8, :] += lane_sum(d_heads[net].astype(F32))
        acc_hc[net * 8 : net * 8 + 8, :] += dot_nt(d_heads[net], h2[rows, :])
        z2[rows, :] = dot_nn(wh_c[:, net * 8 : net * 8 + 8], d_heads[net])
    d_new = -0.5 * valid

    def back_second(source, slope, target, rows, acc):
        for r in rows:
            d_pre = source[r : r + 16, :] * slope[r : r + 16, :]
            target[r : r + 16, :] = d_pre.astype(B16)
            acc_b[r : r + 16, :] += lane_sum(d_pre)

    def back_first(source, slope, target, first, last, shift=0):
        for r in range(first, last, 16):
            target[r : r + 16, :] = (source[r + shift : r + shift + 16, :] * slope[r : r + 16, :]).astype(B16)

    back_second(z2, g2, dz2, range(H, 3 * H, 16), acc_b)
    for net in range(2):
        for r in range(0, H, 16):
            column = wh_c[r : r + 16, net * 8 : net * 8 + 1].astype(F32)
            d_hidden = column * d_new
            base = net * H + r
            dzq2[base : base + 16, :] = (d_hidden * g2q[base : base + 16, :]).astype(B16)
    for net in range(2):
        rows = slice(net * H, net * H + H)
        rows_c = slice((1 + net) * H, (2 + net) * H)
        z1q[rows, :] = dot_nn(w2[rows_c, :], dzq2[rows, :])
        z1[rows_c, :] = dot_nn(w2[rows_c, :], dz2[rows_c, :])
    back_first(z1q, g1q, dzq1, 0, 2 * H)
    back_first(z1, g1, dz1, H, 3 * H)
    d_act = dot_nn(w1a[0:32, :], dzq1[0:H, :]) + dot_nn(w1a[32:64, :], dzq1[H : 2 * H, :])
    d_act = d_act[0:24]

    d_logp = alpha * valid
    d_u = d_act * (1.0 - act_new * act_new) + (2.0 * d_logp) * act_new
    d_ls = (d_u * spread_new - d_logp) * (1.0 - tl_new * tl_new)
    d_out = jnp.concatenate([d_u, d_ls], axis=0).astype(B16)
    acc_s[0:48, :] += lane_sum(d_out.astype(F32))
    acc_ha[...] += dot_nt(d_out, h2[0:H, :])
    z2[0:H, :] = dot_nn(wh_a[...], d_out)
    back_second(z2, g2, dz2, range(0, H, 16), acc_b)
    z1[0:H, :] = dot_nn(w2[0:H, :], dz2[0:H, :])
    back_first(z1, g1, dz1, 0, H)

    for net in range(3):
        rows = slice(net * H, net * H + H)
        acc2[rows, :] += dot_nt(h1[rows, :], dz2[rows, :])
    acc1[...] += dot_nt(xd[0:K_USE, :], dz1[...])

    @pl.when(step == n_steps - 1)
    def _():
        d_index = lax.axis_index("dp")
        flat[:, FLAT_SMALL:FLAT_ROWS, :] = jnp.zeros((2, FLAT_ROWS - FLAT_SMALL, 128), F32)
        flat[:, FLAT_AW1 - 8 : FLAT_AW1, :] = jnp.zeros((2, 8, 128), F32)
        flat[:, FLAT_AW2 - 8 : FLAT_AW2, :] = jnp.zeros((2, 8, 128), F32)
        sums = jnp.sum(jnp.transpose(acc_s[...]), axis=0, keepdims=True)
        lane = lax.broadcasted_iota(jnp.int32, (1, 128), 1)
        keep = (lane < ACT) | ((lane >= 24) & (lane < 24 + ACT)) | ((lane >= 48) & (lane < 50))
        keep = keep | ((lane >= 56) & (lane < 58)) | (lane == LANE_LOSS) | (lane == LANE_SIGMA) | (lane == LANE_NEXT)
        sums = jnp.where(keep, sums, 0.0)
        sums = jnp.where(lane == LANE_COUNT, 0.5 * count_ref[0].astype(F32), sums)
        for side in range(2):
            lanes = slice(side * HALF, side * HALF + HALF)
            for net in range(2):
                columns = slice((1 + net) * H + side * HALF, (1 + net) * H + side * HALF + HALF)
                flat[side, pl.ds(FLAT_CW1 + net, C_IN, stride=2), :] = acc1[0:C_IN, columns]
            flat[side, FLAT_AW1 : FLAT_AW1 + OBS, :] = acc1[0:OBS, lanes]
            flat[side, FLAT_AW1 + OBS : FLAT_AW1 + A_IN, :] = acc1[BIAS_ROW : BIAS_ROW + 1, lanes]
            for net in range(3):
                rows = slice(net * H + side * HALF, net * H + side * HALF + HALF)
                for part in range(2):
                    base = FLAT_AW2 + (net * 2 + part) * HALF
                    flat[side, base : base + HALF, :] = acc2[rows, part * 128 : part * 128 + 128]
            for part in range(2):
                cols = slice(part * 128, part * 128 + 128)
                base = FLAT_AHEAD + part * 40
                flat[side, base : base + ACT, :] = acc_ha[0:ACT, cols]
                flat[side, base + ACT : base + 2 * ACT, :] = acc_ha[24 : 24 + ACT, cols]
                for net in range(2):
                    base = FLAT_CHEAD + part * 4 + net * 2
                    flat[side, base : base + 2, :] = acc_hc[net * 8 : net * 8 + 2, cols]
            for net in range(3):
                for part in range(2):
                    rows = slice(net * H + part * 128, net * H + part * 128 + 128)
                    row = FLAT_B2 + part * 4 + net
                    flat[side, row : row + 1, :] = jnp.sum(jnp.transpose(acc_b[rows, :]), axis=0, keepdims=True)
            flat[side, FLAT_SUMS : FLAT_SUMS + 1, :] = sums
        size = FLAT_ROWS // len(chunk_ids)
        per = len(chunk_ids) // n_own
        for place, rel in enumerate(chunk_ids):
            start = pl.multiple_of(jnp.bitwise_xor(d_index, rel) * size, size)
            own_outs[place // per][(place % per) * size : (place % per) * size + size, :] = flat[0, pl.ds(start, size), :]
            par_out[place * size : place * size + size, :] = flat[1, pl.ds(start, size), :]


def run_step(groups, arrays, pack_own, pack_par, small, count, state):
    obs, next_obs, action, noise, next_noise, reward, terminal = arrays
    rows = obs.shape[1] // groups["tensor"]
    rt = min(512, rows)
    steps = rows // rt
    chunk_ids, n_own = groups["order"], groups["first"]

    def tile(height):
        return pl.BlockSpec((height, rt), lambda i: (0, lax.axis_index("tensor") * steps + i))

    whole = pl.BlockSpec(memory_space=VMEM)
    smem = pl.BlockSpec(memory_space=pltpu.SMEM)
    scratch = [
        VMEM((5 * H, K_PAD), B16), VMEM((5 * H, H), B16), VMEM((5 * H, H), B16), VMEM((64, H), B16),
        VMEM((48, H), F32), VMEM((H, 48), B16), VMEM((32, H), F32), VMEM((H, 32), B16),
        VMEM((80, 128), F32), VMEM((5 * H, 128), F32),
        VMEM((K_PAD, rt), B16), VMEM((K_PAD, rt), B16), VMEM((K_PAD, rt), B16),
        VMEM((3 * H, rt), F32), VMEM((2 * H, rt), F32), VMEM((3 * H, rt), F32), VMEM((2 * H, rt), F32),
        VMEM((H, rt), F32), VMEM((2 * H, rt), F32),
        VMEM((H, rt), B16), VMEM((H, rt), B16), VMEM((3 * H, rt), B16), VMEM((3 * H, rt), B16),
        VMEM((2 * H, rt), B16), VMEM((2 * H, rt), B16), VMEM((2 * H, rt), B16), VMEM((2 * H, rt), B16),
        VMEM((3 * H, rt), F32), VMEM((2 * H, rt), F32), VMEM((3 * H, rt), F32), VMEM((2 * H, rt), F32),
        VMEM((3 * H, rt), B16), VMEM((3 * H, rt), B16), VMEM((2 * H, rt), B16), VMEM((2 * H, rt), B16),
        VMEM((K_USE, 3 * H), F32), VMEM((3 * H, H), F32), VMEM((48, H), F32), VMEM((16, H), F32),
        VMEM((3 * H, 128), F32), VMEM((128, 128), F32), VMEM((2, FLAT_ROWS, 128), F32),
    ]
    outs = [jax.ShapeDtypeStruct((FLAT_ROWS // n_own, 128), F32)] * n_own + [jax.ShapeDtypeStruct((FLAT_ROWS, 128), F32)]
    return pl.pallas_call(
        functools.partial(step_kernel, rt, chunk_ids, n_own),
        grid=(steps,),
        in_specs=[smem, smem, tile(OBS), tile(OBS), tile(ACT), tile(ACT), tile(ACT), tile(1), tile(1)] + [whole] * 7,
        out_specs=[whole] * (n_own + 1),
        out_shape=outs,
        scratch_shapes=scratch,
        compiler_params=pltpu.CompilerParams(vmem_limit_bytes=VMEM_LIMIT),
        name="step",
    )(count, state, obs, next_obs, action, noise, next_noise, reward, terminal, pack_own, pack_par, *small)


def last_sum_kernel(size, n_in, *refs):
    total = refs[0][...]
    for ref in refs[1:n_in]:
        total = total + ref[...]
    out, square = refs[n_in:]
    out[...] = total
    row = lax.axis_index("dp") * size + lax.broadcasted_iota(jnp.int32, (size, 128), 0)
    lane = lax.broadcasted_iota(jnp.int32, (size, 128), 1)
    weight = jnp.where(row < FLAT_SMALL, 1.0, 0.5)
    weight = jnp.where((row >= FLAT_SUMS) & (lane >= LANE_LOSS), 0.0, weight)
    squares = total * total * weight
    part = squares[0:8]
    for r in range(8, size, 8):
        part = part + squares[r : r + 8]
    square[...] = part


def last_sum(values, size):
    return pl.pallas_call(
        functools.partial(last_sum_kernel, size, len(values)),
        out_shape=[jax.ShapeDtypeStruct((size, 128), F32), jax.ShapeDtypeStruct((8, 128), F32)],
        name="lastsum",
    )(*values)


def one_minus_power(gap, exponent):
    total = jnp.float32(0.0)
    for bit in range(30, -1, -1):
        total = total * (2.0 - total)
        total = jnp.where((exponent >> bit) & 1 == 1, total + gap * (1.0 - total), total)
    return total


def update_kernel(order, n_parts, sizes, *refs):
    parts = refs[:n_parts]
    (
        step_ref, state_ref,
        a_w1, a_w1_m, a_w2, a_w2_m, a_head, a_head_m,
        c_w1, c_w1_m, c_w2, c_w2_m, c_head, c_head_m, bias2, bias2_m,
        t_w1, t_w2, t_head, t_bias2,
        o_a_w1, o_a_w1_f, o_a_w1_s, o_a_w2, o_a_w2_f, o_a_w2_s, o_a_head, o_a_head_f, o_a_head_s,
        o_c_w1, o_c_w1_f, o_c_w1_s, o_c_w2, o_c_w2_f, o_c_w2_s, o_c_head, o_c_head_f, o_c_head_s,
        o_bias2, o_bias2_f, o_bias2_s, o_scalars, o_norm,
        flat,
    ) = refs[n_parts:]
    size, stride = sizes
    d_index = lax.axis_index("dp")
    per = len(order) // n_parts
    square = jnp.zeros((8, 128), F32)
    for place, rel in enumerate(order):
        start = pl.multiple_of(jnp.bitwise_xor(d_index, rel) * size, size)
        base = (place % per) * stride
        flat[pl.ds(start, size), :] = parts[place // per][base : base + size, :]
        square = square + parts[place // per][base + size : base + size + 8, :]
    sums = flat[FLAT_SUMS : FLAT_SUMS + 1, :]
    lane = lax.broadcasted_iota(jnp.int32, (1, 128), 1)

    def pick(index):
        return jnp.sum(jnp.where(lane == index, sums, 0.0), axis=1, keepdims=True)

    loss_sum, sigma_sum, next_sum, count = (pick(i) for i in (LANE_LOSS, LANE_SIGMA, LANE_NEXT, LANE_COUNT))
    inverse = 1.0 / count
    total = jnp.sum(jnp.sum(square, axis=0, keepdims=True), axis=1, keepdims=True)
    norm = jnp.sqrt(total) * inverse
    clip = jnp.minimum(1.0, CLIP / (norm + 1e-06))
    scale = clip * inverse
    t = step_ref[0]
    first_fix = one_minus_power(jnp.float32(0.1), t)
    second_fix = one_minus_power(jnp.float32(0.001), t)
    unfix_one = 1.0 / jnp.full((1, 1), first_fix, F32)
    unfix_two = 1.0 / jnp.full((1, 1), second_fix, F32)

    def adam(weight, first, second, grad, decay=DECAY):
        first = BETA_ONE * first + (1.0 - BETA_ONE) * grad
        second = BETA_TWO * second + (1.0 - BETA_TWO) * (grad * grad)
        step = first * unfix_one / (jnp.sqrt(second * unfix_two) + ADAM_EPS)
        if decay:
            step = step + decay * weight
        return weight - RATE * step, first, second

    def polyak(target, new):
        return (1.0 - RHO) * target + RHO * new

    new, first, second = adam(a_w1[...], a_w1_m[:, 0, :], a_w1_m[:, 1, :], flat[FLAT_AW1 : FLAT_AW1 + A_IN, :] * scale)
    o_a_w1[...] = new
    o_a_w1_f[...] = first
    o_a_w1_s[...] = second
    for net in range(3):
        for part in range(2):
            lanes = slice(part * 128, part * 128 + 128)
            base = FLAT_AW2 + (net * 2 + part) * HALF
            grad = flat[base : base + HALF, :] * scale
            if net == 0:
                new, first, second = adam(a_w2[:, lanes], a_w2_m[0, :, lanes], a_w2_m[1, :, lanes], grad)
                o_a_w2[:, lanes] = new
                o_a_w2_f[:, lanes] = first
                o_a_w2_s[:, lanes] = second
            else:
                c = net - 1
                new, first, second = adam(c_w2[c, :, lanes], c_w2_m[0, c, :, lanes], c_w2_m[1, c, :, lanes], grad)
                o_c_w2[c, :, lanes] = new
                o_c_w2[2 + c, :, lanes] = polyak(t_w2[c, :, lanes], new)
                o_c_w2_f[c, :, lanes] = first
                o_c_w2_s[c, :, lanes] = second
    for c in range(2):
        grad = flat[pl.ds(FLAT_CW1 + c, C_IN, stride=2), :] * scale
        new, first, second = adam(c_w1[:, c, :], c_w1_m[0, :, c, :], c_w1_m[1, :, c, :], grad)
        o_c_w1[:, c, :] = new
        o_c_w1[:, 2 + c, :] = polyak(t_w1[:, c, :], new)
        o_c_w1_f[:, c, :] = first
        o_c_w1_s[:, c, :] = second
    columns = jnp.transpose(jnp.broadcast_to(sums, (128, 128)))
    bias_a = jnp.concatenate([columns[0:ACT, 0:1], columns[24 : 24 + ACT, 0:1]], axis=0)
    grad = jnp.concatenate(
        [flat[FLAT_AHEAD : FLAT_AHEAD + 2 * ACT, :], flat[FLAT_AHEAD + 40 : FLAT_AHEAD + 40 + 2 * ACT, :], bias_a], axis=1
    )
    new, first, second = adam(a_head[...], a_head_m[:, 0, :], a_head_m[:, 1, :], grad * scale)
    o_a_head[...] = new
    o_a_head_f[...] = first
    o_a_head_s[...] = second
    for c in range(2):
        rows = slice(FLAT_CHEAD + c * 2, FLAT_CHEAD + c * 2 + 2)
        rows_b = slice(FLAT_CHEAD + 4 + c * 2, FLAT_CHEAD + 6 + c * 2)
        bias_c = columns[LANE_C + 8 * c : LANE_C + 8 * c + 2, 0:1]
        grad = jnp.concatenate([flat[rows, :], flat[rows_b, :], bias_c], axis=1) * scale
        new, first, second = adam(c_head[c], c_head_m[0, c], c_head_m[1, c], grad)
        o_c_head[c] = new
        o_c_head[2 + c] = polyak(t_head[c], new)
        o_c_head_f[c] = first
        o_c_head_s[c] = second
    grad = jnp.concatenate([flat[FLAT_B2 : FLAT_B2 + 3, :], flat[FLAT_B2 + 4 : FLAT_B2 + 7, :]], axis=1) * scale
    new, first, second = adam(bias2[...], bias2_m[:, 0, :], bias2_m[:, 1, :], grad)
    o_bias2[0:3, :] = new
    o_bias2[3:5, :] = polyak(t_bias2[...], new[1:3])
    o_bias2_f[...] = first
    o_bias2_s[...] = second
    log_alpha = jnp.full((1, 1), state_ref[0], F32)
    g_alpha = -next_sum
    new, first, second = adam(
        log_alpha, jnp.full((1, 1), state_ref[1], F32), jnp.full((1, 1), state_ref[2], F32), g_alpha * inverse, 0.0
    )
    stat = (1.0 - TAU_STAT) * state_ref[3] + TAU_STAT * sigma_sum / (2.0 * count)
    loss = (loss_sum + log_alpha * g_alpha) * inverse
    for place, value in enumerate((new, first, second, stat, loss)):
        o_scalars[place] = value[0, 0]
    o_norm[0] = norm[0, 0]


def kernel_view(value, order):
    return jnp.transpose(value, order)


def shards(
    groups, obs, action, next_obs, reward, terminal, noise, next_noise, counts, step_count,
    a_w1, a_w2, a_head, c_w1, c_w2, c_head, bias2, tc_w1, tc_w2, tc_head, tc_bias2,
    a_w1_mom, a_w2_mom, a_head_mom, c_w1_mom, c_w2_mom, c_head_mom, bias2_mom, state,
):
    n_dp = groups["dp"]
    swap = [(0, 1), (1, 0)]

    def partner(value):
        return lax.ppermute(value, "tensor", swap)

    def across(value, mask):
        return lax.ppermute(value, "dp", [(i, i ^ mask) for i in range(n_dp)])

    tr = jnp.transpose
    c_w1v, tc_w1v = tr(c_w1, (1, 0, 2)), tr(tc_w1, (1, 0, 2))
    a_headv, c_headv, tc_headv = tr(a_head), tr(c_head, (0, 2, 1)), tr(tc_head, (0, 2, 1))
    pack = pack_weights(a_w1, c_w1v, tc_w1v, a_w2, c_w2, tc_w2)
    pack_par = partner(pack)
    arrays = (
        tr(obs), tr(next_obs), tr(action), tr(noise), tr(next_noise), reward.reshape(1, -1), terminal.reshape(1, -1),
    )
    small = (a_headv, c_headv, tc_headv, bias2, tc_bias2)
    outs = run_step(groups, arrays, pack, pack_par, small, counts, state)
    own, par = outs[:-1], outs[-1]
    received = partner(par)
    size = FLAT_ROWS // len(own)
    values = [item + received[i * size : i * size + size] for i, item in enumerate(own)]

    phases = groups["phases"]
    for number, (shift, width) in enumerate(phases):
        ways = 1 << width
        got = [values[0]] + [across(values[k], k << shift) for k in range(1, ways)]
        if number < len(phases) - 1:
            following = 1 << phases[number + 1][1]
            size = got[0].shape[0] // following
            values = [sum(item[j * size : j * size + size] for item in got) for j in range(following)]
        else:
            size = got[0].shape[0]
            chunk, square = last_sum(got, size)
    square = square + partner(square)
    block = jnp.concatenate([chunk, square])
    for number, (shift, width) in reversed(list(enumerate(phases))):
        ways = 1 << width
        got = [block] + [across(block, k << shift) for k in range(1, ways)]
        if number:
            block = jnp.concatenate(got)
    parts = got

    sds = jax.ShapeDtypeStruct
    shapes = [
        (A_IN, HALF)] * 3 + [(HALF, H)] * 3 + [(2 * ACT, H + 1)] * 3 + [
        (C_IN, 4, HALF), (C_IN, 2, HALF), (C_IN, 2, HALF),
        (4, HALF, H), (2, HALF, H), (2, HALF, H),
        (4, 2, H + 1), (2, 2, H + 1), (2, 2, H + 1),
        (5, H), (3, H), (3, H), (5,), (1,),
    ]
    whole = pl.BlockSpec(memory_space=VMEM)
    smem = pl.BlockSpec(memory_space=pltpu.SMEM)
    res = pl.pallas_call(
        functools.partial(update_kernel, groups["order"], len(parts), (size, size + 8)),
        in_specs=[whole] * len(parts) + [smem, smem] + [whole] * 18,
        out_specs=[whole] * 21 + [smem, smem],
        out_shape=[sds(s, F32) for s in shapes],
        scratch_shapes=[VMEM((FLAT_ROWS, 128), F32)],
        compiler_params=pltpu.CompilerParams(vmem_limit_bytes=VMEM_LIMIT),
        name="update",
    )(
        *parts, step_count, state,
        a_w1, tr(a_w1_mom, (1, 0, 2)), a_w2, a_w2_mom, a_headv, tr(a_head_mom, (2, 0, 1)),
        c_w1v, tr(c_w1_mom, (0, 2, 1, 3)), c_w2, c_w2_mom, c_headv, tr(c_head_mom, (0, 1, 3, 2)),
        bias2, tr(bias2_mom, (1, 0, 2)), tc_w1v, tc_w2, tc_headv, tc_bias2,
    )
    res = list(res)
    for place in (6, 7, 8):
        res[place] = tr(res[place])
    for place in (9, 10, 11):
        res[place] = tr(res[place], (1, 0, 2))
    for place in (15, 16, 17):
        res[place] = tr(res[place], (0, 2, 1))
    return tuple(res)


def plan(mesh):
    n_dp = mesh.shape["dp"]
    bits = n_dp.bit_length() - 1
    assert n_dp == 1 << bits and mesh.shape["tensor"] == 2
    phases = []
    low = 0
    while low < bits:
        width = min(2, bits - low)
        phases.append((low, width))
        low += width
    order = [0]
    for shift, width in phases:
        order = [rel | (k << shift) for rel in order for k in range(1 << width)]
    return {
        "dp": n_dp, "tensor": mesh.shape["tensor"], "phases": phases, "order": tuple(order), "first": 1 << phases[0][1],
    }


def solution(mesh):
    in_specs = (
        P("dp", None), P("dp", None), P("dp", None), P("dp"), P("dp"), P("dp", None), P("dp", None), P("dp"), P(),
        P(None, "tensor"), P("tensor", None), P(), P(None, None, "tensor"), P(None, "tensor", None), P(), P(),
        P(None, None, "tensor"), P(None, "tensor", None), P(), P(),
        P(None, None, "tensor"), P(None, "tensor", None), P(), P(None, None, None, "tensor"),
        P(None, None, "tensor", None), P(), P(), P(),
    )
    out_specs = (
        P(None, "tensor"), P(None, "tensor"), P(None, "tensor"),
        P("tensor", None), P("tensor", None), P("tensor", None),
        P(), P(), P(),
        P(None, None, "tensor"), P(None, None, "tensor"), P(None, None, "tensor"),
        P(None, "tensor", None), P(None, "tensor", None), P(None, "tensor", None),
        P(), P(), P(), P(), P(), P(), P(), P(),
    )
    return jax.shard_map(
        functools.partial(shards, plan(mesh)), mesh=mesh, in_specs=in_specs, out_specs=out_specs, check_vma=False
    )
```

time: 475 us -> 107 us (0.23); the launches traced: 467 us -> 107 us
  blocking collectives: 128 us -> 0 us
  matrix products: 114 us -> 0 us
  other arithmetic: 94.4 us -> 3.53 us
  local copies, waits for them, and re-layouts: 69.6 us -> 3.21 us
  Pallas kernels: 0 us -> 41.4 us
  between operations: 38 us -> 2.18 us
  waiting for transfers between devices: 22.1 us -> 39.5 us
  starting transfers between devices: 1.3 us -> 16.9 us
    psum x3 -> x0, blocking collectives: 123 us -> none  [the longest x1 78 us: shards(): count = lax.psum(count_local.astype(F32), 'dp')]
    dot_general x30 -> x0, matrix products: 111 us -> none  [the longest x4 21.5 us: net_forward(): jnp.einsum('crh,chg->crg', h_first, w_second, preferred_element_type=F32)]
    pallas_call x0 -> x4, Pallas kernels: none -> 41.4 us  [the longest x1 28.1 us: run_step(): pl.pallas_call(functools.partial(step_kernel, rt, chunk_ids, n_own), grid...]
    ppermute x0 -> x15, waiting for transfers between devices: none -> 39.5 us  [the longest x12 34.7 us: across(): return lax.ppermute(value, 'dp', [(i, i ^ mask) for i in range(n_dp)])]
    unnamed x201 -> x19, local copies, waits for them, and re-layouts: 34.2 us -> 3.21 us
    unnamed x8 -> x1, other arithmetic: 23.4 us -> 0.69 us
    convert_element_type x10 -> x0, other arithmetic: 22.7 us -> none  [the longest x2 14.7 us: net_forward(): h_second = with_ones(jax.nn.gelu(pre_second).astype(B16))]
    reduce_scatter x6 -> x0, waiting for transfers between devices: 21.2 us -> none  [the longest x4 14.7 us: reduce_layer(): lax.psum_scatter(partial_value, 'tensor', scatter_dimension=1, tiled=True)]
  transfers between devices with their start and end apart: 11 -> 15, of which waited for: 3 -> 13; matrix products, arithmetic and copies ran while one was open for 27% -> 1% of each run, Pallas kernels for 0% -> 0%
where the time goes in v1:
time: 107 us
  Pallas kernels  41.4 us (39%)
  waiting for transfers between devices  39.5 us (37%)
  starting transfers between devices  16.9 us (16%)
  other arithmetic  3.53 us (3%)
  local copies, waits for them, and re-layouts  3.21 us (3%)
  between operations  2.18 us (2%)
    ppermute x12, waiting for transfers between devices, across(): return lax.ppermute(value, 'dp', [(i, i ^ mask) for i in range(n_dp)])  34.7 us
    pallas_call x1, Pallas kernels, run_step(): pl.pallas_call(functools.partial(step_kernel, rt, chunk_ids, n_own), grid...  28.1 us
    ppermute x12, starting transfers between devices, across(): return lax.ppermute(value, 'dp', [(i, i ^ mask) for i in range(n_dp)])  15.9 us
    pallas_call x1, Pallas kernels, shards(): pl.pallas_call(functools.partial(update_kernel, groups['order'], len(part...  8.79 us
    ppermute x3, waiting for transfers between devices, partner(): return lax.ppermute(value, 'tensor', swap)  4.8 us
    unnamed x19, local copies, waits for them, and re-layouts  3.21 us
    pallas_call x1, Pallas kernels, pack_weights(): pl.pallas_call(pack_kernel, out_shape=jax.ShapeDtypeStruct((PACK_ROWS, 12...  2.9 us
  transfers between devices with their start and end apart: 15, of which 13 were waited for; matrix products, arithmetic and copies ran while one was open for 1% of the time, Pallas kernels for 0%

profile of v1, /device:TPU:0, one launch (start us, length us, event | category | flops | bytes accessed | tf_op | source)
XLA Modules:
  0.0 106.7 jit_solution(16512502794730008182)
XLA Ops:
  0.7 2.9 %pack.1.pack_own = bf16[3904,128]{1,0:T(8,128)(2,1)} custom-call(f32[377,128]{1,0:T(8,128)} %refs_6_.1, f32[394,2,128]{2,1,0:T(2,128)} %bitcast.28, f32[394,2,128]{2,1,0:T(2,128)} %bitcast.30, f32[128,256]{1,0:T(8,128)} %refs_8_.1, f32[2,128,256]{2,1,0:T(8,128)} %refs_14_.1, f32[2,128,256]{2,1,0:T(8,128)} %refs_21_.1), custom_call_target="tpu_custom_call" | custom-call | tf_op jit(solution)/shard_map/pack/pallas_call | solution.py:109
  3.6 0.5 collective-permute-start
  4.7 1.8 %collective-permute-done.pack_par = bf16[3904,128]{1,0:T(8,128)(2,1)S(1)} collective-permute-done((bf16[3904,128]{1,0:T(8,128)(2,1)}, bf16[3904,128]{1,0:T(8,128)(2,1)S(1)}, u32[]{:S(2)}, u32[]{:S(2)}) %collective-permute-start) | collective-permute-done | bytes 999456 | tf_op jit(solution)/shard_map/ppermute | solution.py:602
  6.5 1.0 copy-done
  7.4 28.1 %step.1 = (f32[512,128]{1,0:T(8,128)}, f32[512,128]{1,0:T(8,128)}, f32[512,128]{1,0:T(8,128)}, f32[512,128]{1,0:T(8,128)}, f32[2048,128]{1,0:T(8,128)}) custom-call(s32[1]{0:T(128)S(6)} %copy.55.count_ref, f32[4]{0:T(128)} %refs_5_.1, bf16[376,4096]{1,0:T(8,128)(2,1)} %bitcast.26, bf16[376,4096]{1,0:T(8,128)(2,1)} %bitcast.27, bf16[17,4096]{1,0:T(8,128)(2,1)} %bitcast.38, ...), custom_call_target="tpu_custom_call" | custom-call | tf_op jit(solution)/shard_map/step/pallas_call | solution.py:429
  35.6 0.4 collective-permute-start.1
  36.0 2.5 %collective-permute-done.1 = f32[2048,128]{1,0:T(8,128)S(1)} collective-permute-done((f32[2048,128]{1,0:T(8,128)}, f32[2048,128]{1,0:T(8,128)S(1)}, u32[]{:S(2)}, u32[]{:S(2)}) %collective-permute-start.1) | collective-permute-done | bytes 1048608 | tf_op jit(solution)/shard_map/ppermute | solution.py:602
  38.5 1.3 %slice_add_fusion.3 = (f32[512,128]{1,0:T(8,128)S(1)}, f32[512,128]{1,0:T(8,128)S(1)}, f32[512,128]{1,0:T(8,128)S(1)}, f32[512,128]{1,0:T(8,128)S(1)}) fusion(f32[512,128]{1,0:T(8,128)} %get-tuple-element.53, f32[2048,128]{1,0:T(8,128)S(1)} %collective-permute-done.1, f32[512,128]{1,0:T(8,128)} %get-tuple-element.57, f32[512,128]{1,0:T(8,128)} %get-tuple-element.56, ...), kind=kLoop, calls=%fused_computation.3 | loop fusion | flops 262144 | bytes 3145728 | tf_op jit(solution)/shard_map/add | solution.py:620
  39.8 3.9 %collective-permute-start.4 = (f32[512,128]{1,0:T(8,128)S(1)}, f32[512,128]{1,0:T(8,128)S(1)}, u32[]{:S(2)}, u32[]{:S(2)}) collective-permute-start(f32[512,128]{1,0:T(8,128)S(1)} %get-tuple-element.90), channel_id=1, source_target_pairs={{0,6},{2,4},{4,2},{6,0},{8,14},{10,12},{12,10},{14,8},{16,22},{18,... | collective-permute-start | bytes 786440 | tf_op jit(solution)/shard_map/ppermute | solution.py:605
  43.7 0.5 collective-permute-start.3
  44.2 0.1 collective-permute-start.2
  44.3 6.6 %collective-permute-done.4 = f32[512,128]{1,0:T(8,128)S(1)} collective-permute-done((f32[512,128]{1,0:T(8,128)S(1)}, f32[512,128]{1,0:T(8,128)S(1)}, u32[]{:S(2)}, u32[]{:S(2)}) %collective-permute-start.4) | collective-permute-done | bytes 262176 | tf_op jit(solution)/shard_map/ppermute | solution.py:605
  50.9 5.0 %collective-permute-done.3 = f32[512,128]{1,0:T(8,128)S(1)} collective-permute-done((f32[512,128]{1,0:T(8,128)S(1)}, f32[512,128]{1,0:T(8,128)S(1)}, u32[]{:S(2)}, u32[]{:S(2)}) %collective-permute-start.3) | collective-permute-done | bytes 262176 | tf_op jit(solution)/shard_map/ppermute | solution.py:605
  55.9 0.3 collective-permute-done.2
  56.2 0.7 slice_add_fusion.4
  56.9 3.6 %collective-permute-start.7 = (f32[128,128]{1,0:T(8,128)S(1)}, f32[128,128]{1,0:T(8,128)S(1)}, u32[]{:S(2)}, u32[]{:S(2)}) collective-permute-start(f32[128,128]{1,0:T(8,128)S(1)} %get-tuple-element.85), channel_id=1, source_target_pairs={{0,24},{2,26},{4,28},{6,30},{8,16},{10,18},{12,20},{14,22},{16,8},... | collective-permute-start | bytes 196616 | tf_op jit(solution)/shard_map/ppermute | solution.py:605
  60.5 0.0 collective-permute-start.6
  60.5 0.8 collective-permute-start.5
  61.3 2.0 %collective-permute-done.7.refs_3_ = f32[128,128]{1,0:T(8,128)S(1)} collective-permute-done((f32[128,128]{1,0:T(8,128)S(1)}, f32[128,128]{1,0:T(8,128)S(1)}, u32[]{:S(2)}, u32[]{:S(2)}) %collective-permute-start.7) | collective-permute-done | bytes 65568 | tf_op jit(solution)/shard_map/ppermute | solution.py:605
  63.3 2.9 %collective-permute-done.6.refs_2_ = f32[128,128]{1,0:T(8,128)S(1)} collective-permute-done((f32[128,128]{1,0:T(8,128)S(1)}, f32[128,128]{1,0:T(8,128)S(1)}, u32[]{:S(2)}, u32[]{:S(2)}) %collective-permute-start.6) | collective-permute-done | bytes 65568 | tf_op jit(solution)/shard_map/ppermute | solution.py:605
  66.2 0.0 collective-permute-done.5.refs_1_
  66.2 0.0 copy-done.5
  66.2 0.6 copy-done.6
  66.8 0.0 copy-done.7
  66.9 1.6 %lastsum.1 = (f32[128,128]{1,0:T(8,128)}, f32[8,128]{1,0:T(8,128)}) custom-call(f32[128,128]{1,0:T(8,128)} %get-tuple-element.88.refs_0_, f32[128,128]{1,0:T(8,128)} %copy-done.7, f32[128,128]{1,0:T(8,128)} %copy-done.6, f32[128,128]{1,0:T(8,128)} %copy-done.5), custom_call_target="tpu_custom_call" | custom-call | tf_op jit(solution)/shard_map/lastsum/pallas_call | solution.py:459
  68.4 0.0 collective-permute-start.8
  68.5 0.8 constant_dynamic-update-slice_fusion.4
  69.3 0.5 collective-permute-done.8
  69.8 0.7 constant_dynamic-update-slice_fusion.3
  70.5 0.8 pad_maximum_fusion
  71.4 1.1 collective-permute-start.9
  72.4 1.9 %collective-permute-start.11 = (f32[136,128]{1,0:T(8,128)S(1)}, f32[136,128]{1,0:T(8,128)S(1)}, u32[]{:S(2)}, u32[]{:S(2)}) collective-permute-start(f32[136,128]{1,0:T(8,128)S(1)} %pad_maximum_fusion), channel_id=1, source_target_pairs={{0,24},{2,26},{4,28},{6,30},{8,16},{10,18},{12,20},{14,22},{16,8},... | collective-permute-start | bytes 208904 | tf_op jit(solution)/shard_map/ppermute | solution.py:605
  74.3 0.5 collective-permute-start.10
  74.8 0.8 collective-permute-done.9
  75.7 5.9 %collective-permute-done.10 = f32[136,128]{1,0:T(8,128)S(1)} collective-permute-done((f32[136,128]{1,0:T(8,128)S(1)}, f32[136,128]{1,0:T(8,128)S(1)}, u32[]{:S(2)}, u32[]{:S(2)}) %collective-permute-start.10) | collective-permute-done | bytes 69664 | tf_op jit(solution)/shard_map/ppermute | solution.py:605
  81.6 0.0 collective-permute-done.11
  81.6 0.0 copy-start.1
  81.6 1.3 %collective-permute-start.14 = (f32[544,128]{1,0:T(8,128)S(1)}, f32[544,128]{1,0:T(8,128)S(1)}, u32[]{:S(2)}, u32[]{:S(2)}) collective-permute-start(f32[544,128]{1,0:T(8,128)S(1)} %constant_dynamic-update-slice_fusion.refs_0_), channel_id=1, source_target_pairs={{0,6},{2,4},{4,2},{6,0},{8,14},{10,12},{12,10},{14,8},{16,22},{18,... | collective-permute-start | bytes 835592 | tf_op jit(solution)/shard_map/ppermute | solution.py:605
  83.0 1.7 %collective-permute-start.13 = (f32[544,128]{1,0:T(8,128)S(1)}, f32[544,128]{1,0:T(8,128)S(1)}, u32[]{:S(2)}, u32[]{:S(2)}) collective-permute-start(f32[544,128]{1,0:T(8,128)S(1)} %constant_dynamic-update-slice_fusion.refs_0_), channel_id=1, source_target_pairs={{0,4},{2,6},{4,0},{6,2},{8,12},{10,14},{12,8},{14,10},{16,20},{18,... | collective-permute-start | bytes 835592 | tf_op jit(solution)/shard_map/ppermute | solution.py:605
  84.7 0.5 collective-permute-start.12
  85.9 6.3 %collective-permute-done.14.refs_3_ = f32[544,128]{1,0:T(8,128)S(1)} collective-permute-done((f32[544,128]{1,0:T(8,128)S(1)}, f32[544,128]{1,0:T(8,128)S(1)}, u32[]{:S(2)}, u32[]{:S(2)}) %collective-permute-start.14) | collective-permute-done | bytes 278560 | tf_op jit(solution)/shard_map/ppermute | solution.py:605
  92.2 4.7 %collective-permute-done.13.refs_2_ = f32[544,128]{1,0:T(8,128)S(1)} collective-permute-done((f32[544,128]{1,0:T(8,128)S(1)}, f32[544,128]{1,0:T(8,128)S(1)}, u32[]{:S(2)}, u32[]{:S(2)}) %collective-permute-start.13) | collective-permute-done | bytes 278560 | tf_op jit(solution)/shard_map/ppermute | solution.py:605
  96.9 0.1 collective-permute-done.12.refs_1_
  97.0 0.0 copy-done.1
  97.0 0.0 copy-done.2
  97.0 0.6 copy-done.3
  97.7 0.1 copy-done.4
  97.8 8.8 %update.1 = (f32[377,128]{1,0:T(8,128)}, f32[377,128]{1,0:T(8,128)}, f32[377,128]{1,0:T(8,128)}, f32[128,256]{1,0:T(8,128)}, f32[128,256]{1,0:T(8,128)}, /*index...) custom-call(f32[544,128]{1,0:T(8,128)} %copy-done.1, ...), custom_call_target="tpu_custom_call" | custom-call | tf_op jit(solution)/shard_map/update/pallas_call | solution.py:652
  (10 shorter events, 0.0 us)
Async XLA Ops:
  3.6 2.9 %collective-permute-start = (bf16[3904,128]{1,0:T(8,128)(2,1)}, bf16[3904,128]{1,0:T(8,128)(2,1)S(1)}, u32[]{:S(2)}, u32[]{:S(2)}) collective-permute-start(bf16[3904,128]{1,0:T(8,128)(2,1)} %pack.1.pack_own), channel_id=1, source_target_pairs={{0,1},{1,0},{2,3},{3,2},{4,5},{5,4},{6,7},{7,6},{8,9},{9,8},{10,11... | collective-permute-start | bytes 2998280 | tf_op jit(solution)/shard_map/ppermute | solution.py:602
  6.5 1.0 copy-start
  35.6 2.9 %collective-permute-start.1 = (f32[2048,128]{1,0:T(8,128)}, f32[2048,128]{1,0:T(8,128)S(1)}, u32[]{:S(2)}, u32[]{:S(2)}) collective-permute-start(f32[2048,128]{1,0:T(8,128)} %get-tuple-element.54), channel_id=1, source_target_pairs={{0,1},{1,0},{2,3},{3,2},{4,5},{5,4},{6,7},{7,6},{8,9},{9,8},{10,11... | collective-permute-start | bytes 3145736 | tf_op jit(solution)/shard_map/ppermute | solution.py:602
  39.8 11.1 %collective-permute-start.4 = (f32[512,128]{1,0:T(8,128)S(1)}, f32[512,128]{1,0:T(8,128)S(1)}, u32[]{:S(2)}, u32[]{:S(2)}) collective-permute-start(f32[512,128]{1,0:T(8,128)S(1)} %get-tuple-element.90), channel_id=1, source_target_pairs={{0,6},{2,4},{4,2},{6,0},{8,14},{10,12},{12,10},{14,8},{16,22},{18,... | collective-permute-start | bytes 786440 | tf_op jit(solution)/shard_map/ppermute | solution.py:605
  43.7 12.2 %collective-permute-start.3 = (f32[512,128]{1,0:T(8,128)S(1)}, f32[512,128]{1,0:T(8,128)S(1)}, u32[]{:S(2)}, u32[]{:S(2)}) collective-permute-start(f32[512,128]{1,0:T(8,128)S(1)} %get-tuple-element.91), channel_id=1, source_target_pairs={{0,4},{2,6},{4,0},{6,2},{8,12},{10,14},{12,8},{14,10},{16,20},{18,... | collective-permute-start | bytes 786440 | tf_op jit(solution)/shard_map/ppermute | solution.py:605
  44.2 12.0 %collective-permute-start.2 = (f32[512,128]{1,0:T(8,128)S(1)}, f32[512,128]{1,0:T(8,128)S(1)}, u32[]{:S(2)}, u32[]{:S(2)}) collective-permute-start(f32[512,128]{1,0:T(8,128)S(1)} %get-tuple-element.92), channel_id=1, source_target_pairs={{0,2},{2,0},{4,6},{6,4},{8,10},{10,8},{12,14},{14,12},{16,18},{18,... | collective-permute-start | bytes 786440 | tf_op jit(solution)/shard_map/ppermute | solution.py:605
  56.9 6.4 %collective-permute-start.7 = (f32[128,128]{1,0:T(8,128)S(1)}, f32[128,128]{1,0:T(8,128)S(1)}, u32[]{:S(2)}, u32[]{:S(2)}) collective-permute-start(f32[128,128]{1,0:T(8,128)S(1)} %get-tuple-element.85), channel_id=1, source_target_pairs={{0,24},{2,26},{4,28},{6,30},{8,16},{10,18},{12,20},{14,22},{16,8},... | collective-permute-start | bytes 196616 | tf_op jit(solution)/shard_map/ppermute | solution.py:605
  60.5 5.7 %collective-permute-start.6 = (f32[128,128]{1,0:T(8,128)S(1)}, f32[128,128]{1,0:T(8,128)S(1)}, u32[]{:S(2)}, u32[]{:S(2)}) collective-permute-start(f32[128,128]{1,0:T(8,128)S(1)} %get-tuple-element.86), channel_id=1, source_target_pairs={{0,16},{2,18},{4,20},{6,22},{8,24},{10,26},{12,28},{14,30},{16,0},... | collective-permute-start | bytes 196616 | tf_op jit(solution)/shard_map/ppermute | solution.py:605
  60.5 5.7 %collective-permute-start.5 = (f32[128,128]{1,0:T(8,128)S(1)}, f32[128,128]{1,0:T(8,128)S(1)}, u32[]{:S(2)}, u32[]{:S(2)}) collective-permute-start(f32[128,128]{1,0:T(8,128)S(1)} %get-tuple-element.87), channel_id=1, source_target_pairs={{0,8},{2,10},{4,12},{6,14},{8,0},{10,2},{12,4},{14,6},{16,24},{18,... | collective-permute-start | bytes 196616 | tf_op jit(solution)/shard_map/ppermute | solution.py:605
  63.3 2.9 %copy-start.5 = (f32[128,128]{1,0:T(8,128)}, f32[128,128]{1,0:T(8,128)S(1)}, u32[]{:S(2)}) copy-start(f32[128,128]{1,0:T(8,128)S(1)} %collective-permute-done.7.refs_3_) | copy-start | bytes 196612
  66.2 0.6 copy-start.6
  66.2 0.6 copy-start.7
  68.4 1.4 %collective-permute-start.8 = (f32[8,128]{1,0:T(8,128)}, f32[8,128]{1,0:T(8,128)S(1)}, u32[]{:S(2)}, u32[]{:S(2)}) collective-permute-start(f32[8,128]{1,0:T(8,128)} %get-tuple-element.59), channel_id=1, source_target_pairs={{0,1},{1,0},{2,3},{3,2},{4,5},{5,4},{6,7},{7,6},{8,9},{9,8},{10,11... | collective-permute-start | bytes 12296 | tf_op jit(solution)/shard_map/ppermute | solution.py:602
  71.4 4.3 %collective-permute-start.9 = (f32[136,128]{1,0:T(8,128)S(1)}, f32[136,128]{1,0:T(8,128)S(1)}, u32[]{:S(2)}, u32[]{:S(2)}) collective-permute-start(f32[136,128]{1,0:T(8,128)S(1)} %pad_maximum_fusion), channel_id=1, source_target_pairs={{0,8},{2,10},{4,12},{6,14},{8,0},{10,2},{12,4},{14,6},{16,24},{18,... | collective-permute-start | bytes 208904 | tf_op jit(solution)/shard_map/ppermute | solution.py:605
  72.4 9.2 %collective-permute-start.11 = (f32[136,128]{1,0:T(8,128)S(1)}, f32[136,128]{1,0:T(8,128)S(1)}, u32[]{:S(2)}, u32[]{:S(2)}) collective-permute-start(f32[136,128]{1,0:T(8,128)S(1)} %pad_maximum_fusion), channel_id=1, source_target_pairs={{0,24},{2,26},{4,28},{6,30},{8,16},{10,18},{12,20},{14,22},{16,8},... | collective-permute-start | bytes 208904 | tf_op jit(solution)/shard_map/ppermute | solution.py:605
  74.3 7.3 %collective-permute-start.10 = (f32[136,128]{1,0:T(8,128)S(1)}, f32[136,128]{1,0:T(8,128)S(1)}, u32[]{:S(2)}, u32[]{:S(2)}) collective-permute-start(f32[136,128]{1,0:T(8,128)S(1)} %pad_maximum_fusion), channel_id=1, source_target_pairs={{0,16},{2,18},{4,20},{6,22},{8,24},{10,26},{12,28},{14,30},{16,0},... | collective-permute-start | bytes 208904 | tf_op jit(solution)/shard_map/ppermute | solution.py:605
  81.6 15.4 %copy-start.1 = (f32[544,128]{1,0:T(8,128)}, f32[544,128]{1,0:T(8,128)S(1)}, u32[]{:S(2)}) copy-start(f32[544,128]{1,0:T(8,128)S(1)} %constant_dynamic-update-slice_fusion.refs_0_) | copy-start | bytes 835588
  81.6 10.5 %collective-permute-start.14 = (f32[544,128]{1,0:T(8,128)S(1)}, f32[544,128]{1,0:T(8,128)S(1)}, u32[]{:S(2)}, u32[]{:S(2)}) collective-permute-start(f32[544,128]{1,0:T(8,128)S(1)} %constant_dynamic-update-slice_fusion.refs_0_), channel_id=1, source_target_pairs={{0,6},{2,4},{4,2},{6,0},{8,14},{10,12},{12,10},{14,8},{16,22},{18,... | collective-permute-start | bytes 835592 | tf_op jit(solution)/shard_map/ppermute | solution.py:605
  83.0 14.0 %collective-permute-start.13 = (f32[544,128]{1,0:T(8,128)S(1)}, f32[544,128]{1,0:T(8,128)S(1)}, u32[]{:S(2)}, u32[]{:S(2)}) collective-permute-start(f32[544,128]{1,0:T(8,128)S(1)} %constant_dynamic-update-slice_fusion.refs_0_), channel_id=1, source_target_pairs={{0,4},{2,6},{4,0},{6,2},{8,12},{10,14},{12,8},{14,10},{16,20},{18,... | collective-permute-start | bytes 835592 | tf_op jit(solution)/shard_map/ppermute | solution.py:605
  84.7 12.4 %collective-permute-start.12 = (f32[544,128]{1,0:T(8,128)S(1)}, f32[544,128]{1,0:T(8,128)S(1)}, u32[]{:S(2)}, u32[]{:S(2)}) collective-permute-start(f32[544,128]{1,0:T(8,128)S(1)} %constant_dynamic-update-slice_fusion.refs_0_), channel_id=1, source_target_pairs={{0,2},{2,0},{4,6},{6,4},{8,10},{10,8},{12,14},{14,12},{16,18},{18,... | collective-permute-start | bytes 835592 | tf_op jit(solution)/shard_map/ppermute | solution.py:605
  92.2 4.8 %copy-start.2 = (f32[544,128]{1,0:T(8,128)}, f32[544,128]{1,0:T(8,128)S(1)}, u32[]{:S(2)}) copy-start(f32[544,128]{1,0:T(8,128)S(1)} %collective-permute-done.14.refs_3_) | copy-start | bytes 835588
  96.9 0.7 copy-start.3
  97.0 0.7 copy-start.4

commit v2 on v1

v2 whole, which is shorter than its diff:
```python
import functools
import math

import jax
import jax.numpy as jnp
from jax import lax
from jax.experimental import pallas as pl
from jax.experimental.pallas import tpu as pltpu
from jax.sharding import PartitionSpec as P

OBS = 376
ACT = 17
H = 256
GAMMA = 0.99
RHO = 0.005
TAU_STAT = 0.1
CLIP = 0.005
RATE = 0.05
BETA_ONE = 0.9
BETA_TWO = 0.999
ADAM_EPS = 1e-08
DECAY = 0.01
HALF_LOG_TAU = 0.5 * math.log(2.0 * math.pi)
LOG_TWO = math.log(2.0)
GELU_A = math.sqrt(2.0 / math.pi)
GELU_B = GELU_A * 0.044715
F32 = jnp.float32
B16 = jnp.bfloat16

A_IN = OBS + 1
C_IN = OBS + ACT + 1
BIAS_ROW = OBS + ACT
K_PAD = 512
K_USE = 400
HALF = H // 2
VMEM = pltpu.VMEM
STEP_VMEM = 50 * 1024 * 1024
UPDATE_VMEM = 24 * 1024 * 1024
SMALL_VMEM = 8 * 1024 * 1024

PACK_W2 = 5 * 4 * HALF
PACK_ACT = PACK_W2 + 5 * 2 * HALF
PACK_ROWS = PACK_ACT + 2 * 32

FLAT_CW1 = 0
FLAT_AW1 = 792
FLAT_AW2 = FLAT_AW1 + 384
FLAT_CW2 = FLAT_AW2 + H
FLAT_SMALL = FLAT_CW2 + 2 * H
FLAT_AHEAD = FLAT_SMALL
FLAT_CHEAD = FLAT_AHEAD + 80
FLAT_B2 = FLAT_CHEAD + 8
FLAT_SUMS = FLAT_B2 + 8
FLAT_ROWS = FLAT_SUMS + 8
LANE_C = 48
LANE_LOSS = 64
LANE_SIGMA = 72
LANE_NEXT = 80
LANE_COUNT = 88


def dot_nn(a, b):
    return lax.dot_general(a, b, (((1,), (0,)), ((), ())), preferred_element_type=F32)


def dot_nt(a, b):
    return lax.dot_general(a, b, (((1,), (1,)), ((), ())), preferred_element_type=F32)


def gelu_only(y):
    t = jnp.tanh(y * (2.0 * GELU_A + (8.0 * GELU_B) * (y * y)))
    return y * (1.0 + t)


def gelu_both(y):
    w = y * y
    t = jnp.tanh(y * (2.0 * GELU_A + (8.0 * GELU_B) * w))
    e = 1.0 + t
    value = y * e
    return value, e + (value * (1.0 - t)) * (2.0 * GELU_A + (24.0 * GELU_B) * w)


def own_chunk(orders):
    d_index = lax.axis_index("dp")
    found = []
    for order in orders:
        number = jnp.int32(0)
        for place, bit in enumerate(order):
            number = number | (((d_index >> bit) & 1) << place)
        found.append(number)
    return jnp.where(lax.axis_index("tensor") == 0, found[0], found[1])


def pack_kernel(a_w1, c_w1, t_w1, a_w2, c_w2, t_w2, out, wide):
    for net in range(5):
        wide[...] = jnp.zeros_like(wide)
        if net == 0:
            wide[0:OBS, :] = a_w1[0:OBS, :]
            wide[BIAS_ROW : BIAS_ROW + 1, :] = a_w1[OBS:A_IN, :]
        else:
            source = c_w1 if net < 3 else t_w1
            wide[0:C_IN, :] = source.reshape(2 * C_IN, 128)[pl.ds((net - 1) % 2, C_IN, stride=2), :]
        for tile in range(4):
            base = (net * 4 + tile) * HALF
            out[base : base + HALF, :] = jnp.transpose(0.5 * wide[tile * 128 : tile * 128 + 128, :]).astype(B16)
        if net in (1, 2):
            base = PACK_ACT + (net - 1) * 32
            rows = lax.broadcasted_iota(jnp.int32, (32, 128), 0)
            out[base : base + 32, :] = jnp.where(rows < ACT, wide[OBS : OBS + 32, :], 0.0).astype(B16)
        for part in range(2):
            base = PACK_W2 + (net * 2 + part) * HALF
            lanes = slice(part * 128, part * 128 + 128)
            if net == 0:
                block = a_w2[:, lanes]
            else:
                block = (c_w2 if net < 3 else t_w2)[(net - 1) % 2, :, lanes]
            out[base : base + HALF, :] = (0.5 * block).astype(B16)


def in_hbm(*values):
    return [pltpu.with_memory_space_constraint(value, pltpu.HBM) for value in values]


def pack_weights(a_w1, c_w1, t_w1, a_w2, c_w2, t_w2):
    return pl.pallas_call(
        pack_kernel,
        out_shape=jax.ShapeDtypeStruct((PACK_ROWS, 128), B16),
        scratch_shapes=[VMEM((K_PAD, 128), F32)],
        compiler_params=pltpu.CompilerParams(vmem_limit_bytes=SMALL_VMEM),
        name="pack",
    )(*in_hbm(a_w1, c_w1, t_w1, a_w2, c_w2, t_w2))


def step_kernel(
    rows_tile,
    subs,
    offset,
    order,
    orders,
    n_own,
    count_ref,
    state_ref,
    obs_ref,
    next_ref,
    action_ref,
    noise_ref,
    next_noise_ref,
    reward_ref,
    terminal_ref,
    pack_own,
    pack_par,
    a_head_ref,
    c_head_ref,
    t_head_ref,
    bias2_ref,
    t_bias2_ref,
    *rest,
):
    own_outs = rest[:n_own]
    par_out = rest[n_own]
    (
        w1t, w2, w2t, w1a, wht_a, wh_a, wht_c, wh_c, hb, b2b, wqb,
        xn_all, xd_all, xq_all,
        z1_all, z1q_all, z2_all, z2q_all, zn_all, zt_all,
        h1n_all, h2n_all, h1_all, h2_all, h1q_all, h2q_all, h1t_all, h2t_all,
        g1_all, g1q_all, g2_all, dz1_all, dz2_all, dzq1_all, dzq2_all,
        acc1, acc2, acc_ha, acc_hc, acc_b, acc_s, flat,
    ) = rest[n_own + 1 :]
    step = pl.program_id(0)
    n_steps = pl.num_programs(0)
    t_index = lax.axis_index("tensor")
    rt = rows_tile
    lane_tiles = rt // 128

    @pl.when(step == 0)
    def _():
        for net in range(5):
            for side, pack in enumerate((pack_own, pack_par)):
                rows = slice(net * H + side * HALF, net * H + side * HALF + HALF)
                for tile in range(4):
                    base = (net * 4 + tile) * HALF
                    w1t[rows, tile * 128 : tile * 128 + 128] = pack[base : base + HALF, :]
                for part in range(2):
                    base = PACK_W2 + (net * 2 + part) * HALF
                    w2[rows, part * 128 : part * 128 + 128] = pack[base : base + HALF, :]
        for side, pack in enumerate((pack_own, pack_par)):
            w1a[:, side * HALF : side * HALF + HALF] = pack[PACK_ACT:PACK_ROWS, :]
        for net in range(5):
            w2t[net * H : net * H + H, :] = jnp.transpose(w2[net * H : net * H + H, :])
        wht_a[...] = jnp.zeros_like(wht_a)
        hb[...] = jnp.zeros_like(hb)
        for part in range(2):
            rows = a_head_ref[part * ACT : part * ACT + ACT, :].astype(B16)
            wht_a[part * 24 : part * 24 + ACT, :] = rows[:, 0:H].astype(F32)
            hb[part * 24 : part * 24 + ACT, :] = jnp.broadcast_to(rows[:, H : H + 1].astype(F32), (ACT, 128))
        wh_a[...] = jnp.transpose(0.5 * wht_a[...]).astype(B16)
        wht_c[...] = jnp.zeros_like(wht_c)
        for net in range(4):
            head = (c_head_ref if net < 2 else t_head_ref)[net % 2].astype(B16).astype(F32)
            wht_c[net * 8 : net * 8 + 2, :] = head[:, 0:H]
            hb[48 + net * 8 : 48 + net * 8 + 2, :] = jnp.broadcast_to(head[:, H : H + 1], (2, 128))
        wh_c[...] = jnp.transpose(0.5 * wht_c[...]).astype(B16)
        for net in range(2):
            row = 0.5 * wht_c[net * 8 : net * 8 + 1, :]
            wqb[net * H : net * H + H, :] = jnp.transpose(jnp.broadcast_to(row, (128, H)))
        for net in range(5):
            bias = bias2_ref[net : net + 1, :] if net < 3 else t_bias2_ref[net - 3 : net - 2, :]
            b2b[net * H : net * H + H, :] = jnp.transpose(jnp.broadcast_to(0.5 * bias, (128, H)))
        tail = lax.broadcasted_iota(jnp.int32, (K_PAD - OBS, rt), 0)
        ones = jnp.where(tail == ACT, 1.0, 0.0).astype(B16)
        for sub in range(subs):
            xn_all[sub, OBS:K_PAD, :] = ones
            xd_all[sub, OBS:K_PAD, :] = ones
            xq_all[sub, OBS:K_PAD, :] = ones
        acc1[...] = jnp.zeros_like(acc1)
        acc2[...] = jnp.zeros_like(acc2)
        acc_ha[...] = jnp.zeros_like(acc_ha)
        acc_hc[...] = jnp.zeros_like(acc_hc)
        acc_b[...] = jnp.zeros_like(acc_b)
        acc_s[...] = jnp.zeros_like(acc_s)

    def lanes_of(column):
        return jnp.concatenate([column] * lane_tiles, axis=1)

    def lane_sum(value):
        total = value[:, 0:128]
        for tile in range(1, lane_tiles):
            total = total + value[:, tile * 128 : tile * 128 + 128]
        return total

    def biased(source, r, bias_base):
        y = source[r : r + 16, :]
        if bias_base is not None:
            y = y + lanes_of(b2b[bias_base + r : bias_base + r + 16, :])
        return y

    def forward(source, target, rows, bias_base=None):
        for r in range(0, rows, 16):
            target[r : r + 16, :] = gelu_only(biased(source, r, bias_base)).astype(B16)

    def forward_slope(source, target, slope, rows, bias_base=None):
        for r in range(0, rows, 16):
            value, grad = gelu_both(biased(source, r, bias_base))
            target[r : r + 16, :] = value.astype(B16)
            slope[r : r + 16, :] = grad

    def policy(hidden, noise):
        out = dot_nn(wht_a[...].astype(B16), hidden) + lanes_of(hb[0:48, :])
        eps = jnp.concatenate([noise, jnp.zeros((24 - ACT, rt), F32)], axis=0)
        tl = jnp.tanh(out[24:48])
        ls = tl - 1.0
        spread = jnp.exp(ls) * eps
        u = out[0:24] + spread
        act = jnp.tanh(u)
        soft = jnp.maximum(-2.0 * u, 0.0) + jnp.log(1.0 + jnp.exp(-jnp.abs(2.0 * u)))
        terms = -0.5 * eps * eps - ls - HALF_LOG_TAU - 2.0 * (LOG_TWO - u - soft)
        keep = lax.broadcasted_iota(jnp.int32, (24, rt), 0) < ACT
        logp = jnp.sum(jnp.where(keep, terms, 0.0), axis=0, keepdims=True)
        return act, logp, tl, spread

    def head(net, hidden):
        rows = slice(net * 8, net * 8 + 8)
        return dot_nn(wht_c[rows, :].astype(B16), hidden) + lanes_of(hb[48 + net * 8 : 56 + net * 8, :])

    def back_second(source, slope, target, first, last):
        for r in range(first, last, 16):
            d_pre = source[r : r + 16, :] * slope[r : r + 16, :]
            target[r : r + 16, :] = d_pre.astype(B16)
            acc_b[r : r + 16, :] += lane_sum(d_pre)

    def back_first(source, slope, target, first, last):
        for r in range(first, last, 16):
            target[r : r + 16, :] = (source[r : r + 16, :] * slope[r : r + 16, :]).astype(B16)

    def stages(sub):
        cols = slice(sub * rt, sub * rt + rt)
        xn, xd, xq = xn_all.at[sub], xd_all.at[sub], xq_all.at[sub]
        z1, z1q, z2, z2q, zn, zt = (r.at[sub] for r in (z1_all, z1q_all, z2_all, z2q_all, zn_all, zt_all))
        h1n, h2n, h1, h2 = (r.at[sub] for r in (h1n_all, h2n_all, h1_all, h2_all))
        h1q, h2q, h1t, h2t = (r.at[sub] for r in (h1q_all, h2q_all, h1t_all, h2t_all))
        g1, g1q, g2 = (r.at[sub] for r in (g1_all, g1q_all, g2_all))
        dz1, dz2, dzq1, dzq2 = (r.at[sub] for r in (dz1_all, dz2_all, dzq1_all, dzq2_all))

        xn[0:OBS, :] = next_ref[:, cols]
        xd[0:OBS, :] = obs_ref[:, cols]
        xq[0:OBS, :] = obs_ref[:, cols]
        xd[OBS : OBS + ACT, :] = action_ref[:, cols]
        zn[...] = dot_nn(w1t[0:H, :], xn[...])
        z1[...] = dot_nn(w1t[0 : 3 * H, :], xd[...])
        yield
        forward(zn, h1n, H)
        forward_slope(z1, h1, g1, 3 * H)
        yield
        zn[...] = dot_nn(w2t[0:H, :], h1n[...])
        for net in range(3):
            rows = slice(net * H, net * H + H)
            z2[rows, :] = dot_nn(w2t[rows, :], h1[rows, :])
        forward(zn, h2n, H, 0)
        forward_slope(z2, h2, g2, 3 * H, 0)
        yield
        index = t_index * (n_steps * subs * rt) + (step * subs + sub) * rt
        index = index + lax.broadcasted_iota(jnp.int32, (1, rt), 1)
        valid = (index < count_ref[0]).astype(F32)
        alpha = jnp.exp(jnp.full((1, rt), state_ref[0], F32))
        omega = state_ref[3] * state_ref[3]
        act_next, logp_next, _, _ = policy(h2n[...], next_noise_ref[:, cols])
        act_new, logp_new, tl_new, spread_new = policy(h2[0:H, :], noise_ref[:, cols])
        xn[OBS : OBS + ACT, :] = act_next[0:ACT].astype(B16)
        xq[OBS : OBS + ACT, :] = act_new[0:ACT].astype(B16)
        zt[...] = dot_nn(w1t[3 * H : 5 * H, :], xn[...])
        z1q[...] = dot_nn(w1t[H : 3 * H, :], xq[...])
        yield
        forward(zt, h1t, 2 * H)
        forward_slope(z1q, h1q, g1q, 2 * H)
        yield
        for net in range(2):
            rows = slice(net * H, net * H + H)
            zt[rows, :] = dot_nn(w2t[(3 + net) * H : (4 + net) * H, :], h1t[rows, :])
            z2q[rows, :] = dot_nn(w2t[(1 + net) * H : (2 + net) * H, :], h1q[rows, :])
        forward(zt, h2t, 2 * H, 3 * H)
        for r in range(0, 2 * H, 16):
            value, grad = gelu_both(biased(z2q, r, H))
            h2q[r : r + 16, :] = value.astype(B16)
            dzq2[r : r + 16, :] = (lanes_of(wqb[r : r + 16, :]) * grad).astype(B16)
        yield
        out_t = [head(2 + net, h2t[net * H : net * H + H, :])[0:1] for net in range(2)]
        out_d = [head(net, h2[(1 + net) * H : (2 + net) * H, :]) for net in range(2)]
        out_q = [head(net, h2q[net * H : net * H + H, :])[0:1] for net in range(2)]
        for net in range(2):
            rows = slice(net * H, net * H + H)
            z1q[rows, :] = dot_nn(w2[(1 + net) * H : (2 + net) * H, :], dzq2[rows, :])
        alive = 1.0 - terminal_ref[:, cols].astype(F32)
        target = reward_ref[:, cols] + GAMMA * alive * (jnp.minimum(out_t[0], out_t[1]) - alpha * logp_next)
        loss_row = valid * (alpha * logp_new - 0.5 * (out_q[0] + out_q[1]))
        sigma_row = jnp.zeros((1, rt), F32)
        next_row = valid * (logp_next - ACT)
        d_heads = []
        for net in range(2):
            log_sigma = jnp.tanh(out_d[net][1:2])
            sigma = jnp.exp(log_sigma)
            error = target - out_d[net][0:1]
            inverse = 1.0 / (sigma * sigma)
            scaled = error * inverse
            square = error * scaled
            loss_row = loss_row + valid * (omega * (0.5 * square + log_sigma))
            sigma_row = sigma_row + valid * sigma
            d_q = -(omega * valid) * scaled
            d_s = (omega * valid) * (1.0 - square) * (1.0 - log_sigma * log_sigma)
            d_heads.append(jnp.concatenate([d_q, d_s, jnp.zeros((6, rt), F32)], axis=0).astype(B16))
        acc_s[64:65, :] += lane_sum(loss_row)
        acc_s[72:73, :] += lane_sum(sigma_row)
        acc_s[80:81, :] += lane_sum(next_row)
        yield
        for net in range(2):
            rows = slice((1 + net) * H, (2 + net) * H)
            acc_s[48 + net * 8 : 56 + net * 8, :] += lane_sum(d_heads[net].astype(F32))
            acc_hc[net * 8 : net * 8 + 8, :] += dot_nt(d_heads[net], h2[rows, :])
            z2[rows, :] = dot_nn(wh_c[:, net * 8 : net * 8 + 8], d_heads[net])
        back_first(z1q, g1q, dzq1, 0, 2 * H)
        d_act = dot_nn(w1a[0:32, :], dzq1[0:H, :]) + dot_nn(w1a[32:64, :], dzq1[H : 2 * H, :])
        back_second(z2, g2, dz2, H, 3 * H)
        yield
        d_act = d_act[0:24] * (-0.5 * valid)
        d_logp = alpha * valid
        d_u = d_act * (1.0 - act_new * act_new) + (2.0 * d_logp) * act_new
        d_ls = (d_u * spread_new - d_logp) * (1.0 - tl_new * tl_new)
        d_out = jnp.concatenate([d_u, d_ls], axis=0).astype(B16)
        acc_s[0:48, :] += lane_sum(d_out.astype(F32))
        acc_ha[...] += dot_nt(d_out, h2[0:H, :])
        z2[0:H, :] = dot_nn(wh_a[...], d_out)
        for net in range(1, 3):
            rows = slice(net * H, net * H + H)
            z1[rows, :] = dot_nn(w2[rows, :], dz2[rows, :])
        back_second(z2, g2, dz2, 0, H)
        z1[0:H, :] = dot_nn(w2[0:H, :], dz2[0:H, :])
        back_first(z1, g1, dz1, H, 3 * H)
        yield
        back_first(z1, g1, dz1, 0, H)
        for net in (1, 2, 0):
            rows = slice(net * H, net * H + H)
            acc2[rows, :] += dot_nt(h1[rows, :], dz2[rows, :])
        acc1[...] += dot_nt(xd[0:K_USE, :], dz1[...])

    running = [stages(sub) for sub in range(subs)]
    alive_count = subs
    turn = 0
    done = [False] * subs
    while alive_count:
        for sub in range(subs):
            if not done[sub] and turn >= sub * offset:
                if next(running[sub], "end") == "end":
                    done[sub] = True
                    alive_count -= 1
        turn += 1

    @pl.when(step == n_steps - 1)
    def _():
        mine, others = own_chunk(orders), own_chunk(orders[::-1])
        flat[:, FLAT_SMALL:FLAT_ROWS, :] = jnp.zeros((2, FLAT_ROWS - FLAT_SMALL, 128), F32)
        flat[:, FLAT_AW1 - 8 : FLAT_AW1, :] = jnp.zeros((2, 8, 128), F32)
        flat[:, FLAT_AW2 - 8 : FLAT_AW2, :] = jnp.zeros((2, 8, 128), F32)
        sums = jnp.sum(jnp.transpose(acc_s[...]), axis=0, keepdims=True)
        lane = lax.broadcasted_iota(jnp.int32, (1, 128), 1)
        keep = (lane < ACT) | ((lane >= 24) & (lane < 24 + ACT)) | ((lane >= 48) & (lane < 50))
        keep = keep | ((lane >= 56) & (lane < 58)) | (lane == LANE_LOSS) | (lane == LANE_SIGMA) | (lane == LANE_NEXT)
        sums = jnp.where(keep, sums, 0.0)
        sums = jnp.where(lane == LANE_COUNT, 0.5 * count_ref[0].astype(F32), sums)
        for side in range(2):
            lanes = slice(side * HALF, side * HALF + HALF)
            for net in range(2):
                columns = slice((1 + net) * H + side * HALF, (1 + net) * H + side * HALF + HALF)
                flat[side, pl.ds(FLAT_CW1 + net, C_IN, stride=2), :] = acc1[0:C_IN, columns]
            flat[side, FLAT_AW1 : FLAT_AW1 + OBS, :] = acc1[0:OBS, lanes]
            flat[side, FLAT_AW1 + OBS : FLAT_AW1 + A_IN, :] = acc1[BIAS_ROW : BIAS_ROW + 1, lanes]
            for net in range(3):
                rows = slice(net * H + side * HALF, net * H + side * HALF + HALF)
                for part in range(2):
                    base = FLAT_AW2 + (net * 2 + part) * HALF
                    flat[side, base : base + HALF, :] = acc2[rows, part * 128 : part * 128 + 128]
            for part in range(2):
                cols = slice(part * 128, part * 128 + 128)
                base = FLAT_AHEAD + part * 40
                flat[side, base : base + ACT, :] = acc_ha[0:ACT, cols]
                flat[side, base + ACT : base + 2 * ACT, :] = acc_ha[24 : 24 + ACT, cols]
                for net in range(2):
                    base = FLAT_CHEAD + part * 4 + net * 2
                    flat[side, base : base + 2, :] = acc_hc[net * 8 : net * 8 + 2, cols]
            for net in range(3):
                for part in range(2):
                    rows = slice(net * H + part * 128, net * H + part * 128 + 128)
                    row = FLAT_B2 + part * 4 + net
                    flat[side, row : row + 1, :] = jnp.sum(jnp.transpose(acc_b[rows, :]), axis=0, keepdims=True)
            flat[side, FLAT_SUMS : FLAT_SUMS + 1, :] = sums
        size = FLAT_ROWS // len(order)
        per = len(order) // n_own
        for place, rel in enumerate(order):
            start = pl.multiple_of(jnp.bitwise_xor(mine, rel) * size, size)
            own_outs[place // per][(place % per) * size : (place % per) * size + size, :] = flat[0, pl.ds(start, size), :]
            start = pl.multiple_of(jnp.bitwise_xor(others, rel) * size, size)
            par_out[place * size : place * size + size, :] = flat[1, pl.ds(start, size), :]


SUB_ROWS = 256
SUBS = 2
SUB_OFFSET = 2


def run_step(groups, arrays, pack_own, pack_par, small, count, state):
    obs, next_obs, action, noise, next_noise, reward, terminal = arrays
    rows = obs.shape[1] // groups["tensor"]
    rt = min(SUB_ROWS, rows)
    subs = min(SUBS, rows // rt)
    steps = rows // (rt * subs)
    order, n_own = groups["order"], groups["first"]

    def tile(height):
        return pl.BlockSpec((height, rt * subs), lambda i: (0, lax.axis_index("tensor") * steps + i))

    def each(height, dtype):
        return VMEM((subs, height, rt), dtype)

    whole = pl.BlockSpec(memory_space=VMEM)
    smem = pl.BlockSpec(memory_space=pltpu.SMEM)
    scratch = [
        VMEM((5 * H, K_PAD), B16), VMEM((5 * H, H), B16), VMEM((5 * H, H), B16), VMEM((64, H), B16),
        VMEM((48, H), F32), VMEM((H, 48), B16), VMEM((32, H), F32), VMEM((H, 32), B16),
        VMEM((80, 128), F32), VMEM((5 * H, 128), F32), VMEM((2 * H, 128), F32),
        each(K_PAD, B16), each(K_PAD, B16), each(K_PAD, B16),
        each(3 * H, F32), each(2 * H, F32), each(3 * H, F32), each(2 * H, F32), each(H, F32), each(2 * H, F32),
        each(H, B16), each(H, B16), each(3 * H, B16), each(3 * H, B16),
        each(2 * H, B16), each(2 * H, B16), each(2 * H, B16), each(2 * H, B16),
        each(3 * H, F32), each(2 * H, F32), each(3 * H, F32),
        each(3 * H, B16), each(3 * H, B16), each(2 * H, B16), each(2 * H, B16),
        VMEM((K_USE, 3 * H), F32), VMEM((3 * H, H), F32), VMEM((48, H), F32), VMEM((16, H), F32),
        VMEM((3 * H, 128), F32), VMEM((128, 128), F32), VMEM((2, FLAT_ROWS, 128), F32),
    ]
    outs = [jax.ShapeDtypeStruct((FLAT_ROWS // n_own, 128), F32)] * n_own + [jax.ShapeDtypeStruct((FLAT_ROWS, 128), F32)]
    return pl.pallas_call(
        functools.partial(step_kernel, rt, subs, SUB_OFFSET, order, groups["orders"], n_own),
        grid=(steps,),
        in_specs=[smem, smem, tile(OBS), tile(OBS), tile(ACT), tile(ACT), tile(ACT), tile(1), tile(1)] + [whole] * 7,
        out_specs=[whole] * (n_own + 1),
        out_shape=outs,
        scratch_shapes=scratch,
        compiler_params=pltpu.CompilerParams(vmem_limit_bytes=STEP_VMEM),
        name="step",
    )(
        count, state, *in_hbm(obs, next_obs, action, noise, next_noise, reward, terminal),
        pack_own, pack_par, *in_hbm(*small),
    )


def last_sum_kernel(size, n_in, orders, *refs):
    out = refs[n_in]
    first = own_chunk(orders) * size
    part = jnp.zeros((8, 128), F32)
    lane = lax.broadcasted_iota(jnp.int32, (8, 128), 1)
    for r in range(0, size, 8):
        total = refs[0][r : r + 8, :]
        for ref in refs[1:n_in]:
            total = total + ref[r : r + 8, :]
        out[r : r + 8, :] = total
        row = first + r + lax.broadcasted_iota(jnp.int32, (8, 128), 0)
        weight = jnp.where(row < FLAT_SMALL, 1.0, 0.5)
        weight = jnp.where((row >= FLAT_SUMS) & (lane >= LANE_LOSS), 0.0, weight)
        part = part + total * total * weight
    out[size : size + 8, :] = part


def last_sum(values, orders):
    size = values[0].shape[0]
    return pl.pallas_call(
        functools.partial(last_sum_kernel, size, len(values), orders),
        out_shape=jax.ShapeDtypeStruct((size + 8, 128), F32),
        compiler_params=pltpu.CompilerParams(vmem_limit_bytes=SMALL_VMEM),
        name="lastsum",
    )(*values)


def one_minus_power(gap, exponent):
    total = jnp.float32(0.0)
    for bit in range(30, -1, -1):
        total = total * (2.0 - total)
        total = jnp.where((exponent >> bit) & 1 == 1, total + gap * (1.0 - total), total)
    return total


def update_kernel(order, orders, n_parts, sizes, *refs):
    parts = refs[:n_parts]
    (
        square_own, square_other, step_ref, state_ref,
        a_w1, a_w1_m, a_w2, a_w2_m, a_head, a_head_m,
        c_w1, c_w1_m, c_w2, c_w2_m, c_head, c_head_m, bias2, bias2_m,
        t_w1, t_w2, t_head, t_bias2,
        o_a_w1, o_a_w1_f, o_a_w1_s, o_a_w2, o_a_w2_f, o_a_w2_s, o_a_head, o_a_head_f, o_a_head_s,
        o_c_w1, o_c_w1_f, o_c_w1_s, o_c_w2, o_c_w2_f, o_c_w2_s, o_c_head, o_c_head_f, o_c_head_s,
        o_bias2, o_bias2_f, o_bias2_s, o_scalars, o_norm,
        flat, rows_new, rows_target,
    ) = refs[n_parts:]
    size, stride = sizes
    mine = own_chunk(orders)
    per = len(order) // n_parts
    square = square_own[...] + square_other[...]
    for place, rel in enumerate(order):
        start = pl.multiple_of(jnp.bitwise_xor(mine, rel) * size, size)
        base = (place % per) * stride
        flat[pl.ds(start, size), :] = parts[place // per][base : base + size, :]
    sums = flat[FLAT_SUMS : FLAT_SUMS + 1, :]
    lane = lax.broadcasted_iota(jnp.int32, (1, 128), 1)

    def pick(index):
        return jnp.sum(jnp.where(lane == index, sums, 0.0), axis=1, keepdims=True)

    loss_sum, sigma_sum, next_sum, count = (pick(i) for i in (LANE_LOSS, LANE_SIGMA, LANE_NEXT, LANE_COUNT))
    inverse = 1.0 / count
    total = jnp.sum(jnp.sum(square, axis=0, keepdims=True), axis=1, keepdims=True)
    norm = jnp.sqrt(total) * inverse
    clip = jnp.minimum(1.0, CLIP / (norm + 1e-06))
    scale = clip * inverse
    t = step_ref[0]
    first_fix = one_minus_power(jnp.float32(0.1), t)
    second_fix = one_minus_power(jnp.float32(0.001), t)
    unfix_one = 1.0 / jnp.full((1, 1), first_fix, F32)
    unfix_two = 1.0 / jnp.full((1, 1), second_fix, F32)

    def adam(weight, first, second, grad, decay=DECAY):
        first = BETA_ONE * first + (1.0 - BETA_ONE) * grad
        second = BETA_TWO * second + (1.0 - BETA_TWO) * (grad * grad)
        step = first * unfix_one / (jnp.sqrt(second * unfix_two) + ADAM_EPS)
        if decay:
            step = step + decay * weight
        return weight - RATE * step, first, second

    def polyak(target, new):
        return (1.0 - RHO) * target + RHO * new

    moments = a_w1_m.reshape(2 * A_IN, 128)
    new, first, second = adam(
        a_w1[...], moments[pl.ds(0, A_IN, stride=2), :], moments[pl.ds(1, A_IN, stride=2), :],
        flat[FLAT_AW1 : FLAT_AW1 + A_IN, :] * scale,
    )
    o_a_w1[...] = new
    o_a_w1_f[...] = first
    o_a_w1_s[...] = second
    for net in range(3):
        for part in range(2):
            lanes = slice(part * 128, part * 128 + 128)
            base = FLAT_AW2 + (net * 2 + part) * HALF
            grad = flat[base : base + HALF, :] * scale
            if net == 0:
                new, first, second = adam(a_w2[:, lanes], a_w2_m[0, :, lanes], a_w2_m[1, :, lanes], grad)
                o_a_w2[:, lanes] = new
                o_a_w2_f[:, lanes] = first
                o_a_w2_s[:, lanes] = second
            else:
                c = net - 1
                new, first, second = adam(c_w2[c, :, lanes], c_w2_m[0, c, :, lanes], c_w2_m[1, c, :, lanes], grad)
                o_c_w2[c, :, lanes] = new
                o_c_w2[2 + c, :, lanes] = polyak(t_w2[c, :, lanes], new)
                o_c_w2_f[c, :, lanes] = first
                o_c_w2_s[c, :, lanes] = second
    both = 2 * C_IN
    new, first, second = adam(
        c_w1.reshape(both, 128)[...], c_w1_m.at[0].reshape(both, 128)[...], c_w1_m.at[1].reshape(both, 128)[...],
        flat[FLAT_CW1 : FLAT_CW1 + both, :] * scale,
    )
    o_c_w1_f.reshape(both, 128)[...] = first
    o_c_w1_s.reshape(both, 128)[...] = second
    rows_new[...] = new
    rows_target[...] = polyak(t_w1.reshape(both, 128)[...], new)
    four = o_c_w1.reshape(2 * both, 128)
    for c in range(2):
        four[pl.ds(c, C_IN, stride=4), :] = rows_new[pl.ds(c, C_IN, stride=2), :]
        four[pl.ds(2 + c, C_IN, stride=4), :] = rows_target[pl.ds(c, C_IN, stride=2), :]
    columns = jnp.transpose(jnp.broadcast_to(sums, (128, 128)))
    bias_a = jnp.concatenate([columns[0:ACT, 0:1], columns[24 : 24 + ACT, 0:1]], axis=0)
    grad = jnp.concatenate(
        [flat[FLAT_AHEAD : FLAT_AHEAD + 2 * ACT, :], flat[FLAT_AHEAD + 40 : FLAT_AHEAD + 40 + 2 * ACT, :], bias_a], axis=1
    )
    new, first, second = adam(a_head[...], a_head_m[:, 0, :], a_head_m[:, 1, :], grad * scale)
    o_a_head[...] = new
    o_a_head_f[...] = first
    o_a_head_s[...] = second
    for c in range(2):
        rows = slice(FLAT_CHEAD + c * 2, FLAT_CHEAD + c * 2 + 2)
        rows_b = slice(FLAT_CHEAD + 4 + c * 2, FLAT_CHEAD + 6 + c * 2)
        bias_c = columns[LANE_C + 8 * c : LANE_C + 8 * c + 2, 0:1]
        grad = jnp.concatenate([flat[rows, :], flat[rows_b, :], bias_c], axis=1) * scale
        new, first, second = adam(c_head[c], c_head_m[0, c], c_head_m[1, c], grad)
        o_c_head[c] = new
        o_c_head[2 + c] = polyak(t_head[c], new)
        o_c_head_f[c] = first
        o_c_head_s[c] = second
    grad = jnp.concatenate([flat[FLAT_B2 : FLAT_B2 + 3, :], flat[FLAT_B2 + 4 : FLAT_B2 + 7, :]], axis=1) * scale
    new, first, second = adam(bias2[...], bias2_m[:, 0, :], bias2_m[:, 1, :], grad)
    o_bias2[0:3, :] = new
    o_bias2[3:5, :] = polyak(t_bias2[...], new[1:3])
    o_bias2_f[...] = first
    o_bias2_s[...] = second
    log_alpha = jnp.full((1, 1), state_ref[0], F32)
    g_alpha = -next_sum
    new, first, second = adam(
        log_alpha, jnp.full((1, 1), state_ref[1], F32), jnp.full((1, 1), state_ref[2], F32), g_alpha * inverse, 0.0
    )
    stat = (1.0 - TAU_STAT) * state_ref[3] + TAU_STAT * sigma_sum / (2.0 * count)
    loss = (loss_sum + log_alpha * g_alpha) * inverse
    for place, value in enumerate((new, first, second, stat, loss)):
        o_scalars[place] = value[0, 0]
    o_norm[0] = norm[0, 0]


def shards(
    groups, obs, action, next_obs, reward, terminal, noise, next_noise, counts, step_count,
    a_w1, a_w2, a_head, c_w1, c_w2, c_head, bias2, tc_w1, tc_w2, tc_head, tc_bias2,
    a_w1_mom, a_w2_mom, a_head_mom, c_w1_mom, c_w2_mom, c_head_mom, bias2_mom, state,
):
    n_dp = groups["dp"]
    swap = [(0, 1), (1, 0)]

    def partner(value):
        return lax.ppermute(value, "tensor", swap)

    def across(value, phase, k):
        masks = [sum(((k >> place) & 1) << bit for place, bit in enumerate(bits)) for bits in phase]
        pairs = [(2 * d + t, 2 * (d ^ masks[t]) + t) for d in range(n_dp) for t in range(2)]
        return lax.ppermute(value, ("dp", "tensor"), pairs)

    tr = jnp.transpose
    c_w1v, tc_w1v = tr(c_w1, (1, 0, 2)), tr(tc_w1, (1, 0, 2))
    a_headv, c_headv, tc_headv = tr(a_head), tr(c_head, (0, 2, 1)), tr(tc_head, (0, 2, 1))
    pack = pack_weights(a_w1, c_w1v, tc_w1v, a_w2, c_w2, tc_w2)
    pack_par = partner(pack)
    arrays = (
        tr(obs), tr(next_obs), tr(action), tr(noise), tr(next_noise), reward.reshape(1, -1), terminal.reshape(1, -1),
    )
    small = (a_headv, c_headv, tc_headv, bias2, tc_bias2)
    outs = run_step(groups, arrays, pack, pack_par, small, counts, state)
    own, par = outs[:-1], outs[-1]
    received = partner(par)
    size = FLAT_ROWS // len(own)
    values = [item + received[i * size : i * size + size] for i, item in enumerate(own)]

    *scatters, last = groups["phases"]
    following = [1 << len(phase[0]) for phase in scatters[1:]] + [1]
    for phase, ways_next in zip(scatters, following):
        got = [values[0]] + [across(values[k], phase, k) for k in range(1, 1 << len(phase[0]))]
        size = got[0].shape[0] // ways_next
        values = [sum(item[j * size : j * size + size] for item in got) for j in range(ways_next)]
    got = [values[0]] + [across(values[0], last, k) for k in range(1, 1 << len(last[0]))]
    block = last_sum(got, groups["orders"])
    for number, phase in reversed(list(enumerate(scatters))):
        got = [block] + [across(block, phase, k) for k in range(1, 1 << len(phase[0]))]
        if number:
            block = jnp.concatenate(got)
    parts = got
    own_square = sum(
        part[r + size : r + size + 8] for part in parts for r in range(0, part.shape[0], size + 8)
    )
    other_square = partner(own_square)

    sds = jax.ShapeDtypeStruct
    shapes = [
        (A_IN, HALF)] * 3 + [(HALF, H)] * 3 + [(2 * ACT, H + 1)] * 3 + [
        (C_IN, 4, HALF), (C_IN, 2, HALF), (C_IN, 2, HALF),
        (4, HALF, H), (2, HALF, H), (2, HALF, H),
        (4, 2, H + 1), (2, 2, H + 1), (2, 2, H + 1),
        (5, H), (3, H), (3, H), (5,), (1,),
    ]
    whole = pl.BlockSpec(memory_space=VMEM)
    smem = pl.BlockSpec(memory_space=pltpu.SMEM)
    res = pl.pallas_call(
        functools.partial(update_kernel, groups["order"], groups["orders"], len(parts), (size, size + 8)),
        in_specs=[whole] * (len(parts) + 2) + [smem, smem] + [whole] * 18,
        out_specs=[whole] * 21 + [smem, smem],
        out_shape=[sds(s, F32) for s in shapes],
        scratch_shapes=[VMEM((FLAT_ROWS, 128), F32), VMEM((2 * C_IN, 128), F32), VMEM((2 * C_IN, 128), F32)],
        compiler_params=pltpu.CompilerParams(vmem_limit_bytes=UPDATE_VMEM),
        name="update",
    )(
        *parts, own_square, other_square, step_count, state,
        a_w1, tr(a_w1_mom, (1, 0, 2)), a_w2, a_w2_mom, a_headv, tr(a_head_mom, (2, 0, 1)),
        c_w1v, tr(c_w1_mom, (0, 2, 1, 3)), c_w2, c_w2_mom, c_headv, tr(c_head_mom, (0, 1, 3, 2)),
        bias2, tr(bias2_mom, (1, 0, 2)), tc_w1v, tc_w2, tc_headv, tc_bias2,
    )
    res = list(res)
    for place in (6, 7, 8):
        res[place] = tr(res[place])
    for place in (9, 10, 11):
        res[place] = tr(res[place], (1, 0, 2))
    for place in (15, 16, 17):
        res[place] = tr(res[place], (0, 2, 1))
    return tuple(res)


def plan(mesh):
    n_dp = mesh.shape["dp"]
    bits = n_dp.bit_length() - 1
    assert n_dp == 1 << bits and mesh.shape["tensor"] == 2
    groups = [tuple(range(low, min(low + 2, bits))) for low in range(0, bits, 2)]
    assert len(groups) > 1
    pairs = [group for group in groups if len(group) == 2]
    turned = pairs[1:] + pairs[:1] + groups[len(pairs) :]
    phases = list(zip(groups, turned))
    order = [0]
    low = 0
    for group in groups[:-1]:
        order = [rel | (k << low) for rel in order for k in range(1 << len(group))]
        low += len(group)
    return {
        "dp": n_dp,
        "tensor": mesh.shape["tensor"],
        "phases": phases,
        "order": tuple(order),
        "orders": tuple(tuple(bit for group in core[:-1] for bit in group) for core in (groups, turned)),
        "first": 1 << len(groups[0]),
    }


def solution(mesh):
    in_specs = (
        P("dp", None), P("dp", None), P("dp", None), P("dp"), P("dp"), P("dp", None), P("dp", None), P("dp"), P(),
        P(None, "tensor"), P("tensor", None), P(), P(None, None, "tensor"), P(None, "tensor", None), P(), P(),
        P(None, None, "tensor"), P(None, "tensor", None), P(), P(),
        P(None, None, "tensor"), P(None, "tensor", None), P(), P(None, None, None, "tensor"),
        P(None, None, "tensor", None), P(), P(), P(),
    )
    out_specs = (
        P(None, "tensor"), P(None, "tensor"), P(None, "tensor"),
        P("tensor", None), P("tensor", None), P("tensor", None),
        P(), P(), P(),
        P(None, None, "tensor"), P(None, None, "tensor"), P(None, None, "tensor"),
        P(None, "tensor", None), P(None, "tensor", None), P(None, "tensor", None),
        P(), P(), P(), P(), P(), P(), P(), P(),
    )
    return jax.shard_map(
        functools.partial(shards, plan(mesh)), mesh=mesh, in_specs=in_specs, out_specs=out_specs, check_vma=False
    )
```

time: 107 us -> 79 us (0.74)
  Pallas kernels: 41.4 us -> 29.9 us
  waiting for transfers between devices: 39.5 us -> 31.3 us
  other arithmetic: 3.53 us -> 0.21 us
  starting transfers between devices: 16.9 us -> 14.4 us
  local copies, waits for them, and re-layouts: 3.21 us -> 0.77 us
    pallas_call x3, Pallas kernels: 38.5 us -> 28.3 us  [the longest x1 24.3 us: run_step(): pl.pallas_call(functools.partial(step_kernel, rt, subs, SUB_OFFSET, order...]
    ppermute x12 -> x9, waiting for transfers between devices: 34.7 us -> 27.2 us  [across(): return lax.ppermute(value, ('dp', 'tensor'), pairs)]
    ppermute x12 -> x9, starting transfers between devices: 15.9 us -> 12.5 us  [across(): return lax.ppermute(value, ('dp', 'tensor'), pairs)]
    unnamed x19 -> x38, local copies, waits for them, and re-layouts: 3.21 us -> 0.77 us
    pallas_call x1, Pallas kernels: 2.9 us -> 1.68 us  [pack_weights(): pl.pallas_call(pack_kernel, out_shape=jax.ShapeDtypeStruct((PACK_ROWS, 12...]
    add x1, other arithmetic: 1.29 us -> 0.11 us  [shards(): item + received[i * size:i * size + size]]
  transfers between devices with their start and end apart: 15 -> 12, of which waited for: 13 -> 10; matrix products, arithmetic and copies ran while one was open for 1% -> 0% of each run, Pallas kernels for 0% -> 0%
where the time goes in v2:
time: 79 us; the launch traced here: 78.8 us
  waiting for transfers between devices  31.3 us (40%)
  Pallas kernels  29.9 us (38%)
  starting transfers between devices  14.4 us (18%)
  between operations  2.25 us (3%)
    ppermute x9, waiting for transfers between devices, across(): return lax.ppermute(value, ('dp', 'tensor'), pairs)  27.2 us
    pallas_call x1, Pallas kernels, run_step(): pl.pallas_call(functools.partial(step_kernel, rt, subs, SUB_OFFSET, order...  24.3 us
    ppermute x9, starting transfers between devices, across(): return lax.ppermute(value, ('dp', 'tensor'), pairs)  12.5 us
    ppermute x3, waiting for transfers between devices, partner(): return lax.ppermute(value, 'tensor', swap)  4.02 us
    pallas_call x1, Pallas kernels, shards(): pl.pallas_call(functools.partial(update_kernel, groups['order'], groups['...  3.86 us
    ppermute x3, starting transfers between devices, partner(): return lax.ppermute(value, 'tensor', swap)  1.93 us
    pallas_call x1, Pallas kernels, pack_weights(): pl.pallas_call(pack_kernel, out_shape=jax.ShapeDtypeStruct((PACK_ROWS, 12...  1.68 us
  transfers between devices with their start and end apart: 12, of which 10 were waited for; matrix products, arithmetic and copies ran while one was open for 0% of the time, Pallas kernels for 0%

profile of v2, /device:TPU:0, one launch (start us, length us, event | category | flops | bytes accessed | tf_op | source)
XLA Modules:
  0.0 78.8 jit_solution(3263969655686881418)
XLA Ops:
  0.7 1.7 %pack.1.pack_own = bf16[3904,128]{1,0:T(8,128)(2,1)S(1)} custom-call(f32[377,128]{1,0:T(8,128)} %refs_8_.1, f32[394,2,128]{2,1,0:T(2,128)} %bitcast.26, f32[394,2,128]{2,1,0:T(2,128)} %bitcast.28, f32[128,256]{1,0:T(8,128)} %refs_10_.1, f32[2,128,256]{2,1,0:T(8,128)} %refs_16_.1, f32[2,128,256]{2,1,0:T(8,128)} %refs_23_.1), custom_call_target="tpu_custom_call" | custom-call | tf_op jit(solution)/shard_map/pack/pallas_call | solution.py:125
  2.3 0.6 collective-permute-start
  3.5 1.6 %collective-permute-done.pack_par = bf16[3904,128]{1,0:T(8,128)(2,1)S(1)} collective-permute-done((bf16[3904,128]{1,0:T(8,128)(2,1)S(1)}, bf16[3904,128]{1,0:T(8,128)(2,1)S(1)}, u32[]{:S(2)}, u32[]{:S(2)}) %collective-permute-start) | collective-permute-done | bytes 999456 | tf_op jit(solution)/shard_map/ppermute | solution.py:661
  5.1 0.7 copy-done.18
  5.8 24.3 %step.1 = (f32[512,128]{1,0:T(8,128)S(1)}, f32[512,128]{1,0:T(8,128)S(1)}, f32[512,128]{1,0:T(8,128)S(1)}, f32[512,128]{1,0:T(8,128)S(1)}, f32[2048,128]{1,0:T(8,128)S(1)}) custom-call(s32[1]{0:T(128)S(6)} %copy.51.count_ref, f32[4]{0:T(128)S(1)} %copy-done.18, bf16[376,4096]{1,0:T(8,128)(2,1)} %bitcast.41, bf16[376,4096]{1,0:T(8,128)(2,1)} %bitcast.42, ...), custom_call_target="tpu_custom_call" | custom-call | tf_op jit(solution)/shard_map/step/pallas_call | solution.py:478
  30.1 0.0 copy-start
  30.1 0.0 copy-start.1
  30.1 0.0 copy-start.2
  30.1 0.0 copy-start.3
  30.1 0.0 copy-start.4
  30.1 0.0 copy-start.5
  30.1 0.0 copy-start.6
  30.1 0.0 copy-start.7
  30.2 0.0 copy-start.8
  30.2 0.0 copy-start.9
  30.2 0.0 copy-start.10
  30.2 0.0 copy-start.11
  30.2 0.0 copy-start.12
  30.2 0.0 copy-start.13
  30.2 0.0 copy-start.14
  30.2 0.0 copy-start.15
  30.3 0.0 copy-start.16
  30.3 0.0 copy-start.17
  30.3 0.4 collective-permute-start.1
  30.7 2.3 %collective-permute-done.1 = f32[2048,128]{1,0:T(8,128)S(1)} collective-permute-done((f32[2048,128]{1,0:T(8,128)S(1)}, f32[2048,128]{1,0:T(8,128)S(1)}, u32[]{:S(2)}, u32[]{:S(2)}) %collective-permute-start.1) | collective-permute-done | bytes 1048608 | tf_op jit(solution)/shard_map/ppermute | solution.py:661
  33.0 0.1 slice_add_fusion.2
  33.1 2.9 %collective-permute-start.2 = (f32[512,128]{1,0:T(8,128)S(1)}, f32[512,128]{1,0:T(8,128)S(1)}, u32[]{:S(2)}, u32[]{:S(2)}) collective-permute-start(f32[512,128]{1,0:T(8,128)S(1)} %get-tuple-element.79), channel_id=1, source_target_pairs={{0,2},{1,9},{2,0},{3,11},{4,6},{5,13},{6,4},{7,15},{8,10},{9,1},{1... | collective-permute-start | bytes 786440 | tf_op jit(solution)/shard_map/ppermute | solution.py:666
  36.0 1.5 %collective-permute-start.4 = (f32[512,128]{1,0:T(8,128)S(1)}, f32[512,128]{1,0:T(8,128)S(1)}, u32[]{:S(2)}, u32[]{:S(2)}) collective-permute-start(f32[512,128]{1,0:T(8,128)S(1)} %get-tuple-element.80), channel_id=1, source_target_pairs={{0,6},{1,25},{2,4},{3,27},{4,2},{5,29},{6,0},{7,31},{8,14},{9,17},... | collective-permute-start | bytes 786440 | tf_op jit(solution)/shard_map/ppermute | solution.py:666
  37.5 0.0 collective-permute-start.3
  37.6 2.8 %collective-permute-done.2 = f32[512,128]{1,0:T(8,128)S(1)} collective-permute-done((f32[512,128]{1,0:T(8,128)S(1)}, f32[512,128]{1,0:T(8,128)S(1)}, u32[]{:S(2)}, u32[]{:S(2)}) %collective-permute-start.2) | collective-permute-done | bytes 262176 | tf_op jit(solution)/shard_map/ppermute | solution.py:666
  40.4 4.4 %collective-permute-done.4 = f32[512,128]{1,0:T(8,128)S(1)} collective-permute-done((f32[512,128]{1,0:T(8,128)S(1)}, f32[512,128]{1,0:T(8,128)S(1)}, u32[]{:S(2)}, u32[]{:S(2)}) %collective-permute-start.4) | collective-permute-done | bytes 262176 | tf_op jit(solution)/shard_map/ppermute | solution.py:666
  44.8 1.9 %collective-permute-done.3 = f32[512,128]{1,0:T(8,128)S(1)} collective-permute-done((f32[512,128]{1,0:T(8,128)S(1)}, f32[512,128]{1,0:T(8,128)S(1)}, u32[]{:S(2)}, u32[]{:S(2)}) %collective-permute-start.3) | collective-permute-done | bytes 262176 | tf_op jit(solution)/shard_map/ppermute | solution.py:666
  46.7 0.1 fusion.2.refs_0_
  46.8 3.7 %collective-permute-start.7 = (f32[512,128]{1,0:T(8,128)S(1)}, f32[512,128]{1,0:T(8,128)S(1)}, u32[]{:S(2)}, u32[]{:S(2)}) collective-permute-start(f32[512,128]{1,0:T(8,128)S(1)} %fusion.2.refs_0_), channel_id=1, source_target_pairs={{0,24},{1,7},{2,26},{3,5},{4,28},{5,3},{6,30},{7,1},{8,16},{9,15},... | collective-permute-start | bytes 786440 | tf_op jit(solution)/shard_map/ppermute | solution.py:666
  50.5 0.8 collective-permute-start.5
  51.2 4.0 %collective-permute-done.7.refs_3_ = f32[512,128]{1,0:T(8,128)S(1)} collective-permute-done((f32[512,128]{1,0:T(8,128)S(1)}, f32[512,128]{1,0:T(8,128)S(1)}, u32[]{:S(2)}, u32[]{:S(2)}) %collective-permute-start.7) | collective-permute-done | bytes 262176 | tf_op jit(solution)/shard_map/ppermute | solution.py:666
  55.2 7.4 %collective-permute-done.6.refs_2_ = f32[512,128]{1,0:T(8,128)S(1)} collective-permute-done((f32[512,128]{1,0:T(8,128)S(1)}, f32[512,128]{1,0:T(8,128)S(1)}, u32[]{:S(2)}, u32[]{:S(2)}) %collective-permute-start.6) | collective-permute-done | bytes 262176 | tf_op jit(solution)/shard_map/ppermute | solution.py:666
  62.7 0.0 collective-permute-done.5.refs_1_
  62.7 0.1 lastsum.1.refs_0_
  62.8 1.8 %collective-permute-start.10 = (f32[520,128]{1,0:T(8,128)S(1)}, f32[520,128]{1,0:T(8,128)S(1)}, u32[]{:S(2)}, u32[]{:S(2)}) collective-permute-start(f32[520,128]{1,0:T(8,128)S(1)} %lastsum.1.refs_0_), channel_id=1, source_target_pairs={{0,6},{1,25},{2,4},{3,27},{4,2},{5,29},{6,0},{7,31},{8,14},{9,17},... | collective-permute-start | bytes 798728 | tf_op jit(solution)/shard_map/ppermute | solution.py:666
  64.6 1.2 %collective-permute-start.9 = (f32[520,128]{1,0:T(8,128)S(1)}, f32[520,128]{1,0:T(8,128)S(1)}, u32[]{:S(2)}, u32[]{:S(2)}) collective-permute-start(f32[520,128]{1,0:T(8,128)S(1)} %lastsum.1.refs_0_), channel_id=1, source_target_pairs={{0,4},{1,17},{2,6},{3,19},{4,0},{5,21},{6,2},{7,23},{8,12},{9,25},... | collective-permute-start | bytes 798728 | tf_op jit(solution)/shard_map/ppermute | solution.py:666
  65.8 0.5 collective-permute-start.8
  66.4 3.9 %collective-permute-done.10.refs_3_ = f32[520,128]{1,0:T(8,128)S(1)} collective-permute-done((f32[520,128]{1,0:T(8,128)S(1)}, f32[520,128]{1,0:T(8,128)S(1)}, u32[]{:S(2)}, u32[]{:S(2)}) %collective-permute-start.10) | collective-permute-done | bytes 266272 | tf_op jit(solution)/shard_map/ppermute | solution.py:666
  70.3 2.8 %collective-permute-done.9.refs_2_ = f32[520,128]{1,0:T(8,128)S(1)} collective-permute-done((f32[520,128]{1,0:T(8,128)S(1)}, f32[520,128]{1,0:T(8,128)S(1)}, u32[]{:S(2)}, u32[]{:S(2)}) %collective-permute-start.9) | collective-permute-done | bytes 266272 | tf_op jit(solution)/shard_map/ppermute | solution.py:666
  73.0 0.0 collective-permute-done.8.refs_1_
  73.1 0.9 %collective-permute-start.11 = (f32[8,128]{1,0:T(8,128)S(1)}, f32[8,128]{1,0:T(8,128)S(1)}, u32[]{:S(2)}, u32[]{:S(2)}) collective-permute-start(f32[8,128]{1,0:T(8,128)S(1)} %slice_add_fusion.4.refs_4_), channel_id=1, source_target_pairs={{0,1},{1,0},{2,3},{3,2},{4,5},{5,4},{6,7},{7,6},{8,9},{9,8},{10,11... | collective-permute-start | bytes 12296 | tf_op jit(solution)/shard_map/ppermute | solution.py:661
  74.6 0.2 collective-permute-done.11.refs_5_
  75.0 3.9 %update.1 = (f32[377,128]{1,0:T(8,128)}, f32[377,128]{1,0:T(8,128)}, f32[377,128]{1,0:T(8,128)}, f32[128,256]{1,0:T(8,128)}, f32[128,256]{1,0:T(8,128)}, /*index...) custom-call(f32[520,128]{1,0:T(8,128)S(1)} %lastsum.1.refs_0_, ...), custom_call_target="tpu_custom_call" | custom-call | tf_op jit(solution)/shard_map/update/pallas_call | solution.py:711
  (21 shorter events, 0.0 us)
Async XLA Ops:
  2.3 2.8 %collective-permute-start = (bf16[3904,128]{1,0:T(8,128)(2,1)S(1)}, bf16[3904,128]{1,0:T(8,128)(2,1)S(1)}, u32[]{:S(2)}, u32[]{:S(2)}) collective-permute-start(bf16[3904,128]{1,0:T(8,128)(2,1)S(1)} %pack.1.pack_own), channel_id=1, source_target_pairs={{0,1},{1,0},{2,3},{3,2},{4,5},{5,4},{6,7},{7,6},{8,9},{9,8},{10,11... | collective-permute-start | bytes 2998280 | tf_op jit(solution)/shard_map/ppermute | solution.py:661
  5.1 0.7 copy-start.18
  30.1 44.8 %copy-start = (f32[2,394,128]{2,0,1:T(2,128)S(1)}, f32[2,394,128]{2,0,1:T(2,128)}, u32[]{:S(2)}) copy-start(f32[2,394,128]{2,0,1:T(2,128)} %param.40) | copy-start | bytes 1210372
  30.1 44.7 %copy-start.1 = (f32[2,394,128]{2,0,1:T(2,128)S(1)}, f32[2,394,128]{2,0,1:T(2,128)}, u32[]{:S(2)}) copy-start(f32[2,394,128]{2,0,1:T(2,128)} %param.44) | copy-start | bytes 1210372
  30.1 44.7 %copy-start.2 = (f32[2,128,256]{2,1,0:T(8,128)S(1)}, f32[2,128,256]{2,1,0:T(8,128)}, u32[]{:S(2)}) copy-start(f32[2,128,256]{2,1,0:T(8,128)} %refs_16_.1) | copy-start | bytes 786436
  30.1 44.7 %copy-start.3 = (f32[2,128,256]{2,1,0:T(8,128)S(1)}, f32[2,128,256]{2,1,0:T(8,128)}, u32[]{:S(2)}) copy-start(f32[2,128,256]{2,1,0:T(8,128)} %refs_23_.1) | copy-start | bytes 786436
  30.1 44.7 %copy-start.4 = (f32[2,2,394,128]{3,1,2,0:T(2,128)S(1)}, f32[2,2,394,128]{3,1,2,0:T(2,128)}, u32[]{:S(2)}) copy-start(f32[2,2,394,128]{3,1,2,0:T(2,128)} %param.51) | copy-start | bytes 2420740
  30.1 44.7 %copy-start.5 = (f32[377,128]{1,0:T(8,128)S(1)}, f32[377,128]{1,0:T(8,128)}, u32[]{:S(2)}) copy-start(f32[377,128]{1,0:T(8,128)} %refs_8_.1) | copy-start | bytes 579076
  30.1 44.7 %copy-start.6 = (f32[2,2,128,256]{3,2,1,0:T(8,128)S(1)}, f32[2,2,128,256]{3,2,1,0:T(8,128)}, u32[]{:S(2)}) copy-start(f32[2,2,128,256]{3,2,1,0:T(8,128)} %refs_17_.1) | copy-start | bytes 1572868
  30.1 44.7 %copy-start.7 = (f32[128,256]{1,0:T(8,128)S(1)}, f32[128,256]{1,0:T(8,128)}, u32[]{:S(2)}) copy-start(f32[128,256]{1,0:T(8,128)} %refs_10_.1) | copy-start | bytes 393220
  30.2 44.7 %copy-start.8 = (f32[2,377,128]{2,0,1:T(2,128)S(1)}, f32[2,377,128]{2,0,1:T(2,128)}, u32[]{:S(2)}) copy-start(f32[2,377,128]{2,0,1:T(2,128)} %param.48) | copy-start | bytes 1158148
  30.2 44.7 %copy-start.9 = (f32[2,128,256]{2,1,0:T(8,128)S(1)}, f32[2,128,256]{2,1,0:T(8,128)}, u32[]{:S(2)}) copy-start(f32[2,128,256]{2,1,0:T(8,128)} %refs_11_.1) | copy-start | bytes 786436
  30.2 44.7 %copy-start.10 = (f32[257,34]{0,1:T(8,128)S(1)}, f32[257,34]{0,1:T(8,128)}, u32[]{:S(2)}) copy-start(f32[257,34]{0,1:T(8,128)} %param.39) | copy-start | bytes 104860
  30.2 44.7 %copy-start.11 = (f32[2,257,34]{1,0,2:T(2,128)S(1)}, f32[2,257,34]{1,0,2:T(2,128)}, u32[]{:S(2)}) copy-start(f32[2,257,34]{1,0,2:T(2,128)} %param.50) | copy-start | bytes 209716
  30.2 44.7 %copy-start.12 = (f32[2,257,2]{1,2,0:T(2,128)S(1)}, f32[2,257,2]{1,2,0:T(2,128)}, u32[]{:S(2)}) copy-start(f32[2,257,2]{1,2,0:T(2,128)} %param.42) | copy-start | bytes 12340
  30.2 44.7 %copy-start.13 = (f32[2,257,2]{1,2,0:T(2,128)S(1)}, f32[2,257,2]{1,2,0:T(2,128)}, u32[]{:S(2)}) copy-start(f32[2,257,2]{1,2,0:T(2,128)} %param.46) | copy-start | bytes 12340
  30.2 44.7 %copy-start.14 = (f32[3,256]{1,0:T(4,128)S(1)}, f32[3,256]{1,0:T(4,128)}, u32[]{:S(2)}) copy-start(f32[3,256]{1,0:T(4,128)} %refs_20_.1) | copy-start | bytes 9220
  30.2 44.7 %copy-start.15 = (f32[2,2,257,2]{2,3,1,0:T(2,128)S(1)}, f32[2,2,257,2]{2,3,1,0:T(2,128)}, u32[]{:S(2)}) copy-start(f32[2,2,257,2]{2,3,1,0:T(2,128)} %param.53) | copy-start | bytes 24676
  30.3 44.7 %copy-start.16 = (f32[2,256]{1,0:T(2,128)S(1)}, f32[2,256]{1,0:T(2,128)}, u32[]{:S(2)}) copy-start(f32[2,256]{1,0:T(2,128)} %refs_25_.1) | copy-start | bytes 6148
  30.3 44.7 %copy-start.17 = (f32[2,3,256]{2,0,1:T(2,128)S(1)}, f32[2,3,256]{2,0,1:T(2,128)}, u32[]{:S(2)}) copy-start(f32[2,3,256]{2,0,1:T(2,128)} %param.54) | copy-start | bytes 18436
  30.3 2.7 %collective-permute-start.1 = (f32[2048,128]{1,0:T(8,128)S(1)}, f32[2048,128]{1,0:T(8,128)S(1)}, u32[]{:S(2)}, u32[]{:S(2)}) collective-permute-start(f32[2048,128]{1,0:T(8,128)S(1)} %get-tuple-element.52), channel_id=1, source_target_pairs={{0,1},{1,0},{2,3},{3,2},{4,5},{5,4},{6,7},{7,6},{8,9},{9,8},{10,11... | collective-permute-start | bytes 3145736 | tf_op jit(solution)/shard_map/ppermute | solution.py:661
  33.1 7.3 %collective-permute-start.2 = (f32[512,128]{1,0:T(8,128)S(1)}, f32[512,128]{1,0:T(8,128)S(1)}, u32[]{:S(2)}, u32[]{:S(2)}) collective-permute-start(f32[512,128]{1,0:T(8,128)S(1)} %get-tuple-element.79), channel_id=1, source_target_pairs={{0,2},{1,9},{2,0},{3,11},{4,6},{5,13},{6,4},{7,15},{8,10},{9,1},{1... | collective-permute-start | bytes 786440 | tf_op jit(solution)/shard_map/ppermute | solution.py:666
  36.0 8.7 %collective-permute-start.4 = (f32[512,128]{1,0:T(8,128)S(1)}, f32[512,128]{1,0:T(8,128)S(1)}, u32[]{:S(2)}, u32[]{:S(2)}) collective-permute-start(f32[512,128]{1,0:T(8,128)S(1)} %get-tuple-element.80), channel_id=1, source_target_pairs={{0,6},{1,25},{2,4},{3,27},{4,2},{5,29},{6,0},{7,31},{8,14},{9,17},... | collective-permute-start | bytes 786440 | tf_op jit(solution)/shard_map/ppermute | solution.py:666
  37.5 9.2 %collective-permute-start.3 = (f32[512,128]{1,0:T(8,128)S(1)}, f32[512,128]{1,0:T(8,128)S(1)}, u32[]{:S(2)}, u32[]{:S(2)}) collective-permute-start(f32[512,128]{1,0:T(8,128)S(1)} %get-tuple-element.81), channel_id=1, source_target_pairs={{0,4},{1,17},{2,6},{3,19},{4,0},{5,21},{6,2},{7,23},{8,12},{9,25},... | collective-permute-start | bytes 786440 | tf_op jit(solution)/shard_map/ppermute | solution.py:666
  46.8 8.4 %collective-permute-start.7 = (f32[512,128]{1,0:T(8,128)S(1)}, f32[512,128]{1,0:T(8,128)S(1)}, u32[]{:S(2)}, u32[]{:S(2)}) collective-permute-start(f32[512,128]{1,0:T(8,128)S(1)} %fusion.2.refs_0_), channel_id=1, source_target_pairs={{0,24},{1,7},{2,26},{3,5},{4,28},{5,3},{6,30},{7,1},{8,16},{9,15},... | collective-permute-start | bytes 786440 | tf_op jit(solution)/shard_map/ppermute | solution.py:666
  50.5 12.2 %collective-permute-start.6 = (f32[512,128]{1,0:T(8,128)S(1)}, f32[512,128]{1,0:T(8,128)S(1)}, u32[]{:S(2)}, u32[]{:S(2)}) collective-permute-start(f32[512,128]{1,0:T(8,128)S(1)} %fusion.2.refs_0_), channel_id=1, source_target_pairs={{0,16},{1,5},{2,18},{3,7},{4,20},{5,1},{6,22},{7,3},{8,24},{9,13},... | collective-permute-start | bytes 786440 | tf_op jit(solution)/shard_map/ppermute | solution.py:666
  50.5 12.2 %collective-permute-start.5 = (f32[512,128]{1,0:T(8,128)S(1)}, f32[512,128]{1,0:T(8,128)S(1)}, u32[]{:S(2)}, u32[]{:S(2)}) collective-permute-start(f32[512,128]{1,0:T(8,128)S(1)} %fusion.2.refs_0_), channel_id=1, source_target_pairs={{0,8},{1,3},{2,10},{3,1},{4,12},{5,7},{6,14},{7,5},{8,0},{9,11},{1... | collective-permute-start | bytes 786440 | tf_op jit(solution)/shard_map/ppermute | solution.py:666
  62.8 7.5 %collective-permute-start.10 = (f32[520,128]{1,0:T(8,128)S(1)}, f32[520,128]{1,0:T(8,128)S(1)}, u32[]{:S(2)}, u32[]{:S(2)}) collective-permute-start(f32[520,128]{1,0:T(8,128)S(1)} %lastsum.1.refs_0_), channel_id=1, source_target_pairs={{0,6},{1,25},{2,4},{3,27},{4,2},{5,29},{6,0},{7,31},{8,14},{9,17},... | collective-permute-start | bytes 798728 | tf_op jit(solution)/shard_map/ppermute | solution.py:666
  64.6 8.4 %collective-permute-start.9 = (f32[520,128]{1,0:T(8,128)S(1)}, f32[520,128]{1,0:T(8,128)S(1)}, u32[]{:S(2)}, u32[]{:S(2)}) collective-permute-start(f32[520,128]{1,0:T(8,128)S(1)} %lastsum.1.refs_0_), channel_id=1, source_target_pairs={{0,4},{1,17},{2,6},{3,19},{4,0},{5,21},{6,2},{7,23},{8,12},{9,25},... | collective-permute-start | bytes 798728 | tf_op jit(solution)/shard_map/ppermute | solution.py:666
  65.8 7.2 %collective-permute-start.8 = (f32[520,128]{1,0:T(8,128)S(1)}, f32[520,128]{1,0:T(8,128)S(1)}, u32[]{:S(2)}, u32[]{:S(2)}) collective-permute-start(f32[520,128]{1,0:T(8,128)S(1)} %lastsum.1.refs_0_), channel_id=1, source_target_pairs={{0,2},{1,9},{2,0},{3,11},{4,6},{5,13},{6,4},{7,15},{8,10},{9,1},{1... | collective-permute-start | bytes 798728 | tf_op jit(solution)/shard_map/ppermute | solution.py:666
  73.1 1.8 %collective-permute-start.11 = (f32[8,128]{1,0:T(8,128)S(1)}, f32[8,128]{1,0:T(8,128)S(1)}, u32[]{:S(2)}, u32[]{:S(2)}) collective-permute-start(f32[8,128]{1,0:T(8,128)S(1)} %slice_add_fusion.4.refs_4_), channel_id=1, source_target_pairs={{0,1},{1,0},{2,3},{3,2},{4,5},{5,4},{6,7},{7,6},{8,9},{9,8},{10,11... | collective-permute-start | bytes 12296 | tf_op jit(solution)/shard_map/ppermute | solution.py:661

commit v3 on v2

--- a/solution.py
+++ b/solution.py
@@ -131,6 +131,14 @@
     )(*in_hbm(a_w1, c_w1, t_w1, a_w2, c_w2, t_w2))
 
 
+def one_minus_power(gap, exponent):
+    total = jnp.float32(0.0)
+    for bit in range(30, -1, -1):
+        total = total * (2.0 - total)
+        total = jnp.where((exponent >> bit) & 1 == 1, total + gap * (1.0 - total), total)
+    return total
+
+
 def step_kernel(
     rows_tile,
     subs,
@@ -140,6 +148,7 @@
     n_own,
     count_ref,
     state_ref,
+    when_ref,
     obs_ref,
     next_ref,
     action_ref,
@@ -157,7 +166,7 @@
     *rest,
 ):
     own_outs = rest[:n_own]
-    par_out = rest[n_own]
+    par_out, fix_out = rest[n_own : n_own + 2]
     (
         w1t, w2, w2t, w1a, wht_a, wh_a, wht_c, wh_c, hb, b2b, wqb,
         xn_all, xd_all, xq_all,
@@ -165,7 +174,7 @@
         h1n_all, h2n_all, h1_all, h2_all, h1q_all, h2q_all, h1t_all, h2t_all,
         g1_all, g1q_all, g2_all, dz1_all, dz2_all, dzq1_all, dzq2_all,
         acc1, acc2, acc_ha, acc_hc, acc_b, acc_s, flat,
-    ) = rest[n_own + 1 :]
+    ) = rest[n_own + 2 :]
     step = pl.program_id(0)
     n_steps = pl.num_programs(0)
     t_index = lax.axis_index("tensor")
@@ -174,6 +183,9 @@
 
     @pl.when(step == 0)
     def _():
+        for row, gap in enumerate((0.1, 0.001)):
+            fix = one_minus_power(jnp.float32(gap), when_ref[0])
+            fix_out[row : row + 1, :] = 1.0 / jnp.full((1, 128), fix, F32)
         for net in range(5):
             for side, pack in enumerate((pack_own, pack_par)):
                 rows = slice(net * H + side * HALF, net * H + side * HALF + HALF)
@@ -445,7 +457,7 @@
 SUB_OFFSET = 2
 
 
-def run_step(groups, arrays, pack_own, pack_par, small, count, state):
+def run_step(groups, arrays, pack_own, pack_par, small, count, state, when):
     obs, next_obs, action, noise, next_noise, reward, terminal = arrays
     rows = obs.shape[1] // groups["tensor"]
     rt = min(SUB_ROWS, rows)
@@ -475,17 +487,18 @@
         VMEM((3 * H, 128), F32), VMEM((128, 128), F32), VMEM((2, FLAT_ROWS, 128), F32),
     ]
     outs = [jax.ShapeDtypeStruct((FLAT_ROWS // n_own, 128), F32)] * n_own + [jax.ShapeDtypeStruct((FLAT_ROWS, 128), F32)]
+    outs = outs + [jax.ShapeDtypeStruct((8, 128), F32)]
     return pl.pallas_call(
         functools.partial(step_kernel, rt, subs, SUB_OFFSET, order, groups["orders"], n_own),
         grid=(steps,),
-        in_specs=[smem, smem, tile(OBS), tile(OBS), tile(ACT), tile(ACT), tile(ACT), tile(1), tile(1)] + [whole] * 7,
-        out_specs=[whole] * (n_own + 1),
+        in_specs=[smem, smem, smem, tile(OBS), tile(OBS), tile(ACT), tile(ACT), tile(ACT), tile(1), tile(1)] + [whole] * 7,
+        out_specs=[whole] * (n_own + 2),
         out_shape=outs,
         scratch_shapes=scratch,
         compiler_params=pltpu.CompilerParams(vmem_limit_bytes=STEP_VMEM),
         name="step",
     )(
-        count, state, *in_hbm(obs, next_obs, action, noise, next_noise, reward, terminal),
+        count, *in_hbm(state), when, *in_hbm(obs, next_obs, action, noise, next_noise, reward, terminal),
         pack_own, pack_par, *in_hbm(*small),
     )
 
@@ -517,18 +530,13 @@
     )(*values)
 
 
-def one_minus_power(gap, exponent):
-    total = jnp.float32(0.0)
-    for bit in range(30, -1, -1):
-        total = total * (2.0 - total)
-        total = jnp.where((exponent >> bit) & 1 == 1, total + gap * (1.0 - total), total)
-    return total
+AT_ONCE = 64
 
 
 def update_kernel(order, orders, n_parts, sizes, *refs):
     parts = refs[:n_parts]
     (
-        square_own, square_other, step_ref, state_ref,
+        square_own, square_other, fix_ref, state_ref,
         a_w1, a_w1_m, a_w2, a_w2_m, a_head, a_head_m,
         c_w1, c_w1_m, c_w2, c_w2_m, c_head, c_head_m, bias2, bias2_m,
         t_w1, t_w2, t_head, t_bias2,
@@ -557,11 +565,7 @@
     norm = jnp.sqrt(total) * inverse
     clip = jnp.minimum(1.0, CLIP / (norm + 1e-06))
     scale = clip * inverse
-    t = step_ref[0]
-    first_fix = one_minus_power(jnp.float32(0.1), t)
-    second_fix = one_minus_power(jnp.float32(0.001), t)
-    unfix_one = 1.0 / jnp.full((1, 1), first_fix, F32)
-    unfix_two = 1.0 / jnp.full((1, 1), second_fix, F32)
+    unfix_one, unfix_two = fix_ref[0:1, 0:1], fix_ref[1:2, 0:1]
 
     def adam(weight, first, second, grad, decay=DECAY):
         first = BETA_ONE * first + (1.0 - BETA_ONE) * grad
@@ -575,13 +579,16 @@
         return (1.0 - RHO) * target + RHO * new
 
     moments = a_w1_m.reshape(2 * A_IN, 128)
-    new, first, second = adam(
-        a_w1[...], moments[pl.ds(0, A_IN, stride=2), :], moments[pl.ds(1, A_IN, stride=2), :],
-        flat[FLAT_AW1 : FLAT_AW1 + A_IN, :] * scale,
-    )
-    o_a_w1[...] = new
-    o_a_w1_f[...] = first
-    o_a_w1_s[...] = second
+    for r in range(0, A_IN, AT_ONCE):
+        n = min(AT_ONCE, A_IN - r)
+        rows = slice(r, r + n)
+        new, first, second = adam(
+            a_w1[rows, :], moments[pl.ds(2 * r, n, stride=2), :], moments[pl.ds(2 * r + 1, n, stride=2), :],
+            flat[FLAT_AW1 + r : FLAT_AW1 + r + n, :] * scale,
+        )
+        o_a_w1[rows, :] = new
+        o_a_w1_f[rows, :] = first
+        o_a_w1_s[rows, :] = second
     for net in range(3):
         for part in range(2):
             lanes = slice(part * 128, part * 128 + 128)
@@ -600,14 +607,16 @@
                 o_c_w2_f[c, :, lanes] = first
                 o_c_w2_s[c, :, lanes] = second
     both = 2 * C_IN
-    new, first, second = adam(
-        c_w1.reshape(both, 128)[...], c_w1_m.at[0].reshape(both, 128)[...], c_w1_m.at[1].reshape(both, 128)[...],
-        flat[FLAT_CW1 : FLAT_CW1 + both, :] * scale,
-    )
-    o_c_w1_f.reshape(both, 128)[...] = first
-    o_c_w1_s.reshape(both, 128)[...] = second
-    rows_new[...] = new
-    rows_target[...] = polyak(t_w1.reshape(both, 128)[...], new)
+    for r in range(0, both, AT_ONCE):
+        rows = slice(r, min(r + AT_ONCE, both))
+        new, first, second = adam(
+            c_w1.reshape(both, 128)[rows, :], c_w1_m.at[0].reshape(both, 128)[rows, :],
+            c_w1_m.at[1].reshape(both, 128)[rows, :], flat[rows, :] * scale,
+        )
+        o_c_w1_f.reshape(both, 128)[rows, :] = first
+        o_c_w1_s.reshape(both, 128)[rows, :] = second
+        rows_new[rows, :] = new
+        rows_target[rows, :] = polyak(t_w1.reshape(both, 128)[rows, :], new)
     four = o_c_w1.reshape(2 * both, 128)
     for c in range(2):
         four[pl.ds(c, C_IN, stride=4), :] = rows_new[pl.ds(c, C_IN, stride=2), :]
@@ -674,8 +683,8 @@
         tr(obs), tr(next_obs), tr(action), tr(noise), tr(next_noise), reward.reshape(1, -1), terminal.reshape(1, -1),
     )
     small = (a_headv, c_headv, tc_headv, bias2, tc_bias2)
-    outs = run_step(groups, arrays, pack, pack_par, small, counts, state)
-    own, par = outs[:-1], outs[-1]
+    outs = run_step(groups, arrays, pack, pack_par, small, counts, state, step_count)
+    own, par, fixes = outs[:-2], outs[-2], outs[-1]
     received = partner(par)
     size = FLAT_ROWS // len(own)
     values = [item + received[i * size : i * size + size] for i, item in enumerate(own)]
@@ -710,14 +719,14 @@
     smem = pl.BlockSpec(memory_space=pltpu.SMEM)
     res = pl.pallas_call(
         functools.partial(update_kernel, groups["order"], groups["orders"], len(parts), (size, size + 8)),
-        in_specs=[whole] * (len(parts) + 2) + [smem, smem] + [whole] * 18,
+        in_specs=[whole] * (len(parts) + 3) + [smem] + [whole] * 18,
         out_specs=[whole] * 21 + [smem, smem],
         out_shape=[sds(s, F32) for s in shapes],
         scratch_shapes=[VMEM((FLAT_ROWS, 128), F32), VMEM((2 * C_IN, 128), F32), VMEM((2 * C_IN, 128), F32)],
         compiler_params=pltpu.CompilerParams(vmem_limit_bytes=UPDATE_VMEM),
         name="update",
     )(
-        *parts, own_square, other_square, step_count, state,
+        *parts, own_square, other_square, fixes, state,
         a_w1, tr(a_w1_mom, (1, 0, 2)), a_w2, a_w2_mom, a_headv, tr(a_head_mom, (2, 0, 1)),
         c_w1v, tr(c_w1_mom, (0, 2, 1, 3)), c_w2, c_w2_mom, c_headv, tr(c_head_mom, (0, 1, 3, 2)),
         bias2, tr(bias2_mom, (1, 0, 2)), tc_w1v, tc_w2, tc_headv, tc_bias2,

time: 79 us -> 78.1 us (0.989)
  no operation moved by 1% of the time
where the time goes in v3:
time: 78.1 us; the launch traced here: 77.9 us
  waiting for transfers between devices  31.3 us (40%)
  Pallas kernels  29.7 us (38%)
  starting transfers between devices  14.4 us (18%)
  between operations  2.26 us (3%)
    ppermute x9, waiting for transfers between devices, across(): return lax.ppermute(value, ('dp', 'tensor'), pairs)  27.2 us
    pallas_call x1, Pallas kernels, run_step(): pl.pallas_call(functools.partial(step_kernel, rt, subs, SUB_OFFSET, order...  24.3 us
    ppermute x9, starting transfers between devices, across(): return lax.ppermute(value, ('dp', 'tensor'), pairs)  12.5 us
    ppermute x3, waiting for transfers between devices, partner(): return lax.ppermute(value, 'tensor', swap)  4.03 us
    pallas_call x1, Pallas kernels, shards(): pl.pallas_call(functools.partial(update_kernel, groups['order'], groups['...  3.58 us
    ppermute x3, starting transfers between devices, partner(): return lax.ppermute(value, 'tensor', swap)  1.96 us
    pallas_call x1, Pallas kernels, pack_weights(): pl.pallas_call(pack_kernel, out_shape=jax.ShapeDtypeStruct((PACK_ROWS, 12...  1.68 us
  transfers between devices with their start and end apart: 12, of which 10 were waited for; matrix products, arithmetic and copies ran while one was open for 0% of the time, Pallas kernels for 0%

profile of v3, /device:TPU:0, one launch (start us, length us, event | category | flops | bytes accessed | tf_op | source)
XLA Modules:
  0.0 77.9 jit_solution(4680232615920700352)
XLA Ops:
  0.7 1.7 %pack.1.pack_own = bf16[3904,128]{1,0:T(8,128)(2,1)S(1)} custom-call(f32[377,128]{1,0:T(8,128)} %refs_8_.1, f32[394,2,128]{2,1,0:T(2,128)} %bitcast.26, f32[394,2,128]{2,1,0:T(2,128)} %bitcast.28, f32[128,256]{1,0:T(8,128)} %refs_10_.1, f32[2,128,256]{2,1,0:T(8,128)} %refs_16_.1, f32[2,128,256]{2,1,0:T(8,128)} %refs_23_.1), custom_call_target="tpu_custom_call" | custom-call | tf_op jit(solution)/shard_map/pack/pallas_call | solution.py:125
  2.3 0.6 collective-permute-start
  4.2 0.9 %collective-permute-done.pack_par = bf16[3904,128]{1,0:T(8,128)(2,1)S(1)} collective-permute-done((bf16[3904,128]{1,0:T(8,128)(2,1)S(1)}, bf16[3904,128]{1,0:T(8,128)(2,1)S(1)}, u32[]{:S(2)}, u32[]{:S(2)}) %collective-permute-start) | collective-permute-done | bytes 999456 | tf_op jit(solution)/shard_map/ppermute | solution.py:670
  5.1 24.3 %step.1 = (f32[512,128]{1,0:T(8,128)S(1)}, f32[512,128]{1,0:T(8,128)S(1)}, f32[512,128]{1,0:T(8,128)S(1)}, f32[512,128]{1,0:T(8,128)S(1)}, f32[2048,128]{1,0:T(8,128)S(1)}, /*index=5*/f32[8,128]{1,0:T(8,128)S(1)}) custom-call(s32[1]{0:T(128)S(6)} %copy.51.count_ref, f32[4]{0:T(128)} %refs_7_.1, s32[1]{0:T(128)S(6)} %copy.52.when_ref, ...), custom_call_target="tpu_custom_call" | custom-call | tf_op jit(solution)/shard_map/step/pallas_call | solution.py:491
  29.4 0.0 copy-start
  29.4 0.0 copy-start.1
  29.4 0.0 copy-start.2
  29.4 0.0 copy-start.3
  29.5 0.0 copy-start.4
  29.5 0.0 copy-start.5
  29.5 0.0 copy-start.6
  29.5 0.0 copy-start.7
  29.5 0.0 copy-start.8
  29.5 0.0 copy-start.9
  29.5 0.0 copy-start.10
  29.5 0.0 copy-start.11
  29.5 0.0 copy-start.12
  29.6 0.0 copy-start.13
  29.6 0.0 copy-start.14
  29.6 0.0 copy-start.15
  29.6 0.0 copy-start.16
  29.6 0.0 copy-start.17
  29.6 0.0 copy-start.18
  29.6 0.4 collective-permute-start.1
  30.1 2.3 %collective-permute-done.1 = f32[2048,128]{1,0:T(8,128)S(1)} collective-permute-done((f32[2048,128]{1,0:T(8,128)S(1)}, f32[2048,128]{1,0:T(8,128)S(1)}, u32[]{:S(2)}, u32[]{:S(2)}) %collective-permute-start.1) | collective-permute-done | bytes 1048608 | tf_op jit(solution)/shard_map/ppermute | solution.py:670
  32.4 0.1 slice_add_fusion.2
  32.5 2.9 %collective-permute-start.2 = (f32[512,128]{1,0:T(8,128)S(1)}, f32[512,128]{1,0:T(8,128)S(1)}, u32[]{:S(2)}, u32[]{:S(2)}) collective-permute-start(f32[512,128]{1,0:T(8,128)S(1)} %get-tuple-element.81), channel_id=1, source_target_pairs={{0,2},{1,9},{2,0},{3,11},{4,6},{5,13},{6,4},{7,15},{8,10},{9,1},{1... | collective-permute-start | bytes 786440 | tf_op jit(solution)/shard_map/ppermute | solution.py:675
  35.4 1.5 %collective-permute-start.4 = (f32[512,128]{1,0:T(8,128)S(1)}, f32[512,128]{1,0:T(8,128)S(1)}, u32[]{:S(2)}, u32[]{:S(2)}) collective-permute-start(f32[512,128]{1,0:T(8,128)S(1)} %get-tuple-element.82), channel_id=1, source_target_pairs={{0,6},{1,25},{2,4},{3,27},{4,2},{5,29},{6,0},{7,31},{8,14},{9,17},... | collective-permute-start | bytes 786440 | tf_op jit(solution)/shard_map/ppermute | solution.py:675
  36.9 0.0 collective-permute-start.3
  36.9 2.8 %collective-permute-done.2 = f32[512,128]{1,0:T(8,128)S(1)} collective-permute-done((f32[512,128]{1,0:T(8,128)S(1)}, f32[512,128]{1,0:T(8,128)S(1)}, u32[]{:S(2)}, u32[]{:S(2)}) %collective-permute-start.2) | collective-permute-done | bytes 262176 | tf_op jit(solution)/shard_map/ppermute | solution.py:675
  39.7 4.4 %collective-permute-done.4 = f32[512,128]{1,0:T(8,128)S(1)} collective-permute-done((f32[512,128]{1,0:T(8,128)S(1)}, f32[512,128]{1,0:T(8,128)S(1)}, u32[]{:S(2)}, u32[]{:S(2)}) %collective-permute-start.4) | collective-permute-done | bytes 262176 | tf_op jit(solution)/shard_map/ppermute | solution.py:675
  44.1 1.9 %collective-permute-done.3 = f32[512,128]{1,0:T(8,128)S(1)} collective-permute-done((f32[512,128]{1,0:T(8,128)S(1)}, f32[512,128]{1,0:T(8,128)S(1)}, u32[]{:S(2)}, u32[]{:S(2)}) %collective-permute-start.3) | collective-permute-done | bytes 262176 | tf_op jit(solution)/shard_map/ppermute | solution.py:675
  46.0 0.1 fusion.2.refs_0_
  46.1 3.7 %collective-permute-start.7 = (f32[512,128]{1,0:T(8,128)S(1)}, f32[512,128]{1,0:T(8,128)S(1)}, u32[]{:S(2)}, u32[]{:S(2)}) collective-permute-start(f32[512,128]{1,0:T(8,128)S(1)} %fusion.2.refs_0_), channel_id=1, source_target_pairs={{0,24},{1,7},{2,26},{3,5},{4,28},{5,3},{6,30},{7,1},{8,16},{9,15},... | collective-permute-start | bytes 786440 | tf_op jit(solution)/shard_map/ppermute | solution.py:675
  49.8 0.8 collective-permute-start.5
  50.6 4.0 %collective-permute-done.7.refs_3_ = f32[512,128]{1,0:T(8,128)S(1)} collective-permute-done((f32[512,128]{1,0:T(8,128)S(1)}, f32[512,128]{1,0:T(8,128)S(1)}, u32[]{:S(2)}, u32[]{:S(2)}) %collective-permute-start.7) | collective-permute-done | bytes 262176 | tf_op jit(solution)/shard_map/ppermute | solution.py:675
  54.6 7.4 %collective-permute-done.6.refs_2_ = f32[512,128]{1,0:T(8,128)S(1)} collective-permute-done((f32[512,128]{1,0:T(8,128)S(1)}, f32[512,128]{1,0:T(8,128)S(1)}, u32[]{:S(2)}, u32[]{:S(2)}) %collective-permute-start.6) | collective-permute-done | bytes 262176 | tf_op jit(solution)/shard_map/ppermute | solution.py:675
  62.0 0.0 collective-permute-done.5.refs_1_
  62.0 0.1 lastsum.1.refs_0_
  62.1 1.8 %collective-permute-start.10 = (f32[520,128]{1,0:T(8,128)S(1)}, f32[520,128]{1,0:T(8,128)S(1)}, u32[]{:S(2)}, u32[]{:S(2)}) collective-permute-start(f32[520,128]{1,0:T(8,128)S(1)} %lastsum.1.refs_0_), channel_id=1, source_target_pairs={{0,6},{1,25},{2,4},{3,27},{4,2},{5,29},{6,0},{7,31},{8,14},{9,17},... | collective-permute-start | bytes 798728 | tf_op jit(solution)/shard_map/ppermute | solution.py:675
  64.0 1.2 %collective-permute-start.9 = (f32[520,128]{1,0:T(8,128)S(1)}, f32[520,128]{1,0:T(8,128)S(1)}, u32[]{:S(2)}, u32[]{:S(2)}) collective-permute-start(f32[520,128]{1,0:T(8,128)S(1)} %lastsum.1.refs_0_), channel_id=1, source_target_pairs={{0,4},{1,17},{2,6},{3,19},{4,0},{5,21},{6,2},{7,23},{8,12},{9,25},... | collective-permute-start | bytes 798728 | tf_op jit(solution)/shard_map/ppermute | solution.py:675
  65.2 0.5 collective-permute-start.8
  65.7 3.9 %collective-permute-done.10.refs_3_ = f32[520,128]{1,0:T(8,128)S(1)} collective-permute-done((f32[520,128]{1,0:T(8,128)S(1)}, f32[520,128]{1,0:T(8,128)S(1)}, u32[]{:S(2)}, u32[]{:S(2)}) %collective-permute-start.10) | collective-permute-done | bytes 266272 | tf_op jit(solution)/shard_map/ppermute | solution.py:675
  69.6 2.8 %collective-permute-done.9.refs_2_ = f32[520,128]{1,0:T(8,128)S(1)} collective-permute-done((f32[520,128]{1,0:T(8,128)S(1)}, f32[520,128]{1,0:T(8,128)S(1)}, u32[]{:S(2)}, u32[]{:S(2)}) %collective-permute-start.9) | collective-permute-done | bytes 266272 | tf_op jit(solution)/shard_map/ppermute | solution.py:675
  72.4 0.0 collective-permute-done.8.refs_1_
  72.4 1.0 %collective-permute-start.11 = (f32[8,128]{1,0:T(8,128)S(1)}, f32[8,128]{1,0:T(8,128)S(1)}, u32[]{:S(2)}, u32[]{:S(2)}) collective-permute-start(f32[8,128]{1,0:T(8,128)S(1)} %slice_add_fusion.4.refs_4_), channel_id=1, source_target_pairs={{0,1},{1,0},{2,3},{3,2},{4,5},{5,4},{6,7},{7,6},{8,9},{9,8},{10,11... | collective-permute-start | bytes 12296 | tf_op jit(solution)/shard_map/ppermute | solution.py:670
  73.3 0.8 %collective-permute-done.11.refs_5_ = f32[8,128]{1,0:T(8,128)S(1)} collective-permute-done((f32[8,128]{1,0:T(8,128)S(1)}, f32[8,128]{1,0:T(8,128)S(1)}, u32[]{:S(2)}, u32[]{:S(2)}) %collective-permute-start.11) | collective-permute-done | bytes 4128 | tf_op jit(solution)/shard_map/ppermute | solution.py:670
  74.3 3.6 %update.1 = (f32[377,128]{1,0:T(8,128)}, f32[377,128]{1,0:T(8,128)}, f32[377,128]{1,0:T(8,128)}, f32[128,256]{1,0:T(8,128)}, f32[128,256]{1,0:T(8,128)}, /*index...) custom-call(f32[520,128]{1,0:T(8,128)S(1)} %lastsum.1.refs_0_, ...), custom_call_target="tpu_custom_call" | custom-call | tf_op jit(solution)/shard_map/update/pallas_call | solution.py:720
  (21 shorter events, 0.0 us)
Async XLA Ops:
  2.3 2.8 %collective-permute-start = (bf16[3904,128]{1,0:T(8,128)(2,1)S(1)}, bf16[3904,128]{1,0:T(8,128)(2,1)S(1)}, u32[]{:S(2)}, u32[]{:S(2)}) collective-permute-start(bf16[3904,128]{1,0:T(8,128)(2,1)S(1)} %pack.1.pack_own), channel_id=1, source_target_pairs={{0,1},{1,0},{2,3},{3,2},{4,5},{5,4},{6,7},{7,6},{8,9},{9,8},{10,11... | collective-permute-start | bytes 2998280 | tf_op jit(solution)/shard_map/ppermute | solution.py:670
  29.4 44.8 %copy-start = (f32[2,394,128]{2,0,1:T(2,128)S(1)}, f32[2,394,128]{2,0,1:T(2,128)}, u32[]{:S(2)}) copy-start(f32[2,394,128]{2,0,1:T(2,128)} %param.40) | copy-start | bytes 1210372
  29.4 44.7 %copy-start.1 = (f32[2,394,128]{2,0,1:T(2,128)S(1)}, f32[2,394,128]{2,0,1:T(2,128)}, u32[]{:S(2)}) copy-start(f32[2,394,128]{2,0,1:T(2,128)} %param.44) | copy-start | bytes 1210372
  29.4 44.7 %copy-start.2 = (f32[2,128,256]{2,1,0:T(8,128)S(1)}, f32[2,128,256]{2,1,0:T(8,128)}, u32[]{:S(2)}) copy-start(f32[2,128,256]{2,1,0:T(8,128)} %refs_16_.1) | copy-start | bytes 786436
  29.4 44.7 %copy-start.3 = (f32[2,128,256]{2,1,0:T(8,128)S(1)}, f32[2,128,256]{2,1,0:T(8,128)}, u32[]{:S(2)}) copy-start(f32[2,128,256]{2,1,0:T(8,128)} %refs_23_.1) | copy-start | bytes 786436
  29.5 44.7 %copy-start.4 = (f32[2,2,394,128]{3,1,2,0:T(2,128)S(1)}, f32[2,2,394,128]{3,1,2,0:T(2,128)}, u32[]{:S(2)}) copy-start(f32[2,2,394,128]{3,1,2,0:T(2,128)} %param.51) | copy-start | bytes 2420740
  29.5 44.7 %copy-start.5 = (f32[377,128]{1,0:T(8,128)S(1)}, f32[377,128]{1,0:T(8,128)}, u32[]{:S(2)}) copy-start(f32[377,128]{1,0:T(8,128)} %refs_8_.1) | copy-start | bytes 579076
  29.5 44.7 %copy-start.6 = (f32[2,2,128,256]{3,2,1,0:T(8,128)S(1)}, f32[2,2,128,256]{3,2,1,0:T(8,128)}, u32[]{:S(2)}) copy-start(f32[2,2,128,256]{3,2,1,0:T(8,128)} %refs_17_.1) | copy-start | bytes 1572868
  29.5 44.7 %copy-start.7 = (f32[128,256]{1,0:T(8,128)S(1)}, f32[128,256]{1,0:T(8,128)}, u32[]{:S(2)}) copy-start(f32[128,256]{1,0:T(8,128)} %refs_10_.1) | copy-start | bytes 393220
  29.5 44.7 %copy-start.8 = (f32[2,377,128]{2,0,1:T(2,128)S(1)}, f32[2,377,128]{2,0,1:T(2,128)}, u32[]{:S(2)}) copy-start(f32[2,377,128]{2,0,1:T(2,128)} %param.48) | copy-start | bytes 1158148
  29.5 44.7 %copy-start.9 = (f32[2,128,256]{2,1,0:T(8,128)S(1)}, f32[2,128,256]{2,1,0:T(8,128)}, u32[]{:S(2)}) copy-start(f32[2,128,256]{2,1,0:T(8,128)} %refs_11_.1) | copy-start | bytes 786436
  29.5 44.7 %copy-start.10 = (f32[257,34]{0,1:T(8,128)S(1)}, f32[257,34]{0,1:T(8,128)}, u32[]{:S(2)}) copy-start(f32[257,34]{0,1:T(8,128)} %param.39) | copy-start | bytes 104860
  29.5 44.7 %copy-start.11 = (f32[2,257,34]{1,0,2:T(2,128)S(1)}, f32[2,257,34]{1,0,2:T(2,128)}, u32[]{:S(2)}) copy-start(f32[2,257,34]{1,0,2:T(2,128)} %param.50) | copy-start | bytes 209716
  29.5 44.7 %copy-start.12 = (f32[2,257,2]{1,2,0:T(2,128)S(1)}, f32[2,257,2]{1,2,0:T(2,128)}, u32[]{:S(2)}) copy-start(f32[2,257,2]{1,2,0:T(2,128)} %param.42) | copy-start | bytes 12340
  29.6 44.7 %copy-start.13 = (f32[2,257,2]{1,2,0:T(2,128)S(1)}, f32[2,257,2]{1,2,0:T(2,128)}, u32[]{:S(2)}) copy-start(f32[2,257,2]{1,2,0:T(2,128)} %param.46) | copy-start | bytes 12340
  29.6 44.7 %copy-start.14 = (f32[3,256]{1,0:T(4,128)S(1)}, f32[3,256]{1,0:T(4,128)}, u32[]{:S(2)}) copy-start(f32[3,256]{1,0:T(4,128)} %refs_20_.1) | copy-start | bytes 9220
  29.6 44.7 %copy-start.15 = (f32[2,2,257,2]{2,3,1,0:T(2,128)S(1)}, f32[2,2,257,2]{2,3,1,0:T(2,128)}, u32[]{:S(2)}) copy-start(f32[2,2,257,2]{2,3,1,0:T(2,128)} %param.53) | copy-start | bytes 24676
  29.6 44.7 %copy-start.16 = (f32[2,256]{1,0:T(2,128)S(1)}, f32[2,256]{1,0:T(2,128)}, u32[]{:S(2)}) copy-start(f32[2,256]{1,0:T(2,128)} %refs_25_.1) | copy-start | bytes 6148
  29.6 44.7 %copy-start.17 = (f32[2,3,256]{2,0,1:T(2,128)S(1)}, f32[2,3,256]{2,0,1:T(2,128)}, u32[]{:S(2)}) copy-start(f32[2,3,256]{2,0,1:T(2,128)} %param.54) | copy-start | bytes 18436
  29.6 44.7 %copy-start.18 = (f32[4]{0:T(128)S(1)}, f32[4]{0:T(128)}, u32[]{:S(2)}) copy-start(f32[4]{0:T(128)} %refs_7_.1) | copy-start | bytes 52
  29.6 2.7 %collective-permute-start.1 = (f32[2048,128]{1,0:T(8,128)S(1)}, f32[2048,128]{1,0:T(8,128)S(1)}, u32[]{:S(2)}, u32[]{:S(2)}) collective-permute-start(f32[2048,128]{1,0:T(8,128)S(1)} %get-tuple-element.53), channel_id=1, source_target_pairs={{0,1},{1,0},{2,3},{3,2},{4,5},{5,4},{6,7},{7,6},{8,9},{9,8},{10,11... | collective-permute-start | bytes 3145736 | tf_op jit(solution)/shard_map/ppermute | solution.py:670
  32.5 7.3 %collective-permute-start.2 = (f32[512,128]{1,0:T(8,128)S(1)}, f32[512,128]{1,0:T(8,128)S(1)}, u32[]{:S(2)}, u32[]{:S(2)}) collective-permute-start(f32[512,128]{1,0:T(8,128)S(1)} %get-tuple-element.81), channel_id=1, source_target_pairs={{0,2},{1,9},{2,0},{3,11},{4,6},{5,13},{6,4},{7,15},{8,10},{9,1},{1... | collective-permute-start | bytes 786440 | tf_op jit(solution)/shard_map/ppermute | solution.py:675
  35.4 8.7 %collective-permute-start.4 = (f32[512,128]{1,0:T(8,128)S(1)}, f32[512,128]{1,0:T(8,128)S(1)}, u32[]{:S(2)}, u32[]{:S(2)}) collective-permute-start(f32[512,128]{1,0:T(8,128)S(1)} %get-tuple-element.82), channel_id=1, source_target_pairs={{0,6},{1,25},{2,4},{3,27},{4,2},{5,29},{6,0},{7,31},{8,14},{9,17},... | collective-permute-start | bytes 786440 | tf_op jit(solution)/shard_map/ppermute | solution.py:675
  36.9 9.2 %collective-permute-start.3 = (f32[512,128]{1,0:T(8,128)S(1)}, f32[512,128]{1,0:T(8,128)S(1)}, u32[]{:S(2)}, u32[]{:S(2)}) collective-permute-start(f32[512,128]{1,0:T(8,128)S(1)} %get-tuple-element.83), channel_id=1, source_target_pairs={{0,4},{1,17},{2,6},{3,19},{4,0},{5,21},{6,2},{7,23},{8,12},{9,25},... | collective-permute-start | bytes 786440 | tf_op jit(solution)/shard_map/ppermute | solution.py:675
  46.1 8.4 %collective-permute-start.7 = (f32[512,128]{1,0:T(8,128)S(1)}, f32[512,128]{1,0:T(8,128)S(1)}, u32[]{:S(2)}, u32[]{:S(2)}) collective-permute-start(f32[512,128]{1,0:T(8,128)S(1)} %fusion.2.refs_0_), channel_id=1, source_target_pairs={{0,24},{1,7},{2,26},{3,5},{4,28},{5,3},{6,30},{7,1},{8,16},{9,15},... | collective-permute-start | bytes 786440 | tf_op jit(solution)/shard_map/ppermute | solution.py:675
  49.8 12.2 %collective-permute-start.6 = (f32[512,128]{1,0:T(8,128)S(1)}, f32[512,128]{1,0:T(8,128)S(1)}, u32[]{:S(2)}, u32[]{:S(2)}) collective-permute-start(f32[512,128]{1,0:T(8,128)S(1)} %fusion.2.refs_0_), channel_id=1, source_target_pairs={{0,16},{1,5},{2,18},{3,7},{4,20},{5,1},{6,22},{7,3},{8,24},{9,13},... | collective-permute-start | bytes 786440 | tf_op jit(solution)/shard_map/ppermute | solution.py:675
  49.8 12.2 %collective-permute-start.5 = (f32[512,128]{1,0:T(8,128)S(1)}, f32[512,128]{1,0:T(8,128)S(1)}, u32[]{:S(2)}, u32[]{:S(2)}) collective-permute-start(f32[512,128]{1,0:T(8,128)S(1)} %fusion.2.refs_0_), channel_id=1, source_target_pairs={{0,8},{1,3},{2,10},{3,1},{4,12},{5,7},{6,14},{7,5},{8,0},{9,11},{1... | collective-permute-start | bytes 786440 | tf_op jit(solution)/shard_map/ppermute | solution.py:675
  62.1 7.5 %collective-permute-start.10 = (f32[520,128]{1,0:T(8,128)S(1)}, f32[520,128]{1,0:T(8,128)S(1)}, u32[]{:S(2)}, u32[]{:S(2)}) collective-permute-start(f32[520,128]{1,0:T(8,128)S(1)} %lastsum.1.refs_0_), channel_id=1, source_target_pairs={{0,6},{1,25},{2,4},{3,27},{4,2},{5,29},{6,0},{7,31},{8,14},{9,17},... | collective-permute-start | bytes 798728 | tf_op jit(solution)/shard_map/ppermute | solution.py:675
  64.0 8.4 %collective-permute-start.9 = (f32[520,128]{1,0:T(8,128)S(1)}, f32[520,128]{1,0:T(8,128)S(1)}, u32[]{:S(2)}, u32[]{:S(2)}) collective-permute-start(f32[520,128]{1,0:T(8,128)S(1)} %lastsum.1.refs_0_), channel_id=1, source_target_pairs={{0,4},{1,17},{2,6},{3,19},{4,0},{5,21},{6,2},{7,23},{8,12},{9,25},... | collective-permute-start | bytes 798728 | tf_op jit(solution)/shard_map/ppermute | solution.py:675
  65.2 7.2 %collective-permute-start.8 = (f32[520,128]{1,0:T(8,128)S(1)}, f32[520,128]{1,0:T(8,128)S(1)}, u32[]{:S(2)}, u32[]{:S(2)}) collective-permute-start(f32[520,128]{1,0:T(8,128)S(1)} %lastsum.1.refs_0_), channel_id=1, source_target_pairs={{0,2},{1,9},{2,0},{3,11},{4,6},{5,13},{6,4},{7,15},{8,10},{9,1},{1... | collective-permute-start | bytes 798728 | tf_op jit(solution)/shard_map/ppermute | solution.py:675
  72.4 1.8 %collective-permute-start.11 = (f32[8,128]{1,0:T(8,128)S(1)}, f32[8,128]{1,0:T(8,128)S(1)}, u32[]{:S(2)}, u32[]{:S(2)}) collective-permute-start(f32[8,128]{1,0:T(8,128)S(1)} %slice_add_fusion.4.refs_4_), channel_id=1, source_target_pairs={{0,1},{1,0},{2,3},{3,2},{4,5},{5,4},{6,7},{7,6},{8,9},{9,8},{10,11... | collective-permute-start | bytes 12296 | tf_op jit(solution)/shard_map/ppermute | solution.py:670
